TPU v7x, 512 devices: a whole 4x8x8 slice. The times are simulated.
512 devices in a mesh: sx: 8 (over z), sy: 8 (over y), cg: 8 (over x, core).
Axes of the slice: x: 4, y: 8, z: 8, core: 2. Of those that a mesh axis runs over, the one named last changes fastest.
Arguments:
- right_side: float32 [512, 1024, 128], P(('sx', 'cg'), 'sy'), may hold values from -6 to 18, as said below
- perm_class: int32 [512, 1024, 128], P(('sx', 'cg'), 'sy'), may hold values from 0 to 15
- perm_table: float32 [2, 16], replicated, may hold values from 0.02 to 2
Outputs:
- solution: float32 [512, 1024, 128], P(('sx', 'cg'), 'sy')
- residual: float32 [512, 1024, 128], P(('sx', 'cg'), 'sy')
Inputs may be any that keep to these rules, and one draw needn't show every extreme that they name: `right_side`: source terms, one real value a cell.
All inputs are finite; a program needn't handle non-finite values.
Results may differ from a plain program's by a relative error of at most 0.0003.
Values sent between devices are 32-bit elements; how exact they have to be, the bound alone decides.
No kernel may reach another device: no remote copies, remote signals or barrier semaphores. Data moves between devices by JAX's collectives and lax.ppermute only.
A program may use at most 64 MiB of HBM per device.

v0:
```python
import jax
import jax.numpy as jnp
from jax import lax
from jax.sharding import PartitionSpec as P

AX = 4
AY = 4
AZ = 4
ITERS = 2
COARSE_ITERS = 4


omega_fine = 2.0 / 3.0
omega_coarse = 2.0 / 3.0


def with_halo(cells, sides, width):
    for axis, dim in sides:
        count = lax.axis_size(axis)
        ends = count - 1
        head = lax.slice_in_dim(cells, 0, width, axis=dim)
        tail = lax.slice_in_dim(cells, cells.shape[dim] - width, cells.shape[dim], axis=dim)
        cells = jnp.concatenate(
            [
                lax.ppermute(tail, axis, [(i, (i + 1) % count) for i in range(ends)]),
                cells,
                lax.ppermute(head, axis, [((i + 1) % count, i) for i in range(ends)]),
            ],
            axis=dim,
        )
    return cells


def lower_shift(values):
    zero_col = jnp.zeros_like(values[..., :1])
    return jnp.concatenate([zero_col, values[..., :-1]], axis=-1)


def upper_shift(values):
    zero_col = jnp.zeros_like(values[..., :1])
    return jnp.concatenate([values[..., 1:], zero_col], axis=-1)


def harmonic(left, right):
    return 2.0 * left * right / (left + right)


def apply_rimmed(coefs, values, rimmed):
    x_low, x_high, y_low, y_high, z_up, centre = coefs
    beside = x_low * rimmed[:-2, 1:-1] + x_high * rimmed[2:, 1:-1]
    beside = beside + y_low * rimmed[1:-1, :-2] + y_high * rimmed[1:-1, 2:]
    beside = beside + z_up * upper_shift(values) + lower_shift(z_up * values)
    return centre * values - beside


def block_sum(values, extent):
    count_x, count_y, count_z = extent
    size_x, size_y, size_z = values.shape
    blocks = values.reshape(
        count_x, size_x // count_x, count_y, size_y // count_y, count_z, size_z // count_z
    )
    return blocks.sum(axis=(1, 3, 5))


def coarse_coefs(fine, extent):
    x_low, x_high, y_low, y_high, z_up, centre = fine
    span_x = x_low.shape[0] // extent[0]
    span_y = x_low.shape[1] // extent[1]
    span_z = x_low.shape[2] // extent[2]
    pieces = [
        block_sum(x_low[0::span_x], extent),
        block_sum(x_high[span_x - 1 :: span_x], extent),
        block_sum(y_low[:, 0::span_y], extent),
        block_sum(y_high[:, span_y - 1 :: span_y], extent),
        block_sum(z_up[:, :, span_z - 1 :: span_z], extent),
    ]
    summed = pieces[0] + pieces[1] + pieces[2] + pieces[3] + pieces[4] + lower_shift(pieces[4])
    return jnp.stack(pieces + [summed])


def prolong(values, extent):
    count_x, count_y, count_z = values.shape
    size_x, size_y, size_z = extent
    spread = jnp.broadcast_to(
        values[:, None, :, None, :, None],
        (count_x, size_x // count_x, count_y, size_y // count_y, count_z, size_z // count_z),
    )
    return spread.reshape(extent)


def fine_coefs(perm_class, perm_table):
    horizontal = jnp.zeros(perm_class.shape, jnp.float32)
    vertical = jnp.zeros(perm_class.shape, jnp.float32)
    for category in range(perm_table.shape[1]):
        matches = perm_class == category
        horizontal = jnp.where(matches, perm_table[0, category], horizontal)
        vertical = jnp.where(matches, perm_table[1, category], vertical)
    rimmed = with_halo(horizontal, ((("sx", "cg"), 0), ("sy", 1)), 1)
    first_x = lax.axis_index(("sx", "cg")) == 0
    last_x = lax.axis_index(("sx", "cg")) == lax.axis_size(("sx", "cg")) - 1
    first_y = lax.axis_index("sy") == 0
    last_y = lax.axis_index("sy") == lax.axis_size("sy") - 1
    x_faces = harmonic(rimmed[:-1, 1:-1], rimmed[1:, 1:-1])
    x_low = x_faces[:-1]
    x_low = x_low.at[0].set(jnp.where(first_x, 2.0 * horizontal[0], x_low[0]))
    x_high = x_faces[1:]
    x_high = x_high.at[-1].set(jnp.where(last_x, 2.0 * horizontal[-1], x_high[-1]))
    y_faces = harmonic(rimmed[1:-1, :-1], rimmed[1:-1, 1:])
    y_low = y_faces[:, :-1]
    y_low = y_low.at[:, 0].set(jnp.where(first_y, 2.0 * horizontal[:, 0], y_low[:, 0]))
    y_high = y_faces[:, 1:]
    y_high = y_high.at[:, -1].set(jnp.where(last_y, 2.0 * horizontal[:, -1], y_high[:, -1]))
    z_up = harmonic(vertical, upper_shift(vertical))
    centre = x_low + x_high + y_low + y_high + z_up + lower_shift(z_up)
    return (x_low, x_high, y_low, y_high, z_up, centre)


def fine_apply(fine, values):
    rimmed = with_halo(values, ((("sx", "cg"), 0), ("sy", 1)), 1)
    return apply_rimmed(fine, values, rimmed)


def rim_grid(values):
    return with_halo(values, ((("sx", "cg"), 0), ("sy", 1)), 1)


def coarse_solve(context, source):
    centre = context[5]
    values = omega_coarse * source / centre
    for sweep in range(COARSE_ITERS - 1):
        values = (
            values
            + omega_coarse
            * (source - apply_rimmed(tuple(context), values, rim_grid(values)))
            / centre
        )
    return values


def precondition(fine, context, residual):
    centre = fine[5]
    sweep_one = omega_fine * residual / centre
    smooth = sweep_one + omega_fine * (residual - fine_apply(fine, sweep_one)) / centre
    correction = coarse_solve(context, block_sum(residual, (AX, AY, AZ)))
    return smooth + prolong(correction, residual.shape)


def residual_fit(residual, smoothed):
    return lax.psum(jnp.sum(residual * smoothed), ("sx", "sy", "cg"))


def body(right_side, perm_class, perm_table):
    fine = fine_coefs(perm_class, perm_table)
    context = coarse_coefs(fine, (AX, AY, AZ))
    solution = jnp.zeros_like(right_side)
    residual = right_side
    direction = precondition(fine, context, residual)
    fit_now = residual_fit(residual, direction)
    for iteration in range(ITERS):
        applied = fine_apply(fine, direction)
        step_size = fit_now / lax.psum(jnp.sum(direction * applied), ("sx", "sy", "cg"))
        solution = solution + step_size * direction
        residual = residual - step_size * applied
        if iteration + 1 < ITERS:
            smoothed = precondition(fine, context, residual)
            fit_next = residual_fit(residual, smoothed)
            direction = smoothed + fit_next / fit_now * direction
            fit_now = fit_next
    return (solution, residual)


def solution(mesh):
    placed = (P(("sx", "cg"), "sy", None), P(("sx", "cg"), "sy", None), P())
    return jax.shard_map(
        body,
        mesh=mesh,
        in_specs=placed,
        out_specs=(P(("sx", "cg"), "sy", None), P(("sx", "cg"), "sy", None)),
        check_vma=False,
    )
```

profile of v0, /device:TPU:1, one launch (start us, length us, event | category | flops | bytes accessed | tf_op | source)
XLA Modules:
  0.0 569.2 jit_solution(5597950333896180555)
XLA Ops:
  4.6 12.7 %select_select_fusion.1 = (f32[8,128,128]{2,1,0:T(8,128)S(1)}, pred[8,128,128]{2,1,0:T(8,128)(4,1)S(1)}, pred[8,128,128]{2,1,0:T(8,128)(4,1)S(1)}, pred[8,128,12...) fusion(f32[]{:T(128)} %bitcast.15, f32[]{:T(128)} %bitcast.14, ...), kind=kLoop, calls=%fused_computation.108 | loop fusion | flops 4194304 | bytes 3145792 | tf_op jit(solution)/shard_map/jit(_where)/select_n | solution.py:96
  17.3 8.7 %collective-permute-start.1 = (f32[1,128,128]{2,1,0:T(8,128)S(1)}, f32[1,128,128]{2,1,0:T(8,128)S(1)}, u32[]{:S(2)}, u32[]{:S(2)}) collective-permute-start(f32[1,128,128]{2,1,0:T(8,128)S(1)} %get-tuple-element.117), channel_id=1, source_target_pairs={{1,0},{2,1},{3,2},{4,3},{5,4},{6,5},{7,6},{64,7},{65,64},{66,65},{... | collective-permute-start | bytes 196616 | tf_op jit(solution)/shard_map/ppermute | solution.py:27
  28.0 11.0 %select_select_fusion = f32[8,128,128]{2,1,0:T(8,128)S(1)} fusion(pred[8,128,128]{2,1,0:T(8,128)(4,1)S(1)} %get-tuple-element.81, pred[8,128,128]{2,1,0:T(8,128)(4,1)S(1)} %get-tuple-element.80, pred[8,128,128]{2,1,0:T(8,128)(4,1)S(1)} %get-tuple-element.79, pred[8,128,128]{2,1,0:T(8,128)(4,1)S(1)} %get-tuple-element.78, ...), kind=kLoop, calls=%fused_computation.107 | loop fusion | flops 2097152 | bytes 2621504 | tf_op jit(solution)/shard_map/jit(_where)/select_n | solution.py:97
  46.1 4.0 collective-permute-start.2
  68.0 3.6 collective-permute-start.4
  73.0 4.0 collective-permute-start.10
  79.8 3.6 collective-permute-start.12
  85.4 4.2 collective-permute-start.14
  92.5 5.1 collective-permute-start.16
  99.6 4.5 collective-permute-start.18
  105.5 4.2 collective-permute-start.6
  111.5 3.1 reshape.157
  114.6 3.4 fusion.44
  120.1 4.8 collective-permute-start.20
  127.5 4.5 collective-permute-start.22
  134.5 124.9 %all-reduce.23 = (f32[]{:T(128)}, f32[]{:T(128)}) all-reduce(f32[]{:T(128)} %get-tuple-element.51, f32[]{:T(128)} %get-tuple-element.50), channel_id=1, replica_groups=mesh['sx'=8,'sy'=8,'cg'=8] {'sx','sy','cg'}, use_global_device_ids=true, to_apply=%region_7.8 | all-reduce | flops 2 | bytes 16 | tf_op jit(solution)/shard_map/psum | solution.py:149
  263.0 3.2 reshape.158
  273.4 3.6 collective-permute-start.28
  278.9 3.6 collective-permute-start.24
  283.9 4.6 collective-permute-start.30
  291.3 3.6 collective-permute-start.32
  297.0 4.2 collective-permute-start.34
  304.0 5.1 collective-permute-start.36
  311.1 4.5 collective-permute-start.38
  317.0 4.2 collective-permute-start.26
  323.1 3.1 reshape.159
  326.1 4.7 multiply_reduce_fusion.1
  330.9 114.5 %psum.30 = f32[]{:T(128)} all-reduce(f32[]{:T(128)} %get-tuple-element.56), channel_id=1, replica_groups=mesh['sx'=8,'sy'=8,'cg'=8] {'sx','sy','cg'}, use_global_device_ids=true, to_apply=%region_12.13 | all-reduce | flops 1 | bytes 8 | tf_op jit(solution)/shard_map/psum | solution.py:149
  447.8 3.1 collective-permute-start.41
  450.8 3.6 collective-permute-start.40
  457.1 4.0 collective-permute-start.42
  463.8 101.8 %psum.31 = f32[]{:T(128)} all-reduce(f32[]{:T(128)} %get-tuple-element.54), channel_id=1, replica_groups=mesh['sx'=8,'sy'=8,'cg'=8] {'sx','sy','cg'}, use_global_device_ids=true, to_apply=%region_14.15 | all-reduce | flops 1 | bytes 8 | tf_op jit(solution)/shard_map/psum | solution.py:161
  (163 shorter events, 86.2 us)
Async XLA Ops:
  17.3 27.5 %collective-permute-start.1 = (f32[1,128,128]{2,1,0:T(8,128)S(1)}, f32[1,128,128]{2,1,0:T(8,128)S(1)}, u32[]{:S(2)}, u32[]{:S(2)}) collective-permute-start(f32[1,128,128]{2,1,0:T(8,128)S(1)} %get-tuple-element.117), channel_id=1, source_target_pairs={{1,0},{2,1},{3,2},{4,3},{5,4},{6,5},{7,6},{64,7},{65,64},{66,65},{... | collective-permute-start | bytes 196616 | tf_op jit(solution)/shard_map/ppermute | solution.py:27
  26.0 18.7 %collective-permute-start = (f32[1,128,128]{2,1,0:T(8,128)S(1)}, f32[1,128,128]{2,1,0:T(8,128)S(1)}, u32[]{:S(2)}, u32[]{:S(2)}) collective-permute-start(f32[1,128,128]{2,1,0:T(8,128)S(1)} %get-tuple-element.116), channel_id=1, source_target_pairs={{0,1},{1,2},{2,3},{3,4},{4,5},{5,6},{6,7},{7,64},{64,65},{65,66},{... | collective-permute-start | bytes 196616 | tf_op jit(solution)/shard_map/ppermute | solution.py:25
  44.8 11.6 %collective-permute-start.3 = (f32[10,1,128]{2,1,0:T(1,128)S(1)}, f32[10,1,128]{2,1,0:T(1,128)S(1)}, u32[]{:S(2)}, u32[]{:S(2)}) collective-permute-start(f32[10,1,128]{2,1,0:T(1,128)S(1)} %get-tuple-element.95), channel_id=1, source_target_pairs={{8,0},{16,8},{24,16},{32,24},{40,32},{48,40},{56,48},{9,1},{17,9},... | collective-permute-start | bytes 15368 | tf_op jit(solution)/shard_map/ppermute | solution.py:27
  46.1 10.3 %collective-permute-start.2 = (f32[10,1,128]{2,1,0:T(1,128)S(1)}, f32[10,1,128]{2,1,0:T(1,128)S(1)}, u32[]{:S(2)}, u32[]{:S(2)}) collective-permute-start(f32[10,1,128]{2,1,0:T(1,128)S(1)} %get-tuple-element.94), channel_id=1, source_target_pairs={{0,8},{8,16},{16,24},{24,32},{32,40},{40,48},{48,56},{1,9},{9,17},... | collective-permute-start | bytes 15368 | tf_op jit(solution)/shard_map/ppermute | solution.py:25
  60.5 11.1 %collective-permute-start.9 = (f32[1,4,4]{2,1,0:T(4,128)S(1)}, f32[1,4,4]{2,1,0:T(4,128)S(1)}, u32[]{:S(2)}, u32[]{:S(2)}) collective-permute-start(f32[1,4,4]{2,1,0:T(4,128)S(1)} %get-tuple-element.153), channel_id=1, source_target_pairs={{1,0},{2,1},{3,2},{4,3},{5,4},{6,5},{7,6},{64,7},{65,64},{66,65},{... | collective-permute-start | bytes 200 | tf_op jit(solution)/shard_map/ppermute | solution.py:27
  63.4 8.2 %collective-permute-start.8 = (f32[1,4,4]{2,1,0:T(4,128)S(1)}, f32[1,4,4]{2,1,0:T(4,128)S(1)}, u32[]{:S(2)}, u32[]{:S(2)}) collective-permute-start(f32[1,4,4]{2,1,0:T(4,128)S(1)} %get-tuple-element.152), channel_id=1, source_target_pairs={{0,1},{1,2},{2,3},{3,4},{4,5},{5,6},{6,7},{7,64},{64,65},{65,66},{... | collective-permute-start | bytes 200 | tf_op jit(solution)/shard_map/ppermute | solution.py:25
  66.0 38.1 %collective-permute-start.5 = (f32[1,128,128]{2,1,0:T(8,128)S(1)}, f32[1,128,128]{2,1,0:T(8,128)S(1)}, u32[]{:S(2)}, u32[]{:S(2)}) collective-permute-start(f32[1,128,128]{2,1,0:T(8,128)S(1)} %get-tuple-element.115), channel_id=1, source_target_pairs={{1,0},{2,1},{3,2},{4,3},{5,4},{6,5},{7,6},{64,7},{65,64},{66,65},{... | collective-permute-start | bytes 196616 | tf_op jit(solution)/shard_map/ppermute | solution.py:27
  68.0 36.2 %collective-permute-start.4 = (f32[1,128,128]{2,1,0:T(8,128)S(1)}, f32[1,128,128]{2,1,0:T(8,128)S(1)}, u32[]{:S(2)}, u32[]{:S(2)}) collective-permute-start(f32[1,128,128]{2,1,0:T(8,128)S(1)} %get-tuple-element.114), channel_id=1, source_target_pairs={{0,1},{1,2},{2,3},{3,4},{4,5},{5,6},{6,7},{7,64},{64,65},{65,66},{... | collective-permute-start | bytes 196616 | tf_op jit(solution)/shard_map/ppermute | solution.py:25
  77.8 5.6 collective-permute-start.13
  84.1 5.5 collective-permute-start.15
  90.6 7.0 %collective-permute-start.17 = (f32[1,4,4]{2,1,0:T(4,128)S(1)}, f32[1,4,4]{2,1,0:T(4,128)S(1)}, u32[]{:S(2)}, u32[]{:S(2)}) collective-permute-start(f32[1,4,4]{2,1,0:T(4,128)S(1)} %get-tuple-element.145), channel_id=1, source_target_pairs={{1,0},{2,1},{3,2},{4,3},{5,4},{6,5},{7,6},{64,7},{65,64},{66,65},{... | collective-permute-start | bytes 200 | tf_op jit(solution)/shard_map/ppermute | solution.py:27
  92.5 5.8 %collective-permute-start.16 = (f32[1,4,4]{2,1,0:T(4,128)S(1)}, f32[1,4,4]{2,1,0:T(4,128)S(1)}, u32[]{:S(2)}, u32[]{:S(2)}) collective-permute-start(f32[1,4,4]{2,1,0:T(4,128)S(1)} %get-tuple-element.144), channel_id=1, source_target_pairs={{0,1},{1,2},{2,3},{3,4},{4,5},{5,6},{6,7},{7,64},{64,65},{65,66},{... | collective-permute-start | bytes 200 | tf_op jit(solution)/shard_map/ppermute | solution.py:25
  98.3 11.4 %collective-permute-start.19 = (f32[6,1,4]{2,1,0:T(1,128)S(1)}, f32[6,1,4]{2,1,0:T(1,128)S(1)}, u32[]{:S(2)}, u32[]{:S(2)}) collective-permute-start(f32[6,1,4]{2,1,0:T(1,128)S(1)} %get-tuple-element.125), channel_id=1, source_target_pairs={{8,0},{16,8},{24,16},{32,24},{40,32},{48,40},{56,48},{9,1},{17,9},... | collective-permute-start | bytes 296 | tf_op jit(solution)/shard_map/ppermute | solution.py:27
  99.6 10.1 %collective-permute-start.18 = (f32[6,1,4]{2,1,0:T(1,128)S(1)}, f32[6,1,4]{2,1,0:T(1,128)S(1)}, u32[]{:S(2)}, u32[]{:S(2)}) collective-permute-start(f32[6,1,4]{2,1,0:T(1,128)S(1)} %get-tuple-element.124), channel_id=1, source_target_pairs={{0,8},{8,16},{16,24},{24,32},{32,40},{40,48},{48,56},{1,9},{9,17},... | collective-permute-start | bytes 296 | tf_op jit(solution)/shard_map/ppermute | solution.py:25
  104.2 10.4 %collective-permute-start.7 = (f32[10,1,128]{2,1,0:T(1,128)S(1)}, f32[10,1,128]{2,1,0:T(1,128)S(1)}, u32[]{:S(2)}, u32[]{:S(2)}) collective-permute-start(f32[10,1,128]{2,1,0:T(1,128)S(1)} %get-tuple-element.93), channel_id=1, source_target_pairs={{8,0},{16,8},{24,16},{32,24},{40,32},{48,40},{56,48},{9,1},{17,9},... | collective-permute-start | bytes 15368 | tf_op jit(solution)/shard_map/ppermute | solution.py:27
  105.5 9.1 %collective-permute-start.6 = (f32[10,1,128]{2,1,0:T(1,128)S(1)}, f32[10,1,128]{2,1,0:T(1,128)S(1)}, u32[]{:S(2)}, u32[]{:S(2)}) collective-permute-start(f32[10,1,128]{2,1,0:T(1,128)S(1)} %get-tuple-element.92), channel_id=1, source_target_pairs={{0,8},{8,16},{16,24},{24,32},{32,40},{40,48},{48,56},{1,9},{9,17},... | collective-permute-start | bytes 15368 | tf_op jit(solution)/shard_map/ppermute | solution.py:25
  118.0 6.8 %collective-permute-start.21 = (f32[1,128,128]{2,1,0:T(8,128)S(1)}, f32[1,128,128]{2,1,0:T(8,128)S(1)}, u32[]{:S(2)}, u32[]{:S(2)}) collective-permute-start(f32[1,128,128]{2,1,0:T(8,128)S(1)} %get-tuple-element.109), channel_id=1, source_target_pairs={{1,0},{2,1},{3,2},{4,3},{5,4},{6,5},{7,6},{64,7},{65,64},{66,65},{... | collective-permute-start | bytes 196616 | tf_op jit(solution)/shard_map/ppermute | solution.py:27
  120.1 6.1 %collective-permute-start.20 = (f32[1,128,128]{2,1,0:T(8,128)S(1)}, f32[1,128,128]{2,1,0:T(8,128)S(1)}, u32[]{:S(2)}, u32[]{:S(2)}) collective-permute-start(f32[1,128,128]{2,1,0:T(8,128)S(1)} %get-tuple-element.108), channel_id=1, source_target_pairs={{0,1},{1,2},{2,3},{3,4},{4,5},{5,6},{6,7},{7,64},{64,65},{65,66},{... | collective-permute-start | bytes 196616 | tf_op jit(solution)/shard_map/ppermute | solution.py:25
  126.2 6.0 %collective-permute-start.23 = (f32[10,1,128]{2,1,0:T(1,128)S(1)}, f32[10,1,128]{2,1,0:T(1,128)S(1)}, u32[]{:S(2)}, u32[]{:S(2)}) collective-permute-start(f32[10,1,128]{2,1,0:T(1,128)S(1)} %get-tuple-element.91), channel_id=1, source_target_pairs={{8,0},{16,8},{24,16},{32,24},{40,32},{48,40},{56,48},{9,1},{17,9},... | collective-permute-start | bytes 15368 | tf_op jit(solution)/shard_map/ppermute | solution.py:27
  270.8 11.8 %collective-permute-start.29 = (f32[1,4,4]{2,1,0:T(4,128)S(1)}, f32[1,4,4]{2,1,0:T(4,128)S(1)}, u32[]{:S(2)}, u32[]{:S(2)}) collective-permute-start(f32[1,4,4]{2,1,0:T(4,128)S(1)} %get-tuple-element.141), channel_id=1, source_target_pairs={{1,0},{2,1},{3,2},{4,3},{5,4},{6,5},{7,6},{64,7},{65,64},{66,65},{... | collective-permute-start | bytes 200 | tf_op jit(solution)/shard_map/ppermute | solution.py:27
  273.4 9.2 %collective-permute-start.28 = (f32[1,4,4]{2,1,0:T(4,128)S(1)}, f32[1,4,4]{2,1,0:T(4,128)S(1)}, u32[]{:S(2)}, u32[]{:S(2)}) collective-permute-start(f32[1,4,4]{2,1,0:T(4,128)S(1)} %get-tuple-element.140), channel_id=1, source_target_pairs={{0,1},{1,2},{2,3},{3,4},{4,5},{5,6},{6,7},{7,64},{64,65},{65,66},{... | collective-permute-start | bytes 200 | tf_op jit(solution)/shard_map/ppermute | solution.py:25
  277.0 38.7 %collective-permute-start.25 = (f32[1,128,128]{2,1,0:T(8,128)S(1)}, f32[1,128,128]{2,1,0:T(8,128)S(1)}, u32[]{:S(2)}, u32[]{:S(2)}) collective-permute-start(f32[1,128,128]{2,1,0:T(8,128)S(1)} %get-tuple-element.105), channel_id=1, source_target_pairs={{1,0},{2,1},{3,2},{4,3},{5,4},{6,5},{7,6},{64,7},{65,64},{66,65},{... | collective-permute-start | bytes 196616 | tf_op jit(solution)/shard_map/ppermute | solution.py:27
  278.9 36.8 %collective-permute-start.24 = (f32[1,128,128]{2,1,0:T(8,128)S(1)}, f32[1,128,128]{2,1,0:T(8,128)S(1)}, u32[]{:S(2)}, u32[]{:S(2)}) collective-permute-start(f32[1,128,128]{2,1,0:T(8,128)S(1)} %get-tuple-element.104), channel_id=1, source_target_pairs={{0,1},{1,2},{2,3},{3,4},{4,5},{5,6},{6,7},{7,64},{64,65},{65,66},{... | collective-permute-start | bytes 196616 | tf_op jit(solution)/shard_map/ppermute | solution.py:25
  282.6 5.9 %collective-permute-start.31 = (f32[6,1,4]{2,1,0:T(1,128)S(1)}, f32[6,1,4]{2,1,0:T(1,128)S(1)}, u32[]{:S(2)}, u32[]{:S(2)}) collective-permute-start(f32[6,1,4]{2,1,0:T(1,128)S(1)} %get-tuple-element.123), channel_id=1, source_target_pairs={{8,0},{16,8},{24,16},{32,24},{40,32},{48,40},{56,48},{9,1},{17,9},... | collective-permute-start | bytes 296 | tf_op jit(solution)/shard_map/ppermute | solution.py:27
  289.4 5.6 collective-permute-start.33
  302.1 7.0 %collective-permute-start.37 = (f32[1,4,4]{2,1,0:T(4,128)S(1)}, f32[1,4,4]{2,1,0:T(4,128)S(1)}, u32[]{:S(2)}, u32[]{:S(2)}) collective-permute-start(f32[1,4,4]{2,1,0:T(4,128)S(1)} %get-tuple-element.133), channel_id=1, source_target_pairs={{1,0},{2,1},{3,2},{4,3},{5,4},{6,5},{7,6},{64,7},{65,64},{66,65},{... | collective-permute-start | bytes 200 | tf_op jit(solution)/shard_map/ppermute | solution.py:27
  304.0 5.8 %collective-permute-start.36 = (f32[1,4,4]{2,1,0:T(4,128)S(1)}, f32[1,4,4]{2,1,0:T(4,128)S(1)}, u32[]{:S(2)}, u32[]{:S(2)}) collective-permute-start(f32[1,4,4]{2,1,0:T(4,128)S(1)} %get-tuple-element.132), channel_id=1, source_target_pairs={{0,1},{1,2},{2,3},{3,4},{4,5},{5,6},{6,7},{7,64},{64,65},{65,66},{... | collective-permute-start | bytes 200 | tf_op jit(solution)/shard_map/ppermute | solution.py:25
  309.8 11.4 %collective-permute-start.39 = (f32[6,1,4]{2,1,0:T(1,128)S(1)}, f32[6,1,4]{2,1,0:T(1,128)S(1)}, u32[]{:S(2)}, u32[]{:S(2)}) collective-permute-start(f32[6,1,4]{2,1,0:T(1,128)S(1)} %get-tuple-element.119), channel_id=1, source_target_pairs={{8,0},{16,8},{24,16},{32,24},{40,32},{48,40},{56,48},{9,1},{17,9},... | collective-permute-start | bytes 296 | tf_op jit(solution)/shard_map/ppermute | solution.py:27
  311.1 10.1 %collective-permute-start.38 = (f32[6,1,4]{2,1,0:T(1,128)S(1)}, f32[6,1,4]{2,1,0:T(1,128)S(1)}, u32[]{:S(2)}, u32[]{:S(2)}) collective-permute-start(f32[6,1,4]{2,1,0:T(1,128)S(1)} %get-tuple-element.118), channel_id=1, source_target_pairs={{0,8},{8,16},{16,24},{24,32},{32,40},{40,48},{48,56},{1,9},{9,17},... | collective-permute-start | bytes 296 | tf_op jit(solution)/shard_map/ppermute | solution.py:25
  315.7 10.4 %collective-permute-start.27 = (f32[10,1,128]{2,1,0:T(1,128)S(1)}, f32[10,1,128]{2,1,0:T(1,128)S(1)}, u32[]{:S(2)}, u32[]{:S(2)}) collective-permute-start(f32[10,1,128]{2,1,0:T(1,128)S(1)} %get-tuple-element.89), channel_id=1, source_target_pairs={{8,0},{16,8},{24,16},{32,24},{40,32},{48,40},{56,48},{9,1},{17,9},... | collective-permute-start | bytes 15368 | tf_op jit(solution)/shard_map/ppermute | solution.py:27
  317.0 9.1 %collective-permute-start.26 = (f32[10,1,128]{2,1,0:T(1,128)S(1)}, f32[10,1,128]{2,1,0:T(1,128)S(1)}, u32[]{:S(2)}, u32[]{:S(2)}) collective-permute-start(f32[10,1,128]{2,1,0:T(1,128)S(1)} %get-tuple-element.88), channel_id=1, source_target_pairs={{0,8},{8,16},{16,24},{24,32},{32,40},{40,48},{48,56},{1,9},{9,17},... | collective-permute-start | bytes 15368 | tf_op jit(solution)/shard_map/ppermute | solution.py:25
  447.8 6.7 %collective-permute-start.41 = (f32[1,128,128]{2,1,0:T(8,128)S(1)}, f32[1,128,128]{2,1,0:T(8,128)S(1)}, u32[]{:S(2)}, u32[]{:S(2)}) collective-permute-start(f32[1,128,128]{2,1,0:T(8,128)S(1)} %get-tuple-element.101), channel_id=1, source_target_pairs={{1,0},{2,1},{3,2},{4,3},{5,4},{6,5},{7,6},{64,7},{65,64},{66,65},{... | collective-permute-start | bytes 196616 | tf_op jit(solution)/shard_map/ppermute | solution.py:27
  (21 other events, 483.5 us)
where the time goes:
time: 572 us; the launch traced here: 569 us
  blocking collectives  341 us (60%)
  starting transfers between devices  133 us (23%)
  other arithmetic  56.5 us (10%)
  local copies, waits for them, and re-layouts  23.7 us (4%)
  waiting for transfers between devices  9.25 us (2%)
    psum x2, blocking collectives, residual_fit(): return lax.psum(jnp.sum(residual * smoothed), ('sx', 'sy', 'cg'))  239 us
    psum x1, blocking collectives, body(): lax.psum(jnp.sum(direction * applied), ('sx', 'sy', 'cg'))  102 us
    ppermute x22, starting transfers between devices, with_halo(): lax.ppermute(tail, axis, [(i, (i + 1) % count) for i in range(ends)])  88.2 us
    ppermute x22, starting transfers between devices, with_halo(): lax.ppermute(head, axis, [((i + 1) % count, i) for i in range(ends)])  45.1 us
    select_n x1, other arithmetic, fine_coefs(): horizontal = jnp.where(matches, perm_table[0, category], horizontal)  12.7 us
  transfers between devices with their start and end apart: 44, of which 12 were waited for; matrix products, arithmetic and copies ran while one was open for 6% of the time, Pallas kernels for 0%

commit v1 on v0

v1 whole, which is shorter than its diff:
```python
import jax
import jax.numpy as jnp
from jax import lax
from jax.experimental import pallas as pl
from jax.experimental.pallas import tpu as pltpu
from jax.sharding import PartitionSpec as P

F32 = jnp.float32
W = 2.0 / 3.0
X_AXES = ("sx", "cg")
SWEEPS = 3

NXL, NYL, NZ = 8, 128, 128
HX = 3
PLANES = NXL + 2 * HX
ROWS = 160
OWN = 16
CHUNKS = ((8, 8, -1), (16, 32, 0), (48, 32, 1), (80, 32, 2), (112, 32, 3), (144, 8, 4))
OWN_CHUNKS = CHUNKS[1:5]
X_LOW, X_HIGH, Y_LOW, Y_HIGH, Z_UP, SOURCE = range(6)


def harmonic(a, b):
    return 2.0 * a * b / (a + b)


def up(v):
    return pltpu.roll(v, NZ - 1, 1)


def down(v):
    return pltpu.roll(v, 1, 1)


def look_up(row, index):
    table = jnp.broadcast_to(row, index.shape)
    return jnp.take_along_axis(table, index, axis=1, mode="promise_in_bounds")


def iota(shape, dim):
    return lax.broadcasted_iota(jnp.int32, shape, dim)


def dot(a, b):
    return jnp.dot(a, b, precision=lax.Precision.HIGHEST, preferred_element_type=F32)


def sum_matrix():
    return jnp.where(iota((NZ, NZ), 0) // 32 == iota((NZ, NZ), 1) % 4, 1.0, 0.0).astype(F32)


def top_matrix():
    lane, col = iota((NZ, NZ), 0), iota((NZ, NZ), 1) % 4
    return jnp.where((lane == 32 * col + 31) & (col < 3), 1.0, 0.0).astype(F32)


def row_group(values):
    return (values[0:8] + values[8:16]) + (values[16:24] + values[24:32])


def gather_tile(pieces):
    group = iota((8, NZ), 1) // 4
    sublane = iota((8, NZ), 0)
    tile = jnp.zeros((8, NZ), F32)
    for a, parts in enumerate(pieces):
        acc = jnp.zeros((8, NZ), F32)
        for field, j, part in parts:
            acc = jnp.where(group == 4 * field + j, part, acc)
        tile = jnp.where(sublane == a, jnp.sum(acc, axis=0, keepdims=True), tile)
    return tile


def coarse_kernel(
    inside, table, cls, rhs, xlo, xhi, ylo, yhi, out, kh, tiles, ztiles
):
    khrow, kvrow = table[0:1, :], table[1:2, :]

    def own(x, _):
        index = cls[x]
        kh[x + 1, 8:136, :] = look_up(khrow, index)
        kh[x + 1, 0:8, :] = look_up(khrow, ylo[x].astype(jnp.int32))
        kh[x + 1, 136:144, :] = look_up(khrow, yhi[x].astype(jnp.int32))
        return 0

    lax.fori_loop(0, NXL, own, 0)
    kh[0, 8:136, :] = look_up(khrow, xlo[2].astype(jnp.int32))
    kh[NXL + 1, 8:136, :] = look_up(khrow, xhi[0].astype(jnp.int32))

    first = iota((8, NZ), 0) == 0
    for f in range(5):
        for j in range(4):
            rows = pl.ds(8 + 32 * j, 32)
            low, high = kh[2 * f, rows, :], kh[2 * f + 1, rows, :]
            face = harmonic(low, high)
            if f == 0:
                face = jnp.where(inside[0] > 0.5, face, 2.0 * high)
            if f == 4:
                face = jnp.where(inside[1] > 0.5, face, 2.0 * low)
            tiles[pl.ds(8 * (4 * f + j), 8), :] = row_group(face)
    for a in range(4):
        for j in range(5):
            total = jnp.zeros((8, NZ), F32)
            for x in (2 * a, 2 * a + 1):
                low = kh[x + 1, pl.ds(7 + 32 * j, 8), :]
                high = kh[x + 1, pl.ds(8 + 32 * j, 8), :]
                face = harmonic(low, high)
                if j == 0:
                    face = jnp.where(inside[2] > 0.5, face, 2.0 * high)
                if j == 4:
                    face = jnp.where(inside[3] > 0.5, face, 2.0 * low)
                total = total + face
            tiles[pl.ds(8 * (20 + 5 * a + j), 8), :] = jnp.where(first, total, 0.0)
        for j in range(4):
            rows = pl.ds(32 * j, 32)
            source = rhs[2 * a, rows, :] + rhs[2 * a + 1, rows, :]
            tiles[pl.ds(8 * (40 + 4 * a + j), 8), :] = row_group(source)
            kv0 = look_up(kvrow, cls[2 * a, rows, :])
            kv1 = look_up(kvrow, cls[2 * a + 1, rows, :])
            upper = harmonic(kv0, up(kv0)) + harmonic(kv1, up(kv1))
            ztiles[pl.ds(8 * (4 * a + j), 8), :] = row_group(upper)
    tiles[...] = dot(tiles[...], sum_matrix())
    ztiles[...] = dot(ztiles[...], top_matrix())

    def part(t):
        return tiles[pl.ds(8 * t, 8), :]

    pieces = []
    for a in range(4):
        parts = []
        for j in range(4):
            parts += [
                (X_LOW, j, part(4 * a + j)),
                (X_HIGH, j, part(4 * (a + 1) + j)),
                (Y_LOW, j, part(20 + 5 * a + j)),
                (Y_HIGH, j, part(20 + 5 * a + j + 1)),
                (Z_UP, j, ztiles[pl.ds(8 * (4 * a + j), 8), :]),
                (SOURCE, j, part(40 + 4 * a + j)),
            ]
        pieces.append(parts)
    out[...] = gather_tile(pieces)


def stack_tiles(buf, left, own, right):
    buf[0:4, :] = left[0:4, :]
    buf[4:8, :] = own[0:4, :]
    buf[8:12, :] = right[0:4, :]
    buf[12:16, :] = jnp.zeros((4, NZ), F32)
    return buf[...]


def widen(field, below, own, above):
    lane = iota((16, NZ), 1)

    def placed(v, at):
        shift = (at - 16 * field) % NZ
        return pltpu.roll(v, shift, 1) if shift else v

    wide = jnp.where(lane < 16, placed(below, 0), placed(own, 16))
    wide = jnp.where(lane < 32, wide, placed(above, 32))
    return jnp.where(lane < 48, wide, 0.0)


def coarse_sweeps(coefs, source):
    x_low, x_high, y_low, y_high, z_up, scale = coefs
    start = scale * source
    c = start
    for _ in range(SWEEPS):
        beside = x_low * pltpu.roll(c, 1, 0) + x_high * pltpu.roll(c, 15, 0)
        beside = beside + y_low * pltpu.roll(c, 4, 1) + y_high * pltpu.roll(c, NZ - 4, 1)
        beside = beside + z_up * up(c) + down(z_up * c)
        c = (1.0 - W) * c + (start + scale * beside)
    return c


def spread_coarse(c, spread):
    for k in range(6):
        lane = iota((NZ, NZ), 1)
        pick = jnp.where(iota((NZ, NZ), 0) == 4 * (k + 3) + lane // 32, 1.0, 0.0)
        spread[k] = dot(c, pick.astype(F32))


def neighbours(v, fx, fy, fz, i, at, size):
    here = v[i, pl.ds(at, size), :]
    total = fx[i, pl.ds(at, size), :] * v[i - 1, pl.ds(at, size), :]
    total = total + fx[i + 1, pl.ds(at, size), :] * v[i + 1, pl.ds(at, size), :]
    total = total + fy[i, pl.ds(at, size), :] * v[i, pl.ds(at - 1, size), :]
    total = total + fy[i, pl.ds(at + 1, size), :] * v[i, pl.ds(at + 1, size), :]
    z = fz[i, pl.ds(at, size), :]
    return here, total + z * up(here) + down(z * here)


def smooth(s1, d, fx, fy, fz, scale, spread):
    def plane(i, _):
        for at, size, j in CHUNKS:
            here, total = neighbours(s1, fx, fy, fz, i, at, size)
            value = (2.0 - W) * here + scale[i, pl.ds(at, size), :] * total
            d[i, pl.ds(at, size), :] = value + spread[j + 1, pl.ds((i + 5) // 2, 1), :]
        return 0

    lax.fori_loop(HX - 1, HX + NXL + 1, plane, 0)


def zero_pads(v):
    def plane(i, _):
        v[i, 0:8, :] = jnp.zeros((8, NZ), F32)
        v[i, ROWS - 8 : ROWS, :] = jnp.zeros((8, NZ), F32)
        return 0

    lax.fori_loop(0, PLANES, plane, 0)


def first_kernel(
    inside, table, cls, rhs, xlo, xhi, ylo, yhi, left, own, right, below, above,
    d_out, q_out, xm_lo, xm_hi, tile_out, coefs_out, fx, fy, fz, scale, centre,
    kh, kv, s1, d, stack, spread, tiles,
):
    khrow, kvrow = table[0:1, :], table[1:2, :]

    def put(i, at, size, classes, with_kv):
        index = classes.astype(jnp.int32)
        kh[i, pl.ds(at, size), :] = look_up(khrow, index)
        if with_kv:
            kv[i, pl.ds(at, size), :] = look_up(kvrow, index)

    def plane(x, _):
        i = x + HX
        put(i, OWN, NYL, cls[x], True)
        put(i, 8, 8, ylo[x], True)
        put(i, 144, 8, yhi[x], True)
        s1[i, 16:144, :] = rhs[x]
        s1[i, 8:16, :] = ylo[NXL + x]
        s1[i, 144:152, :] = yhi[NXL + x]
        return 0

    lax.fori_loop(0, NXL, plane, 0)
    for n in range(3):
        for base, msg, corner in ((0, xlo, 0), (HX + NXL, xhi, 3)):
            i = base + n
            with_kv = 0 < i < PLANES - 1
            put(i, OWN, NYL, msg[n], with_kv)
            put(i, 8, 8, below[corner + n], with_kv)
            put(i, 144, 8, above[corner + n], with_kv)
    for n in range(2):
        for i, msg, corner in ((1 + n, xlo, 6), (HX + NXL + n, xhi, 8)):
            s1[i, 16:144, :] = msg[3 + n]
            s1[i, 8:16, :] = below[corner + n]
            s1[i, 144:152, :] = above[corner + n]

    def pads(i, _):
        ones = jnp.ones((8, NZ), F32)
        kh[i, 0:8, :] = ones
        kh[i, ROWS - 8 : ROWS, :] = ones
        fy[i, ROWS - 8 : ROWS, :] = ones
        return 0

    lax.fori_loop(0, PLANES, pads, 0)
    zero_pads(s1)
    zero_pads(d)

    mid = stack_tiles(stack, left, own, right)
    low = stack_tiles(stack, below[10], below[11], below[12])
    high = stack_tiles(stack, above[10], above[11], above[12])
    wide = [widen(k, low, mid, high) for k in range(6)]
    total = wide[0] + wide[1] + wide[2] + wide[3] + wide[4] + down(wide[4])
    valid = total > 0.0
    wide_scale = jnp.where(valid, W / jnp.where(valid, total, 1.0), 0.0)
    coefs = wide[:5] + [wide_scale]
    for k in range(6):
        coefs_out[k] = coefs[k]
    spread_coarse(coarse_sweeps(coefs, wide[SOURCE]), spread)

    def faces(i, _):
        for at, size, _j in CHUNKS:
            rows = pl.ds(at, size)
            here = kh[i, rows, :]
            fx[i, rows, :] = harmonic(kh[i - 1, rows, :], here)
            fy[i, rows, :] = harmonic(kh[i, pl.ds(at - 1, size), :], here)
            k = kv[i, rows, :]
            z = harmonic(k, up(k))
            fz[i, rows, :] = jnp.where(iota((size, NZ), 1) < NZ - 1, z, 0.0)
        return 0

    lax.fori_loop(1, PLANES - 1, faces, 0)
    for at, size, _j in CHUNKS:
        rows = pl.ds(at, size)
        fx[PLANES - 1, rows, :] = harmonic(
            kh[PLANES - 2, rows, :], kh[PLANES - 1, rows, :]
        )

    @pl.when(inside[0] < 0.5)
    def _():
        fx[HX] = 2.0 * kh[HX]

    @pl.when(inside[1] < 0.5)
    def _():
        fx[HX + NXL] = 2.0 * kh[HX + NXL - 1]

    @pl.when(inside[2] < 0.5)
    def _():
        for i in range(1, PLANES - 1):
            fy[i, OWN : OWN + 1, :] = 2.0 * kh[i, OWN : OWN + 1, :]

    @pl.when(inside[3] < 0.5)
    def _():
        for i in range(1, PLANES - 1):
            fy[i, 144:145, :] = 2.0 * kh[i, 143:144, :]

    def scales(i, _):
        x_mask = jnp.where(i < HX, inside[0], jnp.where(i >= HX + NXL, inside[1], 1.0))
        for at, size, j in CHUNKS:
            rows, above_rows = pl.ds(at, size), pl.ds(at + 1, size)
            z = fz[i, rows, :]
            total = fx[i, rows, :] + fx[i + 1, rows, :]
            total = total + fy[i, rows, :] + fy[i, above_rows, :] + (z + down(z))
            mask = x_mask
            if j == -1:
                mask = mask * inside[2]
            if j == 4:
                mask = mask * inside[3]
            inverse = (W * mask) / total
            centre[i, rows, :] = total
            scale[i, rows, :] = inverse
            s1[i, rows, :] = inverse * s1[i, rows, :]
        return 0

    lax.fori_loop(1, PLANES - 1, scales, 0)
    smooth(s1, d, fx, fy, fz, scale, spread)

    def image(x, _):
        i = x + HX
        for at, size, j in OWN_CHUNKS:
            here, total = neighbours(d, fx, fy, fz, i, at, size)
            q = centre[i, pl.ds(at, size), :] * here - total
            q_out[x, pl.ds(at - OWN, size), :] = q
            d_out[x, pl.ds(at - OWN, size), :] = here
        return 0

    lax.fori_loop(0, NXL, image, 0)
    for a in range(4):
        for j in range(4):
            rows = pl.ds(32 * j, 32)
            source = q_out[2 * a, rows, :] + q_out[2 * a + 1, rows, :]
            tiles[pl.ds(8 * (4 * a + j), 8), :] = row_group(source)
    tiles[...] = dot(tiles[...], sum_matrix())
    tile = gather_tile(
        [
            [(SOURCE, j, tiles[pl.ds(8 * (4 * a + j), 8), :]) for j in range(4)]
            for a in range(4)
        ]
    )
    tile_out[...] = tile
    for n in range(2):
        xm_lo[pl.ds(128 * n, 128), :] = q_out[n]
        xm_hi[pl.ds(128 * n, 128), :] = q_out[NXL - 2 + n]
    xm_lo[256:264, :] = tile
    xm_hi[256:264, :] = tile


def second_kernel(
    rhs, d0, q0, xlo, xhi, own, below, above, coefs, fx, fy, fz, scale, centre,
    p_out, s_out, dots, s1, d, stack, spread,
):
    zero_pads(s1)
    zero_pads(d)
    mid = stack_tiles(stack, xlo[256:264, :], own[...], xhi[256:264, :])
    low = stack_tiles(stack, below[12], below[13], below[14])
    high = stack_tiles(stack, above[12], above[13], above[14])
    wide = widen(SOURCE, low, mid, high)
    spread_coarse(coarse_sweeps([coefs[k] for k in range(6)], wide), spread)

    def rims(i):
        s1[i, 8:16, :] = scale[i, 8:16, :] * below[i - 1]
        s1[i, 144:152, :] = scale[i, 144:152, :] * above[i - 1]

    def plane(x, _):
        i = x + HX
        s1[i, 16:144, :] = scale[i, 16:144, :] * q0[x]
        rims(i)
        return 0

    lax.fori_loop(0, NXL, plane, 0)
    for n in range(2):
        for i, msg in ((1 + n, xlo), (HX + NXL + n, xhi)):
            s1[i, 16:144, :] = scale[i, 16:144, :] * msg[pl.ds(128 * n, 128), :]
            rims(i)
    smooth(s1, d, fx, fy, fz, scale, spread)

    def image(x, sums):
        i = x + HX
        for at, size, j in OWN_CHUNKS:
            rows = pl.ds(at - OWN, size)
            p, total = neighbours(d, fx, fy, fz, i, at, size)
            s = centre[i, pl.ds(at, size), :] * p - total
            p_out[x, rows, :] = p
            s_out[x, rows, :] = s
            r, dd, q = rhs[x, rows, :], d0[x, rows, :], q0[x, rows, :]
            pairs = ((r, dd), (dd, q), (r, p), (q, p), (dd, s), (p, s))
            sums = tuple(
                acc + row_group(u * v) for acc, (u, v) in zip(sums, pairs)
            )
        return sums

    zero = jnp.zeros((8, NZ), F32)
    sums = lax.fori_loop(0, NXL, image, (zero,) * 6)
    sublane = iota((8, NZ), 0)
    tile = zero
    for n, acc in enumerate(sums):
        tile = jnp.where(sublane == n, jnp.sum(acc, axis=0, keepdims=True), tile)
    for n in range(dots.shape[0]):
        dots[n] = tile


def last_kernel(parts, rhs, d0, q0, p, s, x_out, r_out):
    total = parts[0]
    for n in range(1, parts.shape[0]):
        total = total + parts[n]
    sums = jnp.sum(total, axis=1, keepdims=True)
    rd, dq, rp, qp, ds, ps = [sums[n : n + 1, :] for n in range(6)]
    a0 = rd / dq
    rz = rd - a0 * rp - a0 * dq + a0 * a0 * qp
    ratio = rz / rd
    grow = 1.0 + ratio
    curve = grow * grow * dq - grow * a0 * (ds + qp) + a0 * a0 * ps
    a1 = rz / curve
    u = jnp.broadcast_to(a0 + a1 * grow, (8, NZ))[0:1, :]
    v = jnp.broadcast_to(a1 * a0, (8, NZ))[0:1, :]

    def plane(x, _):
        for at in range(0, NYL, 32):
            rows = pl.ds(at, 32)
            x_out[x, rows, :] = u * d0[x, rows, :] - v * p[x, rows, :]
            r_out[x, rows, :] = rhs[x, rows, :] - u * q0[x, rows, :] + v * s[x, rows, :]
        return 0

    lax.fori_loop(0, NXL, plane, 0)


VMEM = pl.BlockSpec(memory_space=pltpu.VMEM)
SMEM = pl.BlockSpec(memory_space=pltpu.SMEM)


def call(kernel, name, operands, outs, scratch, scalars=0):
    return pl.pallas_call(
        kernel,
        name=name,
        out_shape=[jax.ShapeDtypeStruct(s, F32) for s in outs],
        in_specs=[SMEM] * scalars + [VMEM] * (len(operands) - scalars),
        out_specs=[VMEM] * len(outs),
        scratch_shapes=[pltpu.VMEM(s, F32) for s in scratch],
        compiler_params=pltpu.CompilerParams(vmem_limit_bytes=40 * 1024 * 1024),
    )(*operands)


def upward(values, axis):
    count = lax.axis_size(axis)
    return lax.ppermute(values, axis, [(i, i + 1) for i in range(count - 1)])


def downward(values, axis):
    count = lax.axis_size(axis)
    return lax.ppermute(values, axis, [(i + 1, i) for i in range(count - 1)])


def axis_total(tiles, axis, last=False):
    tiles = lax.all_to_all(tiles, axis, 0, 0)
    if last:
        return tiles
    return tiles.sum(0)


def body(right_side, perm_class, perm_table):
    x_at, y_at = lax.axis_index(X_AXES), lax.axis_index("sy")
    x_end, y_end = lax.axis_size(X_AXES) - 1, lax.axis_size("sy") - 1
    inside = jnp.stack([x_at > 0, x_at < x_end, y_at > 0, y_at < y_end]).astype(F32)
    table = jnp.pad(perm_table, ((0, 6), (0, NZ - perm_table.shape[1])))
    classes = perm_class.astype(F32)
    xlo = upward(jnp.concatenate([classes[-3:], right_side[-2:]]), X_AXES)
    xhi = downward(jnp.concatenate([classes[:3], right_side[:2]]), X_AXES)
    ylo = upward(jnp.concatenate([classes[:, -8:], right_side[:, -8:]]), "sy")
    yhi = downward(jnp.concatenate([classes[:, :8], right_side[:, :8]]), "sy")

    fine = (inside, table, perm_class, right_side, xlo, xhi, ylo, yhi)
    (own,) = call(
        coarse_kernel, "coarse", fine, [(8, NZ)],
        [(NXL + 2, 144, NZ), (56 * 8, NZ), (16 * 8, NZ)], 1,
    )
    left, right = upward(own, X_AXES), downward(own, X_AXES)

    def rim(rows):
        parts = [xlo[:3, rows], xhi[:3, rows], xlo[3:, rows], xhi[3:, rows]]
        return jnp.concatenate(parts + [left[None], own[None], right[None]])

    below = upward(rim(slice(NYL - 8, NYL)), "sy")
    above = downward(rim(slice(0, 8)), "sy")

    block, big = (NXL, NYL, NZ), (PLANES, ROWS, NZ)
    d0, q0, xm_lo, xm_hi, tile, coefs, fx, fy, fz, scale, centre = call(
        first_kernel, "first", fine + (left, own, right, below, above),
        [block, block, (264, NZ), (264, NZ), (8, NZ), (6, 16, NZ)] + [big] * 5,
        [big] * 4 + [(16, NZ), (6, 16, NZ), (16 * 8, NZ)], 1,
    )
    qlo, qhi = upward(xm_hi, X_AXES), downward(xm_lo, X_AXES)

    def rim_q(at):
        parts = [qlo[at : at + 8][None], qlo[128 + at : 136 + at][None], q0[:, at : at + 8]]
        parts += [qhi[at : at + 8][None], qhi[128 + at : 136 + at][None]]
        return jnp.concatenate(parts + [qlo[256:][None], tile[None], qhi[256:][None]])

    below = upward(rim_q(NYL - 8), "sy")
    above = downward(rim_q(0), "sy")
    members = lax.axis_size("cg")
    p, s, dots = call(
        second_kernel, "second",
        (right_side, d0, q0, qlo, qhi, tile, below, above, coefs, fx, fy, fz, scale, centre),
        [block, block, (members, 8, NZ)],
        [big] * 2 + [(16, NZ), (6, 16, NZ)],
    )
    for axis, after in (("cg", "sy"), ("sy", "sx"), ("sx", None)):
        dots = axis_total(dots, axis, after is None)
        if after is not None:
            dots = jnp.broadcast_to(dots[None], (lax.axis_size(after), 8, NZ))
    return tuple(
        call(last_kernel, "last", (dots, right_side, d0, q0, p, s), [block, block], [])
    )


def solution(mesh):
    cells = P(X_AXES, "sy", None)
    return jax.shard_map(
        body,
        mesh=mesh,
        in_specs=(cells, cells, P()),
        out_specs=(cells, cells),
        check_vma=False,
    )
```

time: 572 us -> 121 us (0.21)
  blocking collectives: 341 us -> 52.1 us
  starting transfers between devices: 133 us -> 36.3 us
  other arithmetic: 56.5 us -> 1.24 us
  local copies, waits for them, and re-layouts: 23.7 us -> 1.11 us
  Pallas kernels: 0 us -> 15.4 us
    psum x3 -> x0, blocking collectives: 341 us -> none  [the longest x2 239 us: residual_fit(): return lax.psum(jnp.sum(residual * smoothed), ('sx', 'sy', 'cg'))]
    ppermute x44 -> x12, starting transfers between devices: 133 us -> 36.3 us  [the longest x6 22.7 us: upward(): return lax.ppermute(values, axis, [(i, i + 1) for i in range(count - 1)])]
    all_to_all x0 -> x3, blocking collectives: none -> 52.1 us  [axis_total(): tiles = lax.all_to_all(tiles, axis, 0, 0)]
    select_n x3 -> x0, other arithmetic: 24.5 us -> none  [the longest x1 12.7 us: fine_coefs(): horizontal = jnp.where(matches, perm_table[0, category], horizontal)]
    reduce_sum x10 -> x2, other arithmetic: 16.2 us -> 0.02 us  [axis_total(): return tiles.sum(0)]
    pallas_call x0 -> x4, Pallas kernels: none -> 15.4 us  [call(): pl.pallas_call(kernel, name=name, out_shape=[jax.ShapeDtypeStruct(s, F32)...]
    reshape x8 -> x0, local copies, waits for them, and re-layouts: 14.7 us -> none  [the longest x6 8.55 us: block_sum(): values.reshape(count_x, size_x // count_x, count_y, size_y // count_y, co...]
    ppermute x44 -> x12, waiting for transfers between devices: 9.25 us -> 12.2 us  [the longest x6 8.61 us: downward(): return lax.ppermute(values, axis, [(i + 1, i) for i in range(count - 1)])]
  transfers between devices with their start and end apart: 44 -> 12, of which waited for: 12 -> 5; matrix products, arithmetic and copies ran while one was open for 6% -> 0% of each run, Pallas kernels for 0% -> 0%
where the time goes in v1:
time: 121 us; the launch traced here: 119 us
  blocking collectives  52.1 us (43%)
  starting transfers between devices  36.3 us (30%)
  Pallas kernels  15.4 us (13%)
  waiting for transfers between devices  12.2 us (10%)
  other arithmetic  1.24 us (1%)
    all_to_all x3, blocking collectives, axis_total(): tiles = lax.all_to_all(tiles, axis, 0, 0)  52.1 us
    ppermute x6, starting transfers between devices, upward(): return lax.ppermute(values, axis, [(i, i + 1) for i in range(count - 1)])  22.7 us
    pallas_call x4, Pallas kernels, call(): pl.pallas_call(kernel, name=name, out_shape=[jax.ShapeDtypeStruct(s, F32)...  15.4 us
    ppermute x6, starting transfers between devices, downward(): return lax.ppermute(values, axis, [(i + 1, i) for i in range(count - 1)])  13.7 us
    ppermute x6, waiting for transfers between devices, downward(): return lax.ppermute(values, axis, [(i + 1, i) for i in range(count - 1)])  8.61 us
    ppermute x6, waiting for transfers between devices, upward(): return lax.ppermute(values, axis, [(i, i + 1) for i in range(count - 1)])  3.62 us
  transfers between devices with their start and end apart: 12, of which 5 were waited for; matrix products, arithmetic and copies ran while one was open for 0% of the time, Pallas kernels for 0%

profile of v1, /device:TPU:1, one launch (start us, length us, event | category | flops | bytes accessed | tf_op | source)
XLA Modules:
  0.0 119.4 jit_solution(14515510965383633992)
XLA Ops:
  0.6 1.0 fusion.3
  1.6 1.1 convert_element_type.9
  2.7 0.0 copy-start
  2.7 0.0 copy-start.2
  2.7 0.0 copy-start.1
  2.8 4.6 %collective-permute-start = (f32[5,128,128]{2,1,0:T(8,128)S(1)}, f32[5,128,128]{2,1,0:T(8,128)S(1)}, u32[]{:S(2)}, u32[]{:S(2)}) collective-permute-start(f32[5,128,128]{2,1,0:T(8,128)S(1)} %pad_maximum_fusion), channel_id=1, source_target_pairs={{0,1},{1,2},{2,3},{3,4},{4,5},{5,6},{6,7},{7,64},{64,65},{65,66},{... | collective-permute-start | bytes 983048 | tf_op jit(solution)/shard_map/ppermute | solution.py:456
  7.5 5.6 %collective-permute-start.1 = (f32[5,128,128]{2,1,0:T(8,128)S(1)}, f32[5,128,128]{2,1,0:T(8,128)S(1)}, u32[]{:S(2)}, u32[]{:S(2)}) collective-permute-start(f32[5,128,128]{2,1,0:T(8,128)S(1)} %pad_maximum_fusion.1), channel_id=1, source_target_pairs={{1,0},{2,1},{3,2},{4,3},{5,4},{6,5},{7,6},{64,7},{65,64},{66,65},{... | collective-permute-start | bytes 983048 | tf_op jit(solution)/shard_map/ppermute | solution.py:461
  13.1 1.3 %collective-permute-start.2 = (f32[16,8,128]{2,1,0:T(8,128)S(1)}, f32[16,8,128]{2,1,0:T(8,128)S(1)}, u32[]{:S(2)}, u32[]{:S(2)}) collective-permute-start(f32[16,8,128]{2,1,0:T(8,128)S(1)} %pad_maximum_fusion.2), channel_id=1, source_target_pairs={{0,8},{8,16},{16,24},{24,32},{32,40},{40,48},{48,56},{1,9},{9,17},... | collective-permute-start | bytes 196616 | tf_op jit(solution)/shard_map/ppermute | solution.py:456
  14.4 1.3 %collective-permute-start.3 = (f32[16,8,128]{2,1,0:T(8,128)S(1)}, f32[16,8,128]{2,1,0:T(8,128)S(1)}, u32[]{:S(2)}, u32[]{:S(2)}) collective-permute-start(f32[16,8,128]{2,1,0:T(8,128)S(1)} %pad_maximum_fusion.3), channel_id=1, source_target_pairs={{8,0},{16,8},{24,16},{32,24},{40,32},{48,40},{56,48},{9,1},{17,9},... | collective-permute-start | bytes 196616 | tf_op jit(solution)/shard_map/ppermute | solution.py:461
  15.8 0.1 add_convert_fusion.inside
  15.8 0.0 collective-permute-done.2.ylo
  15.9 4.3 %collective-permute-done.3.yhi = f32[16,8,128]{2,1,0:T(8,128)S(1)} collective-permute-done((f32[16,8,128]{2,1,0:T(8,128)S(1)}, f32[16,8,128]{2,1,0:T(8,128)S(1)}, u32[]{:S(2)}, u32[]{:S(2)}) %collective-permute-start.3) | collective-permute-done | bytes 65568 | tf_op jit(solution)/shard_map/ppermute | solution.py:461
  20.1 2.6 %coarse.1.own = f32[8,128]{1,0:T(8,128)S(1)} custom-call(f32[4]{0:T(128)S(1)} %add_convert_fusion.inside, f32[8,128]{1,0:T(8,128)S(1)} %pad.4.table, s32[8,128,128]{2,1,0:T(8,128)S(1)} %copy-done.1, f32[8,128,128]{2,1,0:T(8,128)S(1)} %copy-done, f32[5,128,128]{2,1,0:T(8,128)S(1)} %collective-permute-done.xlo, f32[5,128,128]{2,1,0:T(8,128)S(1)} %collective-permute-done.1.xhi, ...), custom_call_target="tpu_custom_call" | custom-call | tf_op jit(solution)/shard_map/coarse/pallas_call | solution.py:443
  22.7 2.3 %collective-permute-start.5 = (f32[8,128]{1,0:T(8,128)S(1)}, f32[8,128]{1,0:T(8,128)S(1)}, u32[]{:S(2)}, u32[]{:S(2)}) collective-permute-start(f32[8,128]{1,0:T(8,128)S(1)} %coarse.1.own), channel_id=1, source_target_pairs={{1,0},{2,1},{3,2},{4,3},{5,4},{6,5},{7,6},{64,7},{65,64},{66,65},{... | collective-permute-start | bytes 12296 | tf_op jit(solution)/shard_map/ppermute | solution.py:461
  25.0 3.3 %collective-permute-start.4 = (f32[8,128]{1,0:T(8,128)S(1)}, f32[8,128]{1,0:T(8,128)S(1)}, u32[]{:S(2)}, u32[]{:S(2)}) collective-permute-start(f32[8,128]{1,0:T(8,128)S(1)} %coarse.1.own), channel_id=1, source_target_pairs={{0,1},{1,2},{2,3},{3,4},{4,5},{5,6},{6,7},{7,64},{64,65},{65,66},{... | collective-permute-start | bytes 12296 | tf_op jit(solution)/shard_map/ppermute | solution.py:456
  28.3 0.7 collective-permute-done.4.left
  29.0 1.3 %collective-permute-start.7 = (f32[13,8,128]{2,1,0:T(8,128)S(1)}, f32[13,8,128]{2,1,0:T(8,128)S(1)}, u32[]{:S(2)}, u32[]{:S(2)}) collective-permute-start(f32[13,8,128]{2,1,0:T(8,128)S(1)} %get-tuple-element.62), channel_id=1, source_target_pairs={{8,0},{16,8},{24,16},{32,24},{40,32},{48,40},{56,48},{9,1},{17,9},... | collective-permute-start | bytes 159752 | tf_op jit(solution)/shard_map/ppermute | solution.py:461
  30.3 4.0 %collective-permute-start.6 = (f32[13,8,128]{2,1,0:T(8,128)S(1)}, f32[13,8,128]{2,1,0:T(8,128)S(1)}, u32[]{:S(2)}, u32[]{:S(2)}) collective-permute-start(f32[13,8,128]{2,1,0:T(8,128)S(1)} %get-tuple-element.63), channel_id=1, source_target_pairs={{0,8},{8,16},{16,24},{24,32},{32,40},{40,48},{48,56},{1,9},{9,17},... | collective-permute-start | bytes 159752 | tf_op jit(solution)/shard_map/ppermute | solution.py:456
  34.3 1.6 %collective-permute-done.6.below = f32[13,8,128]{2,1,0:T(8,128)S(1)} collective-permute-done((f32[13,8,128]{2,1,0:T(8,128)S(1)}, f32[13,8,128]{2,1,0:T(8,128)S(1)}, u32[]{:S(2)}, u32[]{:S(2)}) %collective-permute-start.6) | collective-permute-done | bytes 53280 | tf_op jit(solution)/shard_map/ppermute | solution.py:456
  35.9 8.2 %first.1 = (f32[8,128,128]{2,1,0:T(8,128)S(1)}, f32[8,128,128]{2,1,0:T(8,128)S(1)}, f32[264,128]{1,0:T(8,128)S(1)}, f32[264,128]{1,0:T(8,128)S(1)}, f32[8,128]{1...) custom-call(f32[4]{0:T(128)S(1)} %add_convert_fusion.inside, ...), custom_call_target="tpu_custom_call" | custom-call | tf_op jit(solution)/shard_map/first/pallas_call | solution.py:443
  44.2 4.9 %collective-permute-start.8 = (f32[264,128]{1,0:T(8,128)S(1)}, f32[264,128]{1,0:T(8,128)S(1)}, u32[]{:S(2)}, u32[]{:S(2)}) collective-permute-start(f32[264,128]{1,0:T(8,128)S(1)} %get-tuple-element.18), channel_id=1, source_target_pairs={{0,1},{1,2},{2,3},{3,4},{4,5},{5,6},{6,7},{7,64},{64,65},{65,66},{... | collective-permute-start | bytes 405512 | tf_op jit(solution)/shard_map/ppermute | solution.py:456
  49.1 1.9 %collective-permute-start.9 = (f32[264,128]{1,0:T(8,128)S(1)}, f32[264,128]{1,0:T(8,128)S(1)}, u32[]{:S(2)}, u32[]{:S(2)}) collective-permute-start(f32[264,128]{1,0:T(8,128)S(1)} %get-tuple-element.19), channel_id=1, source_target_pairs={{1,0},{2,1},{3,2},{4,3},{5,4},{6,5},{7,6},{64,7},{65,64},{66,65},{... | collective-permute-start | bytes 405512 | tf_op jit(solution)/shard_map/ppermute | solution.py:461
  51.0 0.0 collective-permute-done.8.xlo
  51.1 4.4 %collective-permute-done.9.xhi = f32[264,128]{1,0:T(8,128)S(1)} collective-permute-done((f32[264,128]{1,0:T(8,128)S(1)}, f32[264,128]{1,0:T(8,128)S(1)}, u32[]{:S(2)}, u32[]{:S(2)}) %collective-permute-start.9) | collective-permute-done | bytes 135200 | tf_op jit(solution)/shard_map/ppermute | solution.py:461
  55.4 1.3 %collective-permute-start.11 = (f32[15,8,128]{2,1,0:T(8,128)S(1)}, f32[15,8,128]{2,1,0:T(8,128)S(1)}, u32[]{:S(2)}, u32[]{:S(2)}) collective-permute-start(f32[15,8,128]{2,1,0:T(8,128)S(1)} %get-tuple-element.48), channel_id=1, source_target_pairs={{8,0},{16,8},{24,16},{32,24},{40,32},{48,40},{56,48},{9,1},{17,9},... | collective-permute-start | bytes 184328 | tf_op jit(solution)/shard_map/ppermute | solution.py:461
  56.7 4.6 %collective-permute-start.10 = (f32[15,8,128]{2,1,0:T(8,128)S(1)}, f32[15,8,128]{2,1,0:T(8,128)S(1)}, u32[]{:S(2)}, u32[]{:S(2)}) collective-permute-start(f32[15,8,128]{2,1,0:T(8,128)S(1)} %get-tuple-element.49), channel_id=1, source_target_pairs={{0,8},{8,16},{16,24},{24,32},{32,40},{40,48},{48,56},{1,9},{9,17},... | collective-permute-start | bytes 184328 | tf_op jit(solution)/shard_map/ppermute | solution.py:456
  61.3 1.3 %collective-permute-done.10.below = f32[15,8,128]{2,1,0:T(8,128)S(1)} collective-permute-done((f32[15,8,128]{2,1,0:T(8,128)S(1)}, f32[15,8,128]{2,1,0:T(8,128)S(1)}, u32[]{:S(2)}, u32[]{:S(2)}) %collective-permute-start.10) | collective-permute-done | bytes 61472 | tf_op jit(solution)/shard_map/ppermute | solution.py:456
  62.6 3.1 %second.1 = (f32[8,128,128]{2,1,0:T(8,128)S(1)}, f32[8,128,128]{2,1,0:T(8,128)S(1)}, f32[8,8,128]{2,1,0:T(8,128)S(1)}) custom-call(f32[8,128,128]{2,1,0:T(8,128)S(1)} %copy-done, f32[8,128,128]{2,1,0:T(8,128)S(1)} %get-tuple-element.16.d0, f32[8,128,128]{2,1,0:T(8,128)S(1)} %get-tuple-element.17.q0, f32[264,128]{1,0:T(8,128)S(1)} %collective-permute-done.8.xlo, ...), custom_call_target="tpu_custom_call" | custom-call | tf_op jit(solution)/shard_map/second/pallas_call | solution.py:443
  65.7 14.8 %all_to_all.15 = f32[8,8,128]{2,1,0:T(8,128)S(1)} all-to-all(f32[8,8,128]{2,1,0:T(8,128)S(1)} %get-tuple-element.27), channel_id=1, replica_groups=mesh['sx'=8,'sy'=8,'cg'=8] {'cg'}, dimensions={0} | all-to-all | bytes 65536 | tf_op jit(solution)/shard_map/all_to_all | solution.py:465
  80.6 18.8 %all_to_all.16 = f32[8,8,128]{2,1,0:T(8,128)S(1)} all-to-all(f32[8,8,128]{2,1,0:T(8,128)S(1)} %broadcast_in_dim.74), channel_id=1, replica_groups=mesh['sx'=8,'sy'=8,'cg'=8] {'sy'}, dimensions={0} | all-to-all | bytes 65536 | tf_op jit(solution)/shard_map/all_to_all | solution.py:465
  99.4 18.5 %all_to_all.17.parts = f32[8,8,128]{2,1,0:T(8,128)S(1)} all-to-all(f32[8,8,128]{2,1,0:T(8,128)S(1)} %broadcast_in_dim.75), channel_id=1, replica_groups=mesh['sx'=8,'sy'=8,'cg'=8] {'sx'}, dimensions={0} | all-to-all | bytes 65536 | tf_op jit(solution)/shard_map/all_to_all | solution.py:465
  117.9 1.5 %last.1 = (f32[8,128,128]{2,1,0:T(8,128)}, f32[8,128,128]{2,1,0:T(8,128)}) custom-call(f32[8,8,128]{2,1,0:T(8,128)S(1)} %all_to_all.17.parts, f32[8,128,128]{2,1,0:T(8,128)S(1)} %copy-done, f32[8,128,128]{2,1,0:T(8,128)S(1)} %get-tuple-element.16.d0, f32[8,128,128]{2,1,0:T(8,128)S(1)} %get-tuple-element.17.q0, f32[8,128,128]{2,1,0:T(8,128)S(1)} %get-tuple-element.28.p, ...), custom_call_target="tpu_custom_call" | custom-call | tf_op jit(solution)/shard_map/last/pallas_call | solution.py:443
  (35 shorter events, 0.2 us)
Async XLA Ops:
  2.7 10.3 %copy-start = (f32[8,128,128]{2,1,0:T(8,128)S(1)}, f32[8,128,128]{2,1,0:T(8,128)}, u32[]{:S(2)}) copy-start(f32[8,128,128]{2,1,0:T(8,128)} %rhs.7) | copy-start | bytes 1572868
  2.7 13.0 %copy-start.2 = (f32[2,16]{1,0:T(2,128)S(1)}, f32[2,16]{1,0:T(2,128)}, u32[]{:S(2)}) copy-start(f32[2,16]{1,0:T(2,128)} %param.5) | copy-start | bytes 388
  2.7 17.4 %copy-start.1 = (s32[8,128,128]{2,1,0:T(8,128)S(1)}, s32[8,128,128]{2,1,0:T(8,128)}, u32[]{:S(2)}) copy-start(s32[8,128,128]{2,1,0:T(8,128)} %cls.3) | copy-start | bytes 1572868
  2.8 17.3 %collective-permute-start = (f32[5,128,128]{2,1,0:T(8,128)S(1)}, f32[5,128,128]{2,1,0:T(8,128)S(1)}, u32[]{:S(2)}, u32[]{:S(2)}) collective-permute-start(f32[5,128,128]{2,1,0:T(8,128)S(1)} %pad_maximum_fusion), channel_id=1, source_target_pairs={{0,1},{1,2},{2,3},{3,4},{4,5},{5,6},{6,7},{7,64},{64,65},{65,66},{... | collective-permute-start | bytes 983048 | tf_op jit(solution)/shard_map/ppermute | solution.py:456
  7.5 12.6 %collective-permute-start.1 = (f32[5,128,128]{2,1,0:T(8,128)S(1)}, f32[5,128,128]{2,1,0:T(8,128)S(1)}, u32[]{:S(2)}, u32[]{:S(2)}) collective-permute-start(f32[5,128,128]{2,1,0:T(8,128)S(1)} %pad_maximum_fusion.1), channel_id=1, source_target_pairs={{1,0},{2,1},{3,2},{4,3},{5,4},{6,5},{7,6},{64,7},{65,64},{66,65},{... | collective-permute-start | bytes 983048 | tf_op jit(solution)/shard_map/ppermute | solution.py:461
  13.1 2.8 %collective-permute-start.2 = (f32[16,8,128]{2,1,0:T(8,128)S(1)}, f32[16,8,128]{2,1,0:T(8,128)S(1)}, u32[]{:S(2)}, u32[]{:S(2)}) collective-permute-start(f32[16,8,128]{2,1,0:T(8,128)S(1)} %pad_maximum_fusion.2), channel_id=1, source_target_pairs={{0,8},{8,16},{16,24},{24,32},{32,40},{40,48},{48,56},{1,9},{9,17},... | collective-permute-start | bytes 196616 | tf_op jit(solution)/shard_map/ppermute | solution.py:456
  14.4 5.7 %collective-permute-start.3 = (f32[16,8,128]{2,1,0:T(8,128)S(1)}, f32[16,8,128]{2,1,0:T(8,128)S(1)}, u32[]{:S(2)}, u32[]{:S(2)}) collective-permute-start(f32[16,8,128]{2,1,0:T(8,128)S(1)} %pad_maximum_fusion.3), channel_id=1, source_target_pairs={{8,0},{16,8},{24,16},{32,24},{40,32},{48,40},{56,48},{9,1},{17,9},... | collective-permute-start | bytes 196616 | tf_op jit(solution)/shard_map/ppermute | solution.py:461
  22.7 6.3 %collective-permute-start.5 = (f32[8,128]{1,0:T(8,128)S(1)}, f32[8,128]{1,0:T(8,128)S(1)}, u32[]{:S(2)}, u32[]{:S(2)}) collective-permute-start(f32[8,128]{1,0:T(8,128)S(1)} %coarse.1.own), channel_id=1, source_target_pairs={{1,0},{2,1},{3,2},{4,3},{5,4},{6,5},{7,6},{64,7},{65,64},{66,65},{... | collective-permute-start | bytes 12296 | tf_op jit(solution)/shard_map/ppermute | solution.py:461
  25.0 4.0 %collective-permute-start.4 = (f32[8,128]{1,0:T(8,128)S(1)}, f32[8,128]{1,0:T(8,128)S(1)}, u32[]{:S(2)}, u32[]{:S(2)}) collective-permute-start(f32[8,128]{1,0:T(8,128)S(1)} %coarse.1.own), channel_id=1, source_target_pairs={{0,1},{1,2},{2,3},{3,4},{4,5},{5,6},{6,7},{7,64},{64,65},{65,66},{... | collective-permute-start | bytes 12296 | tf_op jit(solution)/shard_map/ppermute | solution.py:456
  29.0 5.3 %collective-permute-start.7 = (f32[13,8,128]{2,1,0:T(8,128)S(1)}, f32[13,8,128]{2,1,0:T(8,128)S(1)}, u32[]{:S(2)}, u32[]{:S(2)}) collective-permute-start(f32[13,8,128]{2,1,0:T(8,128)S(1)} %get-tuple-element.62), channel_id=1, source_target_pairs={{8,0},{16,8},{24,16},{32,24},{40,32},{48,40},{56,48},{9,1},{17,9},... | collective-permute-start | bytes 159752 | tf_op jit(solution)/shard_map/ppermute | solution.py:461
  30.3 5.6 %collective-permute-start.6 = (f32[13,8,128]{2,1,0:T(8,128)S(1)}, f32[13,8,128]{2,1,0:T(8,128)S(1)}, u32[]{:S(2)}, u32[]{:S(2)}) collective-permute-start(f32[13,8,128]{2,1,0:T(8,128)S(1)} %get-tuple-element.63), channel_id=1, source_target_pairs={{0,8},{8,16},{16,24},{24,32},{32,40},{40,48},{48,56},{1,9},{9,17},... | collective-permute-start | bytes 159752 | tf_op jit(solution)/shard_map/ppermute | solution.py:456
  44.2 6.9 %collective-permute-start.8 = (f32[264,128]{1,0:T(8,128)S(1)}, f32[264,128]{1,0:T(8,128)S(1)}, u32[]{:S(2)}, u32[]{:S(2)}) collective-permute-start(f32[264,128]{1,0:T(8,128)S(1)} %get-tuple-element.18), channel_id=1, source_target_pairs={{0,1},{1,2},{2,3},{3,4},{4,5},{5,6},{6,7},{7,64},{64,65},{65,66},{... | collective-permute-start | bytes 405512 | tf_op jit(solution)/shard_map/ppermute | solution.py:456
  49.1 6.3 %collective-permute-start.9 = (f32[264,128]{1,0:T(8,128)S(1)}, f32[264,128]{1,0:T(8,128)S(1)}, u32[]{:S(2)}, u32[]{:S(2)}) collective-permute-start(f32[264,128]{1,0:T(8,128)S(1)} %get-tuple-element.19), channel_id=1, source_target_pairs={{1,0},{2,1},{3,2},{4,3},{5,4},{6,5},{7,6},{64,7},{65,64},{66,65},{... | collective-permute-start | bytes 405512 | tf_op jit(solution)/shard_map/ppermute | solution.py:461
  55.4 5.9 %collective-permute-start.11 = (f32[15,8,128]{2,1,0:T(8,128)S(1)}, f32[15,8,128]{2,1,0:T(8,128)S(1)}, u32[]{:S(2)}, u32[]{:S(2)}) collective-permute-start(f32[15,8,128]{2,1,0:T(8,128)S(1)} %get-tuple-element.48), channel_id=1, source_target_pairs={{8,0},{16,8},{24,16},{32,24},{40,32},{48,40},{56,48},{9,1},{17,9},... | collective-permute-start | bytes 184328 | tf_op jit(solution)/shard_map/ppermute | solution.py:461
  56.7 5.9 %collective-permute-start.10 = (f32[15,8,128]{2,1,0:T(8,128)S(1)}, f32[15,8,128]{2,1,0:T(8,128)S(1)}, u32[]{:S(2)}, u32[]{:S(2)}) collective-permute-start(f32[15,8,128]{2,1,0:T(8,128)S(1)} %get-tuple-element.49), channel_id=1, source_target_pairs={{0,8},{8,16},{16,24},{24,32},{32,40},{40,48},{48,56},{1,9},{9,17},... | collective-permute-start | bytes 184328 | tf_op jit(solution)/shard_map/ppermute | solution.py:456

commit v2 on v1

v2 whole, which is shorter than its diff:
```python
import jax
import jax.numpy as jnp
from jax import lax
from jax.experimental import pallas as pl
from jax.experimental.pallas import tpu as pltpu
from jax.sharding import PartitionSpec as P

F32 = jnp.float32
W = 2.0 / 3.0
X_AXES = ("sx", "cg")
SWEEPS = 3

NXL, NYL, NZ = 8, 128, 128
HX = 3
PLANES = NXL + 2 * HX
ROWS = 160
OWN = 16
CHUNKS = ((8, 8, -1), (16, 32, 0), (48, 32, 1), (80, 32, 2), (112, 32, 3), (144, 8, 4))
OWN_CHUNKS = CHUNKS[1:5]
X_LOW, X_HIGH, Y_LOW, Y_HIGH, Z_UP, SOURCE = range(6)


OUTSIDE = 1e-30


def harmonic(a, b):
    return pl.reciprocal(a + b)


def up(v):
    return pltpu.roll(v, NZ - 1, 1)


def down(v):
    return pltpu.roll(v, 1, 1)


def look_up(row, index):
    table = jnp.broadcast_to(row, index.shape)
    return jnp.take_along_axis(table, index, axis=1, mode="promise_in_bounds")


def iota(shape, dim):
    return lax.broadcasted_iota(jnp.int32, shape, dim)


def dot(a, b):
    return jnp.dot(a, b, precision=lax.Precision.HIGHEST, preferred_element_type=F32)


def sum_matrix():
    return jnp.where(iota((NZ, NZ), 0) // 32 == iota((NZ, NZ), 1) % 4, 1.0, 0.0).astype(F32)


def top_matrix():
    lane, col = iota((NZ, NZ), 0), iota((NZ, NZ), 1) % 4
    return jnp.where((lane == 32 * col + 31) & (col < 3), 1.0, 0.0).astype(F32)


def row_group(values):
    return (values[0:8] + values[8:16]) + (values[16:24] + values[24:32])


def gather_tile(pieces):
    group = iota((8, NZ), 1) // 4
    sublane = iota((8, NZ), 0)
    tile = jnp.zeros((8, NZ), F32)
    for a, parts in enumerate(pieces):
        acc = jnp.zeros((8, NZ), F32)
        for field, j, part in parts:
            acc = jnp.where(group == 4 * field + j, part, acc)
        tile = jnp.where(sublane == a, jnp.sum(acc, axis=0, keepdims=True), tile)
    return tile


def own_kernel(table, cls, rhs, kh, kv, fz, tiles):
    khrow, kvrow = 0.5 / table[0:1, :], 0.5 / table[1:2, :]

    def plane(x, _):
        i = x + HX
        for at, size, _j in OWN_CHUNKS:
            rows = pl.ds(at, size)
            index = cls[x, pl.ds(at - OWN, size), :]
            kh[i, rows, :] = look_up(khrow, index)
            k = look_up(kvrow, index)
            kv[i, rows, :] = k
            z = harmonic(k, up(k))
            fz[i, rows, :] = jnp.where(iota((size, NZ), 1) < NZ - 1, z, 0.0)
        return 0

    lax.fori_loop(0, NXL, plane, 0)
    first = iota((8, NZ), 0) == 0
    for f in range(1, 4):
        for j in range(4):
            rows = pl.ds(OWN + 32 * j, 32)
            face = harmonic(kh[2 * f + 2, rows, :], kh[2 * f + 3, rows, :])
            tiles[pl.ds(8 * (4 * (f - 1) + j), 8), :] = row_group(face)
    for a in range(4):
        low, high = 2 * a + HX, 2 * a + HX + 1
        for j in range(1, 4):
            here, under = pl.ds(OWN + 32 * j, 8), pl.ds(OWN + 32 * j - 1, 8)
            total = harmonic(kh[low, under, :], kh[low, here, :])
            total = total + harmonic(kh[high, under, :], kh[high, here, :])
            tiles[pl.ds(8 * (11 + 3 * a + j), 8), :] = jnp.where(first, total, 0.0)
        for j in range(4):
            rows = pl.ds(32 * j, 32)
            source = rhs[2 * a, rows, :] + rhs[2 * a + 1, rows, :]
            tiles[pl.ds(8 * (24 + 4 * a + j), 8), :] = row_group(source)
            rows = pl.ds(OWN + 32 * j, 32)
            upper = fz[low, rows, :] + fz[high, rows, :]
            tiles[pl.ds(8 * (40 + 4 * a + j), 8), :] = row_group(upper)
    tiles[0:320, :] = dot(tiles[0:320, :], sum_matrix())
    tiles[320:448, :] = dot(tiles[320:448, :], top_matrix())


def coarse_kernel(inside, table, xlo, xhi, ylo, yhi, kh, tiles, out, rims):
    khrow = 0.5 / table[0:1, :]

    def rim(classes, side):
        values = look_up(khrow, classes.astype(jnp.int32))
        return jnp.where(inside[side] > 0.5, values, OUTSIDE)

    first = iota((8, NZ), 0) == 0
    for j in range(4):
        rows, own = pl.ds(32 * j, 32), pl.ds(OWN + 32 * j, 32)
        face = harmonic(rim(xlo[2, rows, :], 0), kh[HX, own, :])
        rims[pl.ds(8 * j, 8), :] = row_group(face)
        face = harmonic(kh[HX + NXL - 1, own, :], rim(xhi[0, rows, :], 1))
        rims[pl.ds(8 * (4 + j), 8), :] = row_group(face)
    for a in range(4):
        low = high = jnp.zeros((8, NZ), F32)
        for x in (2 * a, 2 * a + 1):
            i = x + HX
            under = pltpu.roll(rim(ylo[x], 2), 1, 0)
            low = low + harmonic(under, kh[i, OWN : OWN + 8, :])
            high = high + harmonic(kh[i, 143:151, :], rim(yhi[x], 3))
        rims[pl.ds(8 * (8 + a), 8), :] = jnp.where(first, low, 0.0)
        rims[pl.ds(8 * (12 + a), 8), :] = jnp.where(first, high, 0.0)
    rims[...] = dot(rims[...], sum_matrix())

    def inner(t):
        return tiles[pl.ds(8 * t, 8), :]

    def outer(t):
        return rims[pl.ds(8 * t, 8), :]

    def x_face(f, j):
        return outer(f + j) if f in (0, 4) else inner(4 * (f - 1) + j)

    def y_face(a, j):
        return outer(8 + a + j) if j in (0, 4) else inner(11 + 3 * a + j)

    pieces = []
    for a in range(4):
        parts = []
        for j in range(4):
            parts += [
                (X_LOW, j, x_face(a, j)),
                (X_HIGH, j, x_face(a + 1, j)),
                (Y_LOW, j, y_face(a, j)),
                (Y_HIGH, j, y_face(a, j + 1)),
                (Z_UP, j, inner(40 + 4 * a + j)),
                (SOURCE, j, inner(24 + 4 * a + j)),
            ]
        pieces.append(parts)
    out[...] = gather_tile(pieces)


def stack_tiles(buf, left, own, right):
    buf[0:4, :] = left[0:4, :]
    buf[4:8, :] = own[0:4, :]
    buf[8:12, :] = right[0:4, :]
    buf[12:16, :] = jnp.zeros((4, NZ), F32)
    return buf[...]


def widen(field, below, own, above):
    lane = iota((16, NZ), 1)

    def placed(v, at):
        shift = (at - 16 * field) % NZ
        return pltpu.roll(v, shift, 1) if shift else v

    wide = jnp.where(lane < 16, placed(below, 0), placed(own, 16))
    wide = jnp.where(lane < 32, wide, placed(above, 32))
    return jnp.where(lane < 48, wide, 0.0)


def coarse_sweeps(coefs, source):
    x_low, x_high, y_low, y_high, z_up, scale = coefs
    start = scale * source
    c = start
    for _ in range(SWEEPS):
        beside = x_low * pltpu.roll(c, 1, 0) + x_high * pltpu.roll(c, 15, 0)
        beside = beside + y_low * pltpu.roll(c, 4, 1) + y_high * pltpu.roll(c, NZ - 4, 1)
        beside = beside + z_up * up(c) + down(z_up * c)
        c = (1.0 - W) * c + (start + scale * beside)
    return c


def spread_coarse(c, spread):
    for k in range(6):
        lane = iota((NZ, NZ), 1)
        pick = jnp.where(iota((NZ, NZ), 0) == 4 * (k + 3) + lane // 32, 1.0, 0.0)
        spread[k] = dot(c, pick.astype(F32))


def neighbours(v, fx, fy, fz, i, at, size):
    here = v[i, pl.ds(at, size), :]
    total = fx[i, pl.ds(at, size), :] * v[i - 1, pl.ds(at, size), :]
    total = total + fx[i + 1, pl.ds(at, size), :] * v[i + 1, pl.ds(at, size), :]
    total = total + fy[i, pl.ds(at, size), :] * v[i, pl.ds(at - 1, size), :]
    total = total + fy[i, pl.ds(at + 1, size), :] * v[i, pl.ds(at + 1, size), :]
    z = fz[i, pl.ds(at, size), :]
    return here, total + z * up(here) + down(z * here)


def smooth_chunk(s1, d, fx, fy, fz, scale, spread, i, at, size, j):
    here, total = neighbours(s1, fx, fy, fz, i, at, size)
    value = (2.0 - W) * here + scale[i, pl.ds(at, size), :] * total
    if spread is not None:
        value = value + spread[j + 1, pl.ds((i + 5) // 2, 1), :]
    d[i, pl.ds(at, size), :] = value


def zero_pads(v):
    def plane(i, _):
        v[i, 0:8, :] = jnp.zeros((8, NZ), F32)
        v[i, ROWS - 8 : ROWS, :] = jnp.zeros((8, NZ), F32)
        return 0

    lax.fori_loop(0, PLANES, plane, 0)


def looked_up(inside, table, kh, kv, i, at, size, classes, *sides):
    index = classes.astype(jnp.int32)
    values = look_up(0.5 / table[0:1, :], index)
    for side in sides:
        values = jnp.where(inside[side] > 0.5, values, OUTSIDE)
    kh[i, pl.ds(at, size), :] = values
    if 0 < i < PLANES - 1 if isinstance(i, int) else True:
        kv[i, pl.ds(at, size), :] = look_up(0.5 / table[1:2, :], index)


def set_scale(i, at, size, mask, source, fx, fy, fz, scale, centre, s1):
    rows = pl.ds(at, size)
    z = fz[i, rows, :]
    total = fx[i, rows, :] + fx[i + 1, rows, :]
    total = total + fy[i, rows, :] + fy[i, pl.ds(at + 1, size), :] + (z + down(z))
    inverse = (W * mask) * pl.reciprocal(total)
    scale[i, rows, :] = inverse
    s1[i, rows, :] = inverse * source
    if centre is not None:
        centre[i, rows, :] = total


def cells_kernel(
    inside, table, rhs, xlo, xhi, ylo, yhi, _kh, _kv, fz,
    kh, kv, fx, fy, scale, centre, s1,
):
    def rims(x, _):
        looked_up(inside, table, kh, kv, x + HX, 8, 8, ylo[x], 2)
        looked_up(inside, table, kh, kv, x + HX, 144, 8, yhi[x], 3)
        return 0

    lax.fori_loop(0, NXL, rims, 0)
    for n in range(3):
        for side, base, msg in ((0, 0, xlo), (1, HX + NXL, xhi)):
            looked_up(inside, table, kh, kv, base + n, OWN, NYL, msg[n], side)

    def faces(i, _):
        for at, size, j in OWN_CHUNKS:
            rows = pl.ds(at, size)
            here = kh[i, rows, :]
            fx[i, rows, :] = harmonic(kh[i - 1, rows, :], here)
            fy[i, rows, :] = harmonic(kh[i, pl.ds(at - 1, size), :], here)
        fy[i, 144:152, :] = harmonic(kh[i, 143:151, :], kh[i, 144:152, :])
        return 0

    lax.fori_loop(HX, HX + NXL, faces, 0)
    end = HX + NXL
    fx[end, 16:144, :] = harmonic(kh[end - 1, 16:144, :], kh[end, 16:144, :])

    def scales(x, _):
        for at, size, j in OWN_CHUNKS:
            source = rhs[x, pl.ds(at - OWN, size), :]
            set_scale(x + HX, at, size, 1.0, source, fx, fy, fz, scale, centre, s1)
        return 0

    lax.fori_loop(0, NXL, scales, 0)


RIM_PLANES = (1, 2, HX + NXL, HX + NXL + 1)
RIM_CHUNKS = (CHUNKS[0], CHUNKS[5])


def first_kernel(
    inside, table, xlo, xhi, ylo, yhi, left, own, right, below, above, centre,
    _kh, _kv, _fx, _fy, _fz, _scale, _s1,
    d_out, q_out, xm_lo, xm_hi, tile_out, coefs_out, kh, kv, fx, fy, fz, scale, s1,
    d, stack, spread, tiles,
):
    for n in range(3):
        for side, i in ((0, n), (1, HX + NXL + n)):
            corner = 3 * side + n
            looked_up(inside, table, kh, kv, i, 8, 8, below[corner], side, 2)
            looked_up(inside, table, kh, kv, i, 144, 8, above[corner], side, 3)

    def pads(i, _):
        ones = jnp.ones((8, NZ), F32)
        kh[i, 0:8, :] = ones
        kh[i, ROWS - 8 : ROWS, :] = ones
        fy[i, ROWS - 8 : ROWS, :] = ones
        return 0

    lax.fori_loop(0, PLANES, pads, 0)
    zero_pads(s1)
    zero_pads(d)

    mid = stack_tiles(stack, left, own, right)
    low = stack_tiles(stack, below[10], below[11], below[12])
    high = stack_tiles(stack, above[10], above[11], above[12])
    wide = [widen(k, low, mid, high) for k in range(6)]
    total = wide[0] + wide[1] + wide[2] + wide[3] + wide[4] + down(wide[4])
    valid = total > 0.0
    wide_scale = jnp.where(valid, W / jnp.where(valid, total, 1.0), 0.0)
    coefs = wide[:5] + [wide_scale]
    for k in range(6):
        coefs_out[k] = coefs[k]
    spread_coarse(coarse_sweeps(coefs, wide[SOURCE]), spread)

    def set_faces(i, at, size):
        rows = pl.ds(at, size)
        here = kh[i, rows, :]
        fx[i, rows, :] = harmonic(kh[i - 1, rows, :], here)
        fy[i, rows, :] = harmonic(kh[i, pl.ds(at - 1, size), :], here)
        k = kv[i, rows, :]
        z = harmonic(k, up(k))
        fz[i, rows, :] = jnp.where(iota((size, NZ), 1) < NZ - 1, z, 0.0)

    def rim_faces(i, _):
        for at, size, _j in RIM_CHUNKS:
            set_faces(i, at, size)
        return 0

    lax.fori_loop(1, PLANES - 1, rim_faces, 0)
    for i in RIM_PLANES:
        for at, size, _j in OWN_CHUNKS:
            set_faces(i, at, size)
    last = PLANES - 1
    for at, size, _j in CHUNKS:
        rows = pl.ds(at, size)
        fx[last, rows, :] = harmonic(kh[last - 1, rows, :], kh[last, rows, :])

    def rim_scales(i, mask, source_low, source_high):
        set_scale(i, 8, 8, mask * inside[2], source_low, fx, fy, fz, scale, None, s1)
        set_scale(i, 144, 8, mask * inside[3], source_high, fx, fy, fz, scale, None, s1)

    def own_rims(x, _):
        rim_scales(x + HX, 1.0, ylo[NXL + x], yhi[NXL + x])
        return 0

    lax.fori_loop(0, NXL, own_rims, 0)
    for n in range(2):
        for side, i, msg in ((0, 1 + n, xlo), (1, HX + NXL + n, xhi)):
            corner = 6 + 2 * side + n
            rim_scales(i, inside[side], below[corner], above[corner])
            for at, size, _j in OWN_CHUNKS:
                source = msg[3 + n, pl.ds(at - OWN, size), :]
                set_scale(i, at, size, inside[side], source, fx, fy, fz, scale, None, s1)

    def smooth(i, _):
        for at, size, j in CHUNKS:
            smooth_chunk(s1, d, fx, fy, fz, scale, spread, i, at, size, j)
        return 0

    lax.fori_loop(HX - 1, HX + NXL + 1, smooth, 0)

    def image(x, _):
        i = x + HX
        for at, size, j in OWN_CHUNKS:
            here, total = neighbours(d, fx, fy, fz, i, at, size)
            q = centre[i, pl.ds(at, size), :] * here - total
            q_out[x, pl.ds(at - OWN, size), :] = q
            d_out[x, pl.ds(at - OWN, size), :] = here
        return 0

    lax.fori_loop(0, NXL, image, 0)
    for a in range(4):
        for j in range(4):
            rows = pl.ds(32 * j, 32)
            source = q_out[2 * a, rows, :] + q_out[2 * a + 1, rows, :]
            tiles[pl.ds(8 * (4 * a + j), 8), :] = row_group(source)
    tiles[...] = dot(tiles[...], sum_matrix())
    tile = gather_tile(
        [
            [(SOURCE, j, tiles[pl.ds(8 * (4 * a + j), 8), :]) for j in range(4)]
            for a in range(4)
        ]
    )
    tile_out[...] = tile
    for n in range(2):
        xm_lo[pl.ds(128 * n, 128), :] = q_out[n]
        xm_hi[pl.ds(128 * n, 128), :] = q_out[NXL - 2 + n]
    xm_lo[256:264, :] = tile
    xm_hi[256:264, :] = tile


INNER_CHUNKS = ((24, 24, 0), (48, 32, 1), (80, 32, 2), (112, 24, 3))
OUTER_CHUNKS = ((8, 8, -1), (16, 8, 0), (136, 8, 3), (144, 8, 4))


def inner_kernel(rhs, d0, q0, fx, fy, fz, scale, s1, d, known):
    zero_pads(s1)
    zero_pads(d)

    def plane(x, sums):
        i = x + HX
        for at, size, j in OWN_CHUNKS:
            rows = pl.ds(at - OWN, size)
            q = q0[x, rows, :]
            s1[i, pl.ds(at, size), :] = scale[i, pl.ds(at, size), :] * q
            dd = d0[x, rows, :]
            rd, dq = sums
            sums = (rd + row_group(rhs[x, rows, :] * dd), dq + row_group(dd * q))
        return sums

    zero = jnp.zeros((8, NZ), F32)
    rd, dq = lax.fori_loop(0, NXL, plane, (zero, zero))
    known[0:8, :] = rd
    known[8:16, :] = dq

    def smooth(i, _):
        for at, size, j in INNER_CHUNKS:
            smooth_chunk(s1, d, fx, fy, fz, scale, None, i, at, size, j)
        return 0

    lax.fori_loop(HX + 1, HX + NXL - 1, smooth, 0)


def second_kernel(
    rhs, d0, q0, xlo, xhi, own, below, above, coefs, fx, fy, fz, scale, centre, known,
    _s1, _d, p_out, s_out, dots, s1, d, stack, spread,
):
    mid = stack_tiles(stack, xlo[256:264, :], own[...], xhi[256:264, :])
    low = stack_tiles(stack, below[12], below[13], below[14])
    high = stack_tiles(stack, above[12], above[13], above[14])
    wide = widen(SOURCE, low, mid, high)
    spread_coarse(coarse_sweeps([coefs[k] for k in range(6)], wide), spread)

    def rims(i, _):
        s1[i, 8:16, :] = scale[i, 8:16, :] * below[i - 1]
        s1[i, 144:152, :] = scale[i, 144:152, :] * above[i - 1]
        return 0

    lax.fori_loop(1, PLANES - 1, rims, 0)
    for n in range(2):
        for i, msg in ((1 + n, xlo), (HX + NXL + n, xhi)):
            s1[i, 16:144, :] = scale[i, 16:144, :] * msg[pl.ds(128 * n, 128), :]

    for i in (HX - 1, HX, HX + NXL - 1, HX + NXL):
        for at, size, j in CHUNKS:
            smooth_chunk(s1, d, fx, fy, fz, scale, spread, i, at, size, j)

    def smooth(i, _):
        for at, size, j in OUTER_CHUNKS:
            smooth_chunk(s1, d, fx, fy, fz, scale, spread, i, at, size, j)
        for at, size, j in INNER_CHUNKS:
            rows = pl.ds(at, size)
            d[i, rows, :] = d[i, rows, :] + spread[j + 1, pl.ds((i + 5) // 2, 1), :]
        return 0

    lax.fori_loop(HX + 1, HX + NXL - 1, smooth, 0)

    def image(x, sums):
        i = x + HX
        for at, size, j in OWN_CHUNKS:
            rows = pl.ds(at - OWN, size)
            p, total = neighbours(d, fx, fy, fz, i, at, size)
            s = centre[i, pl.ds(at, size), :] * p - total
            p_out[x, rows, :] = p
            s_out[x, rows, :] = s
            r, dd, q = rhs[x, rows, :], d0[x, rows, :], q0[x, rows, :]
            pairs = ((r, p), (q, p), (dd, s), (p, s))
            sums = tuple(
                acc + row_group(u * v) for acc, (u, v) in zip(sums, pairs)
            )
        return sums

    zero = jnp.zeros((8, NZ), F32)
    sums = lax.fori_loop(0, NXL, image, (zero,) * 4)
    sums = (known[0:8, :], known[8:16, :]) + sums
    sublane, lane = iota((8, NZ), 0), iota((8, NZ), 1)
    tile = zero
    for n, acc in enumerate(sums):
        tile = jnp.where(sublane == n, jnp.sum(acc, axis=0, keepdims=True), tile)
    tile = jnp.where(sublane == lane, jnp.sum(tile, axis=1, keepdims=True), 0.0)
    dots[...] = jnp.sum(tile, axis=0, keepdims=True)


def last_kernel(parts, rhs, d0, q0, p, s, x_out, r_out):
    total = parts[0:8, :]
    for n in range(8, parts.shape[0], 8):
        total = total + parts[n : n + 8, :]
    sums = jnp.sum(total, axis=0, keepdims=True)
    rd, dq, rp, qp, ds, ps = [sums[:, n : n + 1] for n in range(6)]
    a0 = rd / dq
    rz = rd - a0 * rp - a0 * dq + a0 * a0 * qp
    ratio = rz / rd
    grow = 1.0 + ratio
    curve = grow * grow * dq - grow * a0 * (ds + qp) + a0 * a0 * ps
    a1 = rz / curve
    u = jnp.broadcast_to(a0 + a1 * grow, (8, NZ))[0:1, :]
    v = jnp.broadcast_to(a1 * a0, (8, NZ))[0:1, :]

    def plane(x, _):
        for at in range(0, NYL, 32):
            rows = pl.ds(at, 32)
            x_out[x, rows, :] = u * d0[x, rows, :] - v * p[x, rows, :]
            r_out[x, rows, :] = rhs[x, rows, :] - u * q0[x, rows, :] + v * s[x, rows, :]
        return 0

    lax.fori_loop(0, NXL, plane, 0)


VMEM = pl.BlockSpec(memory_space=pltpu.VMEM)
SMEM = pl.BlockSpec(memory_space=pltpu.SMEM)


def call(kernel, name, operands, outs, scratch, scalars=0, aliases=None):
    return pl.pallas_call(
        kernel,
        name=name,
        out_shape=[jax.ShapeDtypeStruct(s, F32) for s in outs],
        in_specs=[SMEM] * scalars + [VMEM] * (len(operands) - scalars),
        out_specs=[VMEM] * len(outs),
        scratch_shapes=[pltpu.VMEM(s, F32) for s in scratch],
        input_output_aliases=aliases or {},
        compiler_params=pltpu.CompilerParams(vmem_limit_bytes=24 * 1024 * 1024),
    )(*operands)


def upward(values, axis):
    count = lax.axis_size(axis)
    return lax.ppermute(values, axis, [(i, i + 1) for i in range(count - 1)])


def downward(values, axis):
    count = lax.axis_size(axis)
    return lax.ppermute(values, axis, [(i + 1, i) for i in range(count - 1)])


def exchange(row, axes):
    count = lax.axis_size(axes)
    rows = jnp.broadcast_to(row[None], (count, 1, NZ))
    return lax.all_to_all(rows, axes, 0, 0).reshape(count, NZ)


STAGES = (("sy", "cg"), "sx")


def body(right_side, perm_class, perm_table):
    x_at, y_at = lax.axis_index(X_AXES), lax.axis_index("sy")
    x_end, y_end = lax.axis_size(X_AXES) - 1, lax.axis_size("sy") - 1
    inside = jnp.stack([x_at > 0, x_at < x_end, y_at > 0, y_at < y_end]).astype(F32)
    pad = ((0, 6), (0, NZ - perm_table.shape[1]))
    table = jnp.pad(perm_table, pad, constant_values=1.0)

    def packed(classes, values):
        return jnp.concatenate([classes.astype(F32), values])

    xlo = upward(packed(perm_class[-3:], right_side[-2:]), X_AXES)
    xhi = downward(packed(perm_class[:3], right_side[:2]), X_AXES)
    ylo = upward(packed(perm_class[:, -8:], right_side[:, -8:]), "sy")
    yhi = downward(packed(perm_class[:, :8], right_side[:, :8]), "sy")

    block, big = (NXL, NYL, NZ), (PLANES, ROWS, NZ)
    kh, kv, fz, tiles = call(
        own_kernel, "own", (table, perm_class, right_side), [big] * 3 + [(448, NZ)], []
    )
    halos = (xlo, xhi, ylo, yhi)
    (own,) = call(
        coarse_kernel, "coarse", (inside, table) + halos + (kh, tiles), [(8, NZ)],
        [(128, NZ)], 1,
    )
    kh, kv, fx, fy, scale, centre, s1 = call(
        cells_kernel, "cells", (inside, table, right_side) + halos + (kh, kv, fz),
        [big] * 7, [], 1, {7: 0, 8: 1},
    )
    left, right = upward(own, X_AXES), downward(own, X_AXES)

    def rim(rows):
        parts = [xlo[:3, rows], xhi[:3, rows], xlo[3:, rows], xhi[3:, rows]]
        return jnp.concatenate(parts + [left[None], own[None], right[None]])

    below = upward(rim(slice(NYL - 8, NYL)), "sy")
    above = downward(rim(slice(0, 8)), "sy")

    d0, q0, xm_lo, xm_hi, tile, coefs, _, _, fx, fy, fz, scale, _ = call(
        first_kernel, "first",
        (inside, table) + halos + (left, own, right, below, above, centre)
        + (kh, kv, fx, fy, fz, scale, s1),
        [block, block, (264, NZ), (264, NZ), (8, NZ), (6, 16, NZ)] + [big] * 7,
        [big, (16, NZ), (6, 16, NZ), (16 * 8, NZ)], 1,
        {12 + n: 6 + n for n in range(7)},
    )
    qlo, qhi = upward(xm_hi, X_AXES), downward(xm_lo, X_AXES)
    s1, d, known = call(
        inner_kernel, "inner", (right_side, d0, q0, fx, fy, fz, scale),
        [big, big, (16, NZ)], [],
    )

    def rim_q(at):
        parts = [qlo[at : at + 8][None], qlo[128 + at : 136 + at][None], q0[:, at : at + 8]]
        parts += [qhi[at : at + 8][None], qhi[128 + at : 136 + at][None]]
        return jnp.concatenate(parts + [qlo[256:][None], tile[None], qhi[256:][None]])

    below = upward(rim_q(NYL - 8), "sy")
    above = downward(rim_q(0), "sy")
    p, s, dots, _, _ = call(
        second_kernel, "second",
        (right_side, d0, q0, qlo, qhi, tile, below, above, coefs, fx, fy, fz, scale, centre)
        + (known, s1, d),
        [block, block, (1, NZ), big, big], [(16, NZ), (6, 16, NZ)], 0, {15: 3, 16: 4},
    )
    for axes in STAGES[:-1]:
        dots = exchange(dots, axes).sum(0, keepdims=True)
    dots = exchange(dots, STAGES[-1])
    return tuple(
        call(last_kernel, "last", (dots, right_side, d0, q0, p, s), [block, block], [])
    )


def solution(mesh):
    cells = P(X_AXES, "sy", None)
    return jax.shard_map(
        body,
        mesh=mesh,
        in_specs=(cells, cells, P()),
        out_specs=(cells, cells),
        check_vma=False,
    )
```

time: 121 us -> 113 us (0.934)
  waiting for transfers between devices: 12.2 us -> 7.6 us
  blocking collectives: 52.1 us -> 48.8 us
  Pallas kernels: 15.4 us -> 16.8 us
    all_to_all x3 -> x2, blocking collectives: 52.1 us -> 48.8 us  [exchange(): return lax.all_to_all(rows, axes, 0, 0).reshape(count, NZ)]
    ppermute x6, waiting for transfers between devices: 3.62 us -> 1 us  [upward(): return lax.ppermute(values, axis, [(i, i + 1) for i in range(count - 1)])]
    ppermute x6, waiting for transfers between devices: 8.61 us -> 6.6 us  [downward(): return lax.ppermute(values, axis, [(i + 1, i) for i in range(count - 1)])]
    pallas_call x4 -> x7, Pallas kernels: 15.4 us -> 16.8 us  [call(): pl.pallas_call(kernel, name=name, out_shape=[jax.ShapeDtypeStruct(s, F32)...]
  transfers between devices with their start and end apart: 12 -> 12, of which waited for: 5 -> 4; matrix products, arithmetic and copies ran while one was open for 0% -> 0% of each run, Pallas kernels for 0% -> 5%
where the time goes in v2:
time: 113 us; the launch traced here: 112 us
  blocking collectives  48.8 us (43%)
  starting transfers between devices  35.4 us (31%)
  Pallas kernels  16.8 us (15%)
  waiting for transfers between devices  7.6 us (7%)
  other arithmetic  1.31 us (1%)
    all_to_all x2, blocking collectives, exchange(): return lax.all_to_all(rows, axes, 0, 0).reshape(count, NZ)  48.8 us
    ppermute x6, starting transfers between devices, upward(): return lax.ppermute(values, axis, [(i, i + 1) for i in range(count - 1)])  21.8 us
    pallas_call x7, Pallas kernels, call(): pl.pallas_call(kernel, name=name, out_shape=[jax.ShapeDtypeStruct(s, F32)...  16.8 us
    ppermute x6, starting transfers between devices, downward(): return lax.ppermute(values, axis, [(i + 1, i) for i in range(count - 1)])  13.7 us
    ppermute x6, waiting for transfers between devices, downward(): return lax.ppermute(values, axis, [(i + 1, i) for i in range(count - 1)])  6.6 us
  transfers between devices with their start and end apart: 12, of which 4 were waited for; matrix products, arithmetic and copies ran while one was open for 0% of the time, Pallas kernels for 5%

profile of v2, /device:TPU:1, one launch (start us, length us, event | category | flops | bytes accessed | tf_op | source)
XLA Modules:
  0.0 112.1 jit_solution(15682469737242443835)
XLA Ops:
  0.6 1.0 fusion.1
  1.6 0.0 copy-start.1
  1.6 0.0 copy-start
  1.6 0.0 copy-start.2
  1.7 1.1 %slice_convert_fusion = (f32[3,128,128]{2,1,0:T(8,128)S(1)}, f32[3,128,128]{2,1,0:T(8,128)S(1)}) fusion(s32[8,128,128]{2,1,0:T(8,128)} %cls.1), kind=kLoop, calls=%fused_computation.2 | loop fusion | flops 98304 | bytes 786432 | tf_op jit(solution)/shard_map/convert_element_type | solution.py:570
  2.8 4.5 %collective-permute-start = (f32[5,128,128]{2,1,0:T(8,128)S(1)}, f32[5,128,128]{2,1,0:T(8,128)S(1)}, u32[]{:S(2)}, u32[]{:S(2)}) collective-permute-start(f32[5,128,128]{2,1,0:T(8,128)S(1)} %pad_maximum_fusion), channel_id=1, source_target_pairs={{0,1},{1,2},{2,3},{3,4},{4,5},{5,6},{6,7},{7,64},{64,65},{65,66},{... | collective-permute-start | bytes 983048 | tf_op jit(solution)/shard_map/ppermute | solution.py:545
  7.4 5.6 %collective-permute-start.1 = (f32[5,128,128]{2,1,0:T(8,128)S(1)}, f32[5,128,128]{2,1,0:T(8,128)S(1)}, u32[]{:S(2)}, u32[]{:S(2)}) collective-permute-start(f32[5,128,128]{2,1,0:T(8,128)S(1)} %pad_maximum_fusion.1), channel_id=1, source_target_pairs={{1,0},{2,1},{3,2},{4,3},{5,4},{6,5},{7,6},{64,7},{65,64},{66,65},{... | collective-permute-start | bytes 983048 | tf_op jit(solution)/shard_map/ppermute | solution.py:550
  13.0 1.3 %collective-permute-start.2 = (f32[16,8,128]{2,1,0:T(8,128)S(1)}, f32[16,8,128]{2,1,0:T(8,128)S(1)}, u32[]{:S(2)}, u32[]{:S(2)}) collective-permute-start(f32[16,8,128]{2,1,0:T(8,128)S(1)} %pad_maximum_fusion.2), channel_id=1, source_target_pairs={{0,8},{8,16},{16,24},{24,32},{32,40},{40,48},{48,56},{1,9},{9,17},... | collective-permute-start | bytes 196616 | tf_op jit(solution)/shard_map/ppermute | solution.py:545
  14.3 1.3 %collective-permute-start.3 = (f32[16,8,128]{2,1,0:T(8,128)S(1)}, f32[16,8,128]{2,1,0:T(8,128)S(1)}, u32[]{:S(2)}, u32[]{:S(2)}) collective-permute-start(f32[16,8,128]{2,1,0:T(8,128)S(1)} %pad_maximum_fusion.3), channel_id=1, source_target_pairs={{8,0},{16,8},{24,16},{32,24},{40,32},{48,40},{56,48},{9,1},{17,9},... | collective-permute-start | bytes 196616 | tf_op jit(solution)/shard_map/ppermute | solution.py:550
  15.7 2.0 %own.1 = (f32[14,160,128]{2,1,0:T(8,128)S(1)}, f32[14,160,128]{2,1,0:T(8,128)S(1)}, f32[14,160,128]{2,1,0:T(8,128)S(1)}, f32[448,128]{1,0:T(8,128)S(1)}) custom-call(f32[8,128]{1,0:T(8,128)S(1)} %pad.4.table, s32[8,128,128]{2,1,0:T(8,128)S(1)} %copy-done.1, f32[8,128,128]{2,1,0:T(8,128)S(1)} %copy-done), custom_call_target="tpu_custom_call" | custom-call | tf_op jit(solution)/shard_map/own/pallas_call | solution.py:531
  17.7 0.1 add_convert_fusion.inside
  17.8 2.2 %collective-permute-done.3.yhi = f32[16,8,128]{2,1,0:T(8,128)S(1)} collective-permute-done((f32[16,8,128]{2,1,0:T(8,128)S(1)}, f32[16,8,128]{2,1,0:T(8,128)S(1)}, u32[]{:S(2)}, u32[]{:S(2)}) %collective-permute-start.3) | collective-permute-done | bytes 65568 | tf_op jit(solution)/shard_map/ppermute | solution.py:550
  20.0 0.9 coarse.1.own
  20.9 2.3 %collective-permute-start.5 = (f32[8,128]{1,0:T(8,128)S(1)}, f32[8,128]{1,0:T(8,128)S(1)}, u32[]{:S(2)}, u32[]{:S(2)}) collective-permute-start(f32[8,128]{1,0:T(8,128)S(1)} %coarse.1.own), channel_id=1, source_target_pairs={{1,0},{2,1},{3,2},{4,3},{5,4},{6,5},{7,6},{64,7},{65,64},{66,65},{... | collective-permute-start | bytes 12296 | tf_op jit(solution)/shard_map/ppermute | solution.py:550
  23.3 3.3 %collective-permute-start.4 = (f32[8,128]{1,0:T(8,128)S(1)}, f32[8,128]{1,0:T(8,128)S(1)}, u32[]{:S(2)}, u32[]{:S(2)}) collective-permute-start(f32[8,128]{1,0:T(8,128)S(1)} %coarse.1.own), channel_id=1, source_target_pairs={{0,1},{1,2},{2,3},{3,4},{4,5},{5,6},{6,7},{7,64},{64,65},{65,66},{... | collective-permute-start | bytes 12296 | tf_op jit(solution)/shard_map/ppermute | solution.py:545
  26.6 0.7 collective-permute-done.4.left
  27.3 1.3 %collective-permute-start.7 = (f32[13,8,128]{2,1,0:T(8,128)S(1)}, f32[13,8,128]{2,1,0:T(8,128)S(1)}, u32[]{:S(2)}, u32[]{:S(2)}) collective-permute-start(f32[13,8,128]{2,1,0:T(8,128)S(1)} %get-tuple-element.88), channel_id=1, source_target_pairs={{8,0},{16,8},{24,16},{32,24},{40,32},{48,40},{56,48},{9,1},{17,9},... | collective-permute-start | bytes 159752 | tf_op jit(solution)/shard_map/ppermute | solution.py:550
  28.6 4.0 %collective-permute-start.6 = (f32[13,8,128]{2,1,0:T(8,128)S(1)}, f32[13,8,128]{2,1,0:T(8,128)S(1)}, u32[]{:S(2)}, u32[]{:S(2)}) collective-permute-start(f32[13,8,128]{2,1,0:T(8,128)S(1)} %get-tuple-element.89), channel_id=1, source_target_pairs={{0,8},{8,16},{16,24},{24,32},{32,40},{40,48},{48,56},{1,9},{9,17},... | collective-permute-start | bytes 159752 | tf_op jit(solution)/shard_map/ppermute | solution.py:545
  32.6 2.7 %cells.1 = (f32[14,160,128]{2,1,0:T(8,128)S(1)}, f32[14,160,128]{2,1,0:T(8,128)S(1)}, f32[14,160,128]{2,1,0:T(8,128)S(1)}, f32[14,160,128]{2,1,0:T(8,128)S(1)}, ...) custom-call(f32[4]{0:T(128)S(1)} %add_convert_fusion.inside, ...), custom_call_target="tpu_custom_call", output_to_operand_aliasing={{0}: (7, {}), {1}: (8, {})} | custom-call | tf_op jit(solution)/shard_map/cells/pallas_call | solution.py:531
  35.3 6.0 %first.1 = (f32[8,128,128]{2,1,0:T(8,128)S(1)}, f32[8,128,128]{2,1,0:T(8,128)S(1)}, f32[264,128]{1,0:T(8,128)S(1)}, f32[264,128]{1,0:T(8,128)S(1)}, f32[8,128]{1...) custom-call(f32[4]{0:T(128)S(1)} %add_convert_fusion.inside, ...), custom_call_target="tpu_custom_call", output_to_operand_aliasing={{6}: (12, {}), {7}: (13, {}), {8}: (14, {}), {9}: (15, {}),... | custom-call | tf_op jit(solution)/shard_map/first/pallas_call | solution.py:531
  41.3 4.7 %collective-permute-start.8 = (f32[264,128]{1,0:T(8,128)S(1)}, f32[264,128]{1,0:T(8,128)S(1)}, u32[]{:S(2)}, u32[]{:S(2)}) collective-permute-start(f32[264,128]{1,0:T(8,128)S(1)} %get-tuple-element.42), channel_id=1, source_target_pairs={{0,1},{1,2},{2,3},{3,4},{4,5},{5,6},{6,7},{7,64},{64,65},{65,66},{... | collective-permute-start | bytes 405512 | tf_op jit(solution)/shard_map/ppermute | solution.py:545
  46.0 1.9 %collective-permute-start.9 = (f32[264,128]{1,0:T(8,128)S(1)}, f32[264,128]{1,0:T(8,128)S(1)}, u32[]{:S(2)}, u32[]{:S(2)}) collective-permute-start(f32[264,128]{1,0:T(8,128)S(1)} %get-tuple-element.43), channel_id=1, source_target_pairs={{1,0},{2,1},{3,2},{4,3},{5,4},{6,5},{7,6},{64,7},{65,64},{66,65},{... | collective-permute-start | bytes 405512 | tf_op jit(solution)/shard_map/ppermute | solution.py:550
  48.0 0.0 collective-permute-done.8.xlo
  48.0 4.4 %collective-permute-done.9.xhi = f32[264,128]{1,0:T(8,128)S(1)} collective-permute-done((f32[264,128]{1,0:T(8,128)S(1)}, f32[264,128]{1,0:T(8,128)S(1)}, u32[]{:S(2)}, u32[]{:S(2)}) %collective-permute-start.9) | collective-permute-done | bytes 135200 | tf_op jit(solution)/shard_map/ppermute | solution.py:550
  52.4 1.3 %collective-permute-start.11 = (f32[15,8,128]{2,1,0:T(8,128)S(1)}, f32[15,8,128]{2,1,0:T(8,128)S(1)}, u32[]{:S(2)}, u32[]{:S(2)}) collective-permute-start(f32[15,8,128]{2,1,0:T(8,128)S(1)} %get-tuple-element.74), channel_id=1, source_target_pairs={{8,0},{16,8},{24,16},{32,24},{40,32},{48,40},{56,48},{9,1},{17,9},... | collective-permute-start | bytes 184328 | tf_op jit(solution)/shard_map/ppermute | solution.py:550
  53.7 4.0 %collective-permute-start.10 = (f32[15,8,128]{2,1,0:T(8,128)S(1)}, f32[15,8,128]{2,1,0:T(8,128)S(1)}, u32[]{:S(2)}, u32[]{:S(2)}) collective-permute-start(f32[15,8,128]{2,1,0:T(8,128)S(1)} %get-tuple-element.75), channel_id=1, source_target_pairs={{0,8},{8,16},{16,24},{24,32},{32,40},{40,48},{48,56},{1,9},{9,17},... | collective-permute-start | bytes 184328 | tf_op jit(solution)/shard_map/ppermute | solution.py:545
  57.7 1.0 inner.1
  58.7 0.3 collective-permute-done.10.below
  59.0 2.7 %second.1 = (f32[8,128,128]{2,1,0:T(8,128)S(1)}, f32[8,128,128]{2,1,0:T(8,128)S(1)}, f32[1,128]{1,0:T(1,128)S(1)}, f32[14,160,128]{2,1,0:T(8,128)S(1)}, f32[14,160,128]{2,1,0:T(8,128)S(1)}) custom-call(f32[8,128,128]{2,1,0:T(8,128)S(1)} %copy-done, f32[8,128,128]{2,1,0:T(8,128)S(1)} %get-tuple-element.40.d0, ...), custom_call_target="tpu_custom_call", output_to_operand_aliasing={{3}: (15, {}), {4}: (16, {})} | custom-call | tf_op jit(solution)/shard_map/second/pallas_call | solution.py:531
  61.6 30.6 %all_to_all.10 = f32[64,1,128]{2,1,0:T(1,128)S(1)} all-to-all(f32[64,1,128]{2,1,0:T(1,128)S(1)} %broadcast_in_dim.76), channel_id=1, replica_groups=mesh['sx'=8,'sy'=8,'cg'=8] {'sy','cg'}, dimensions={0} | all-to-all | bytes 65536 | tf_op jit(solution)/shard_map/all_to_all | solution.py:556
  92.3 18.2 %all_to_all.11 = f32[8,1,128]{2,1,0:T(1,128)S(1)} all-to-all(f32[8,1,128]{2,1,0:T(1,128)S(1)} %broadcast_in_dim.77), channel_id=1, replica_groups=mesh['sx'=8,'sy'=8,'cg'=8] {'sx'}, dimensions={0} | all-to-all | bytes 8192 | tf_op jit(solution)/shard_map/all_to_all | solution.py:556
  110.5 1.6 %last.1 = (f32[8,128,128]{2,1,0:T(8,128)}, f32[8,128,128]{2,1,0:T(8,128)}) custom-call(f32[8,128]{1,0:T(8,128)S(1)} %bitcast.63, f32[8,128,128]{2,1,0:T(8,128)S(1)} %copy-done, f32[8,128,128]{2,1,0:T(8,128)S(1)} %get-tuple-element.40.d0, f32[8,128,128]{2,1,0:T(8,128)S(1)} %get-tuple-element.41.q0, f32[8,128,128]{2,1,0:T(8,128)S(1)} %get-tuple-element.54.p, ...), custom_call_target="tpu_custom_call" | custom-call | tf_op jit(solution)/shard_map/last/pallas_call | solution.py:531
  (35 shorter events, 0.2 us)
Async XLA Ops:
  1.6 11.3 %copy-start.1 = (s32[8,128,128]{2,1,0:T(8,128)S(1)}, s32[8,128,128]{2,1,0:T(8,128)}, u32[]{:S(2)}) copy-start(s32[8,128,128]{2,1,0:T(8,128)} %cls.1) | copy-start | bytes 1572868
  1.6 11.3 %copy-start = (f32[8,128,128]{2,1,0:T(8,128)S(1)}, f32[8,128,128]{2,1,0:T(8,128)}, u32[]{:S(2)}) copy-start(f32[8,128,128]{2,1,0:T(8,128)} %rhs.9) | copy-start | bytes 1572868
  1.6 14.0 %copy-start.2 = (f32[2,16]{1,0:T(2,128)S(1)}, f32[2,16]{1,0:T(2,128)}, u32[]{:S(2)}) copy-start(f32[2,16]{1,0:T(2,128)} %param.5) | copy-start | bytes 388
  2.8 17.2 %collective-permute-start = (f32[5,128,128]{2,1,0:T(8,128)S(1)}, f32[5,128,128]{2,1,0:T(8,128)S(1)}, u32[]{:S(2)}, u32[]{:S(2)}) collective-permute-start(f32[5,128,128]{2,1,0:T(8,128)S(1)} %pad_maximum_fusion), channel_id=1, source_target_pairs={{0,1},{1,2},{2,3},{3,4},{4,5},{5,6},{6,7},{7,64},{64,65},{65,66},{... | collective-permute-start | bytes 983048 | tf_op jit(solution)/shard_map/ppermute | solution.py:545
  7.4 12.6 %collective-permute-start.1 = (f32[5,128,128]{2,1,0:T(8,128)S(1)}, f32[5,128,128]{2,1,0:T(8,128)S(1)}, u32[]{:S(2)}, u32[]{:S(2)}) collective-permute-start(f32[5,128,128]{2,1,0:T(8,128)S(1)} %pad_maximum_fusion.1), channel_id=1, source_target_pairs={{1,0},{2,1},{3,2},{4,3},{5,4},{6,5},{7,6},{64,7},{65,64},{66,65},{... | collective-permute-start | bytes 983048 | tf_op jit(solution)/shard_map/ppermute | solution.py:550
  13.0 4.8 %collective-permute-start.2 = (f32[16,8,128]{2,1,0:T(8,128)S(1)}, f32[16,8,128]{2,1,0:T(8,128)S(1)}, u32[]{:S(2)}, u32[]{:S(2)}) collective-permute-start(f32[16,8,128]{2,1,0:T(8,128)S(1)} %pad_maximum_fusion.2), channel_id=1, source_target_pairs={{0,8},{8,16},{16,24},{24,32},{32,40},{40,48},{48,56},{1,9},{9,17},... | collective-permute-start | bytes 196616 | tf_op jit(solution)/shard_map/ppermute | solution.py:545
  14.3 5.7 %collective-permute-start.3 = (f32[16,8,128]{2,1,0:T(8,128)S(1)}, f32[16,8,128]{2,1,0:T(8,128)S(1)}, u32[]{:S(2)}, u32[]{:S(2)}) collective-permute-start(f32[16,8,128]{2,1,0:T(8,128)S(1)} %pad_maximum_fusion.3), channel_id=1, source_target_pairs={{8,0},{16,8},{24,16},{32,24},{40,32},{48,40},{56,48},{9,1},{17,9},... | collective-permute-start | bytes 196616 | tf_op jit(solution)/shard_map/ppermute | solution.py:550
  20.9 6.3 %collective-permute-start.5 = (f32[8,128]{1,0:T(8,128)S(1)}, f32[8,128]{1,0:T(8,128)S(1)}, u32[]{:S(2)}, u32[]{:S(2)}) collective-permute-start(f32[8,128]{1,0:T(8,128)S(1)} %coarse.1.own), channel_id=1, source_target_pairs={{1,0},{2,1},{3,2},{4,3},{5,4},{6,5},{7,6},{64,7},{65,64},{66,65},{... | collective-permute-start | bytes 12296 | tf_op jit(solution)/shard_map/ppermute | solution.py:550
  23.3 4.0 %collective-permute-start.4 = (f32[8,128]{1,0:T(8,128)S(1)}, f32[8,128]{1,0:T(8,128)S(1)}, u32[]{:S(2)}, u32[]{:S(2)}) collective-permute-start(f32[8,128]{1,0:T(8,128)S(1)} %coarse.1.own), channel_id=1, source_target_pairs={{0,1},{1,2},{2,3},{3,4},{4,5},{5,6},{6,7},{7,64},{64,65},{65,66},{... | collective-permute-start | bytes 12296 | tf_op jit(solution)/shard_map/ppermute | solution.py:545
  27.3 8.0 %collective-permute-start.7 = (f32[13,8,128]{2,1,0:T(8,128)S(1)}, f32[13,8,128]{2,1,0:T(8,128)S(1)}, u32[]{:S(2)}, u32[]{:S(2)}) collective-permute-start(f32[13,8,128]{2,1,0:T(8,128)S(1)} %get-tuple-element.88), channel_id=1, source_target_pairs={{8,0},{16,8},{24,16},{32,24},{40,32},{48,40},{56,48},{9,1},{17,9},... | collective-permute-start | bytes 159752 | tf_op jit(solution)/shard_map/ppermute | solution.py:550
  28.6 6.7 %collective-permute-start.6 = (f32[13,8,128]{2,1,0:T(8,128)S(1)}, f32[13,8,128]{2,1,0:T(8,128)S(1)}, u32[]{:S(2)}, u32[]{:S(2)}) collective-permute-start(f32[13,8,128]{2,1,0:T(8,128)S(1)} %get-tuple-element.89), channel_id=1, source_target_pairs={{0,8},{8,16},{16,24},{24,32},{32,40},{40,48},{48,56},{1,9},{9,17},... | collective-permute-start | bytes 159752 | tf_op jit(solution)/shard_map/ppermute | solution.py:545
  41.3 6.7 %collective-permute-start.8 = (f32[264,128]{1,0:T(8,128)S(1)}, f32[264,128]{1,0:T(8,128)S(1)}, u32[]{:S(2)}, u32[]{:S(2)}) collective-permute-start(f32[264,128]{1,0:T(8,128)S(1)} %get-tuple-element.42), channel_id=1, source_target_pairs={{0,1},{1,2},{2,3},{3,4},{4,5},{5,6},{6,7},{7,64},{64,65},{65,66},{... | collective-permute-start | bytes 405512 | tf_op jit(solution)/shard_map/ppermute | solution.py:545
  46.0 6.3 %collective-permute-start.9 = (f32[264,128]{1,0:T(8,128)S(1)}, f32[264,128]{1,0:T(8,128)S(1)}, u32[]{:S(2)}, u32[]{:S(2)}) collective-permute-start(f32[264,128]{1,0:T(8,128)S(1)} %get-tuple-element.43), channel_id=1, source_target_pairs={{1,0},{2,1},{3,2},{4,3},{5,4},{6,5},{7,6},{64,7},{65,64},{66,65},{... | collective-permute-start | bytes 405512 | tf_op jit(solution)/shard_map/ppermute | solution.py:550
  52.4 6.3 %collective-permute-start.11 = (f32[15,8,128]{2,1,0:T(8,128)S(1)}, f32[15,8,128]{2,1,0:T(8,128)S(1)}, u32[]{:S(2)}, u32[]{:S(2)}) collective-permute-start(f32[15,8,128]{2,1,0:T(8,128)S(1)} %get-tuple-element.74), channel_id=1, source_target_pairs={{8,0},{16,8},{24,16},{32,24},{40,32},{48,40},{56,48},{9,1},{17,9},... | collective-permute-start | bytes 184328 | tf_op jit(solution)/shard_map/ppermute | solution.py:550
  53.7 5.3 %collective-permute-start.10 = (f32[15,8,128]{2,1,0:T(8,128)S(1)}, f32[15,8,128]{2,1,0:T(8,128)S(1)}, u32[]{:S(2)}, u32[]{:S(2)}) collective-permute-start(f32[15,8,128]{2,1,0:T(8,128)S(1)} %get-tuple-element.75), channel_id=1, source_target_pairs={{0,8},{8,16},{16,24},{24,32},{32,40},{40,48},{48,56},{1,9},{9,17},... | collective-permute-start | bytes 184328 | tf_op jit(solution)/shard_map/ppermute | solution.py:545

commit v3 on v2

--- a/solution.py
+++ b/solution.py
@@ -297,7 +297,7 @@
 def first_kernel(
     inside, table, xlo, xhi, ylo, yhi, left, own, right, below, above, centre,
     _kh, _kv, _fx, _fy, _fz, _scale, _s1,
-    d_out, q_out, xm_lo, xm_hi, tile_out, coefs_out, kh, kv, fx, fy, fz, scale, s1,
+    d_out, q_out, q_far, q_near, tile_out, coefs_out, kh, kv, fx, fy, fz, scale, s1,
     d, stack, spread, tiles,
 ):
     for n in range(3):
@@ -399,11 +399,14 @@
         ]
     )
     tile_out[...] = tile
+    low_plane, high_plane = 0, NXL - 2
+    odd = inside[4] > 0.5
+    far, near = jnp.where(odd, high_plane, low_plane), jnp.where(odd, low_plane, high_plane)
     for n in range(2):
-        xm_lo[pl.ds(128 * n, 128), :] = q_out[n]
-        xm_hi[pl.ds(128 * n, 128), :] = q_out[NXL - 2 + n]
-    xm_lo[256:264, :] = tile
-    xm_hi[256:264, :] = tile
+        q_far[pl.ds(128 * n, 128), :] = q_out[far + n]
+        q_near[pl.ds(128 * n, 128), :] = q_out[near + n]
+    q_far[256:264, :] = tile
+    q_near[256:264, :] = tile
 
 
 INNER_CHUNKS = ((24, 24, 0), (48, 32, 1), (80, 32, 2), (112, 24, 3))
@@ -540,14 +543,21 @@
     )(*operands)
 
 
-def upward(values, axis):
-    count = lax.axis_size(axis)
-    return lax.ppermute(values, axis, [(i, i + 1) for i in range(count - 1)])
-
-
-def downward(values, axis):
-    count = lax.axis_size(axis)
-    return lax.ppermute(values, axis, [(i + 1, i) for i in range(count - 1)])
+def swap(values, axis, first):
+    pairs = []
+    for i in range(first, lax.axis_size(axis) - 1, 2):
+        pairs += [(i, i + 1), (i + 1, i)]
+    return lax.ppermute(values, axis, pairs)
+
+
+def sides(far, near, odd):
+    return jnp.where(odd, near, far), jnp.where(odd, far, near)
+
+
+def swap_both(to_low, to_high, axis, odd):
+    far = swap(jnp.where(odd, to_high, to_low), axis, 1)
+    near = swap(jnp.where(odd, to_low, to_high), axis, 0)
+    return sides(far, near, odd)
 
 
 def exchange(row, axes):
@@ -562,18 +572,27 @@
 def body(right_side, perm_class, perm_table):
     x_at, y_at = lax.axis_index(X_AXES), lax.axis_index("sy")
     x_end, y_end = lax.axis_size(X_AXES) - 1, lax.axis_size("sy") - 1
-    inside = jnp.stack([x_at > 0, x_at < x_end, y_at > 0, y_at < y_end]).astype(F32)
+    x_odd, y_odd = x_at % 2 == 1, y_at % 2 == 1
+    flags = [x_at > 0, x_at < x_end, y_at > 0, y_at < y_end, x_odd]
+    inside = jnp.stack(flags).astype(F32)
     pad = ((0, 6), (0, NZ - perm_table.shape[1]))
     table = jnp.pad(perm_table, pad, constant_values=1.0)
 
     def packed(classes, values):
         return jnp.concatenate([classes.astype(F32), values])
 
-    xlo = upward(packed(perm_class[-3:], right_side[-2:]), X_AXES)
-    xhi = downward(packed(perm_class[:3], right_side[:2]), X_AXES)
-    ylo = upward(packed(perm_class[:, -8:], right_side[:, -8:]), "sy")
-    yhi = downward(packed(perm_class[:, :8], right_side[:, :8]), "sy")
-
+    def x_planes(low):
+        classes = lax.dynamic_slice_in_dim(perm_class, jnp.where(low, 0, NXL - 3), 3)
+        values = lax.dynamic_slice_in_dim(right_side, jnp.where(low, 0, NXL - 2), 2)
+        return packed(classes, values)
+
+    def y_rows(at):
+        return packed(perm_class[:, at : at + 8], right_side[:, at : at + 8])
+
+    x_far = swap(x_planes(~x_odd), X_AXES, 1)
+    x_near = swap(x_planes(x_odd), X_AXES, 0)
+    ylo, yhi = swap_both(y_rows(0), y_rows(NYL - 8), "sy", y_odd)
+    xlo, xhi = sides(x_far, x_near, x_odd)
     block, big = (NXL, NYL, NZ), (PLANES, ROWS, NZ)
     kh, kv, fz, tiles = call(
         own_kernel, "own", (table, perm_class, right_side), [big] * 3 + [(448, NZ)], []
@@ -587,16 +606,15 @@
         cells_kernel, "cells", (inside, table, right_side) + halos + (kh, kv, fz),
         [big] * 7, [], 1, {7: 0, 8: 1},
     )
-    left, right = upward(own, X_AXES), downward(own, X_AXES)
+    left, right = swap_both(own, own, X_AXES, x_odd)
 
     def rim(rows):
         parts = [xlo[:3, rows], xhi[:3, rows], xlo[3:, rows], xhi[3:, rows]]
         return jnp.concatenate(parts + [left[None], own[None], right[None]])
 
-    below = upward(rim(slice(NYL - 8, NYL)), "sy")
-    above = downward(rim(slice(0, 8)), "sy")
-
-    d0, q0, xm_lo, xm_hi, tile, coefs, _, _, fx, fy, fz, scale, _ = call(
+    below, above = swap_both(rim(slice(0, 8)), rim(slice(NYL - 8, NYL)), "sy", y_odd)
+
+    d0, q0, q_far, q_near, tile, coefs, _, _, fx, fy, fz, scale, _ = call(
         first_kernel, "first",
         (inside, table) + halos + (left, own, right, below, above, centre)
         + (kh, kv, fx, fy, fz, scale, s1),
@@ -604,7 +622,7 @@
         [big, (16, NZ), (6, 16, NZ), (16 * 8, NZ)], 1,
         {12 + n: 6 + n for n in range(7)},
     )
-    qlo, qhi = upward(xm_hi, X_AXES), downward(xm_lo, X_AXES)
+    qlo, qhi = sides(swap(q_far, X_AXES, 1), swap(q_near, X_AXES, 0), x_odd)
     s1, d, known = call(
         inner_kernel, "inner", (right_side, d0, q0, fx, fy, fz, scale),
         [big, big, (16, NZ)], [],
@@ -615,8 +633,7 @@
         parts += [qhi[at : at + 8][None], qhi[128 + at : 136 + at][None]]
         return jnp.concatenate(parts + [qlo[256:][None], tile[None], qhi[256:][None]])
 
-    below = upward(rim_q(NYL - 8), "sy")
-    above = downward(rim_q(0), "sy")
+    below, above = swap_both(rim_q(0), rim_q(NYL - 8), "sy", y_odd)
     p, s, dots, _, _ = call(
         second_kernel, "second",
         (right_side, d0, q0, qlo, qhi, tile, below, above, coefs, fx, fy, fz, scale, centre)

time: 113 us -> 103 us (0.912)
  blocking collectives: 48.8 us -> 39.6 us
    all_to_all x2, blocking collectives: 48.8 us -> 39.6 us  [exchange(): return lax.all_to_all(rows, axes, 0, 0).reshape(count, NZ)]
  transfers between devices with their start and end apart: 12 -> 12, of which waited for: 4 -> 5; matrix products, arithmetic and copies ran while one was open for 0% -> 0% of each run, Pallas kernels for 5% -> 6%
where the time goes in v3:
time: 103 us
  blocking collectives  39.6 us (38%)
  starting transfers between devices  35.8 us (35%)
  Pallas kernels  16.8 us (16%)
  waiting for transfers between devices  6.86 us (7%)
  other arithmetic  1.38 us (1%)
  local copies, waits for them, and re-layouts  1.21 us (1%)
  between operations  1.12 us (1%)
    all_to_all x2, blocking collectives, exchange(): return lax.all_to_all(rows, axes, 0, 0).reshape(count, NZ)  39.6 us
    ppermute x12, starting transfers between devices, swap(): return lax.ppermute(values, axis, pairs)  35.8 us
    pallas_call x7, Pallas kernels, call(): pl.pallas_call(kernel, name=name, out_shape=[jax.ShapeDtypeStruct(s, F32)...  16.8 us
    ppermute x12, waiting for transfers between devices, swap(): return lax.ppermute(values, axis, pairs)  6.86 us
  transfers between devices with their start and end apart: 12, of which 5 were waited for; matrix products, arithmetic and copies ran while one was open for 0% of the time, Pallas kernels for 6%

profile of v3, /device:TPU:1, one launch (start us, length us, event | category | flops | bytes accessed | tf_op | source)
XLA Modules:
  0.0 102.7 jit_solution(1953304041031378156)
XLA Ops:
  0.7 1.0 constant_dynamic-slice_fusion
  1.6 0.0 copy-start.1
  1.7 0.0 copy-start
  1.7 1.1 %dynamic-slice_convert_fusion = (f32[3,128,128]{2,1,0:T(8,128)S(1)}, f32[3,128,128]{2,1,0:T(8,128)S(1)}) fusion(s32[8,128,128]{2,1,0:T(8,128)} %cls.1, s32[]{:T(128)S(6)} %select_n.132, s32[]{:T(128)S(6)} %select_n.130), kind=kLoop, calls=%fused_computation.2 | loop fusion | flops 98304 | bytes 786440 | tf_op jit(solution)/shard_map/convert_element_type | solution.py:582
  2.8 0.0 copy-start.2
  2.9 8.7 %collective-permute-start = (f32[5,128,128]{2,1,0:T(8,128)S(1)}, f32[5,128,128]{2,1,0:T(8,128)S(1)}, u32[]{:S(2)}, u32[]{:S(2)}) collective-permute-start(f32[5,128,128]{2,1,0:T(8,128)S(1)} %pad_maximum_fusion), channel_id=1, source_target_pairs={{0,1},{1,0},{2,3},{3,2},{4,5},{5,4},{6,7},{7,6},{64,65},{65,64},{6... | collective-permute-start | bytes 983048 | tf_op jit(solution)/shard_map/ppermute | solution.py:550
  11.7 1.9 %collective-permute-start.1 = (f32[5,128,128]{2,1,0:T(8,128)S(1)}, f32[5,128,128]{2,1,0:T(8,128)S(1)}, u32[]{:S(2)}, u32[]{:S(2)}) collective-permute-start(f32[5,128,128]{2,1,0:T(8,128)S(1)} %pad_maximum_fusion.1), channel_id=1, source_target_pairs={{1,2},{2,1},{3,4},{4,3},{5,6},{6,5},{7,64},{64,7},{65,66},{66,65},... | collective-permute-start | bytes 983048 | tf_op jit(solution)/shard_map/ppermute | solution.py:550
  13.7 0.7 collective-permute-start.3
  14.3 1.9 %collective-permute-start.2 = (f32[16,8,128]{2,1,0:T(8,128)S(1)}, f32[16,8,128]{2,1,0:T(8,128)S(1)}, u32[]{:S(2)}, u32[]{:S(2)}) collective-permute-start(f32[16,8,128]{2,1,0:T(8,128)S(1)} %get-tuple-element.97), channel_id=1, source_target_pairs={{0,8},{8,0},{16,24},{24,16},{32,40},{40,32},{48,56},{56,48},{1,9},... | collective-permute-start | bytes 196616 | tf_op jit(solution)/shard_map/ppermute | solution.py:550
  16.3 0.1 stack.23
  16.4 2.0 %own.1 = (f32[14,160,128]{2,1,0:T(8,128)S(1)}, f32[14,160,128]{2,1,0:T(8,128)S(1)}, f32[14,160,128]{2,1,0:T(8,128)S(1)}, f32[448,128]{1,0:T(8,128)S(1)}) custom-call(f32[8,128]{1,0:T(8,128)S(1)} %pad.4.table, s32[8,128,128]{2,1,0:T(8,128)S(1)} %copy-done.1, f32[8,128,128]{2,1,0:T(8,128)S(1)} %copy-done), custom_call_target="tpu_custom_call" | custom-call | tf_op jit(solution)/shard_map/own/pallas_call | solution.py:534
  18.4 0.9 collective-permute-done.2
  19.4 0.7 collective-permute-done.1
  20.1 0.9 coarse.1.own
  21.0 4.1 %collective-permute-start.5 = (f32[8,128]{1,0:T(8,128)S(1)}, f32[8,128]{1,0:T(8,128)S(1)}, u32[]{:S(2)}, u32[]{:S(2)}) collective-permute-start(f32[8,128]{1,0:T(8,128)S(1)} %coarse.1.own), channel_id=1, source_target_pairs={{1,2},{2,1},{3,4},{4,3},{5,6},{6,5},{7,64},{64,7},{65,66},{66,65},... | collective-permute-start | bytes 12296 | tf_op jit(solution)/shard_map/ppermute | solution.py:550
  25.2 1.9 %collective-permute-start.4 = (f32[8,128]{1,0:T(8,128)S(1)}, f32[8,128]{1,0:T(8,128)S(1)}, u32[]{:S(2)}, u32[]{:S(2)}) collective-permute-start(f32[8,128]{1,0:T(8,128)S(1)} %coarse.1.own), channel_id=1, source_target_pairs={{0,1},{1,0},{2,3},{3,2},{4,5},{5,4},{6,7},{7,6},{64,65},{65,64},{6... | collective-permute-start | bytes 12296 | tf_op jit(solution)/shard_map/ppermute | solution.py:550
  27.2 1.1 %collective-permute-done.4 = f32[8,128]{1,0:T(8,128)S(1)} collective-permute-done((f32[8,128]{1,0:T(8,128)S(1)}, f32[8,128]{1,0:T(8,128)S(1)}, u32[]{:S(2)}, u32[]{:S(2)}) %collective-permute-start.4) | collective-permute-done | bytes 4128 | tf_op jit(solution)/shard_map/ppermute | solution.py:550
  28.3 0.7 collective-permute-start.7
  29.0 4.7 %collective-permute-start.6 = (f32[13,8,128]{2,1,0:T(8,128)S(1)}, f32[13,8,128]{2,1,0:T(8,128)S(1)}, u32[]{:S(2)}, u32[]{:S(2)}) collective-permute-start(f32[13,8,128]{2,1,0:T(8,128)S(1)} %get-tuple-element.105), channel_id=1, source_target_pairs={{0,8},{8,0},{16,24},{24,16},{32,40},{40,32},{48,56},{56,48},{1,9},... | collective-permute-start | bytes 159752 | tf_op jit(solution)/shard_map/ppermute | solution.py:550
  33.7 2.7 %cells.1 = (f32[14,160,128]{2,1,0:T(8,128)S(1)}, f32[14,160,128]{2,1,0:T(8,128)S(1)}, f32[14,160,128]{2,1,0:T(8,128)S(1)}, f32[14,160,128]{2,1,0:T(8,128)S(1)}, ...) custom-call(f32[5]{0:T(128)S(1)} %convert_element_type.15.inside, ...), custom_call_target="tpu_custom_call", output_to_operand_aliasing={{0}: (7, {}), {1}: (8, {})} | custom-call | tf_op jit(solution)/shard_map/cells/pallas_call | solution.py:534
  36.4 6.0 %first.1 = (f32[8,128,128]{2,1,0:T(8,128)S(1)}, f32[8,128,128]{2,1,0:T(8,128)S(1)}, f32[264,128]{1,0:T(8,128)S(1)}, f32[264,128]{1,0:T(8,128)S(1)}, f32[8,128]{1...) custom-call(f32[5]{0:T(128)S(1)} %convert_element_type.15.inside, ...), custom_call_target="tpu_custom_call", output_to_operand_aliasing={{6}: (12, {}), {7}: (13, {}), {8}: (14, {}), {9}: (15, {}),... | custom-call | tf_op jit(solution)/shard_map/first/pallas_call | solution.py:534
  42.4 2.6 %collective-permute-start.8 = (f32[264,128]{1,0:T(8,128)S(1)}, f32[264,128]{1,0:T(8,128)S(1)}, u32[]{:S(2)}, u32[]{:S(2)}) collective-permute-start(f32[264,128]{1,0:T(8,128)S(1)} %get-tuple-element.42), channel_id=1, source_target_pairs={{0,1},{1,0},{2,3},{3,2},{4,5},{5,4},{6,7},{7,6},{64,65},{65,64},{6... | collective-permute-start | bytes 405512 | tf_op jit(solution)/shard_map/ppermute | solution.py:550
  45.0 2.7 %collective-permute-start.9 = (f32[264,128]{1,0:T(8,128)S(1)}, f32[264,128]{1,0:T(8,128)S(1)}, u32[]{:S(2)}, u32[]{:S(2)}) collective-permute-start(f32[264,128]{1,0:T(8,128)S(1)} %get-tuple-element.43), channel_id=1, source_target_pairs={{1,2},{2,1},{3,4},{4,3},{5,6},{6,5},{7,64},{64,7},{65,66},{66,65},... | collective-permute-start | bytes 405512 | tf_op jit(solution)/shard_map/ppermute | solution.py:550
  47.8 3.6 %collective-permute-done.9 = f32[264,128]{1,0:T(8,128)S(1)} collective-permute-done((f32[264,128]{1,0:T(8,128)S(1)}, f32[264,128]{1,0:T(8,128)S(1)}, u32[]{:S(2)}, u32[]{:S(2)}) %collective-permute-start.9) | collective-permute-done | bytes 135200 | tf_op jit(solution)/shard_map/ppermute | solution.py:550
  51.5 0.7 collective-permute-start.11
  52.2 5.1 %collective-permute-start.10 = (f32[15,8,128]{2,1,0:T(8,128)S(1)}, f32[15,8,128]{2,1,0:T(8,128)S(1)}, u32[]{:S(2)}, u32[]{:S(2)}) collective-permute-start(f32[15,8,128]{2,1,0:T(8,128)S(1)} %get-tuple-element.101), channel_id=1, source_target_pairs={{0,8},{8,0},{16,24},{24,16},{32,40},{40,32},{48,56},{56,48},{1,9},... | collective-permute-start | bytes 184328 | tf_op jit(solution)/shard_map/ppermute | solution.py:550
  57.3 1.0 inner.1
  58.3 0.6 collective-permute-done.10
  58.9 2.7 %second.1 = (f32[8,128,128]{2,1,0:T(8,128)S(1)}, f32[8,128,128]{2,1,0:T(8,128)S(1)}, f32[1,128]{1,0:T(1,128)S(1)}, f32[14,160,128]{2,1,0:T(8,128)S(1)}, f32[14,160,128]{2,1,0:T(8,128)S(1)}) custom-call(f32[8,128,128]{2,1,0:T(8,128)S(1)} %copy-done, f32[8,128,128]{2,1,0:T(8,128)S(1)} %get-tuple-element.40.d0, ...), custom_call_target="tpu_custom_call", output_to_operand_aliasing={{3}: (15, {}), {4}: (16, {})} | custom-call | tf_op jit(solution)/shard_map/second/pallas_call | solution.py:534
  61.6 21.6 %all_to_all.10 = f32[64,1,128]{2,1,0:T(1,128)S(1)} all-to-all(f32[64,1,128]{2,1,0:T(1,128)S(1)} %broadcast_in_dim.76), channel_id=1, replica_groups=mesh['sx'=8,'sy'=8,'cg'=8] {'sy','cg'}, dimensions={0} | all-to-all | bytes 65536 | tf_op jit(solution)/shard_map/all_to_all | solution.py:566
  83.2 17.9 %all_to_all.11 = f32[8,1,128]{2,1,0:T(1,128)S(1)} all-to-all(f32[8,1,128]{2,1,0:T(1,128)S(1)} %broadcast_in_dim.77), channel_id=1, replica_groups=mesh['sx'=8,'sy'=8,'cg'=8] {'sx'}, dimensions={0} | all-to-all | bytes 8192 | tf_op jit(solution)/shard_map/all_to_all | solution.py:566
  101.2 1.6 %last.1 = (f32[8,128,128]{2,1,0:T(8,128)}, f32[8,128,128]{2,1,0:T(8,128)}) custom-call(f32[8,128]{1,0:T(8,128)S(1)} %bitcast.64, f32[8,128,128]{2,1,0:T(8,128)S(1)} %copy-done, f32[8,128,128]{2,1,0:T(8,128)S(1)} %get-tuple-element.40.d0, f32[8,128,128]{2,1,0:T(8,128)S(1)} %get-tuple-element.41.q0, f32[8,128,128]{2,1,0:T(8,128)S(1)} %get-tuple-element.54.p, ...), custom_call_target="tpu_custom_call" | custom-call | tf_op jit(solution)/shard_map/last/pallas_call | solution.py:534
  (44 shorter events, 0.4 us)
Async XLA Ops:
  1.6 11.9 %copy-start.1 = (s32[8,128,128]{2,1,0:T(8,128)S(1)}, s32[8,128,128]{2,1,0:T(8,128)}, u32[]{:S(2)}) copy-start(s32[8,128,128]{2,1,0:T(8,128)} %cls.1) | copy-start | bytes 1572868
  1.7 12.0 %copy-start = (f32[8,128,128]{2,1,0:T(8,128)S(1)}, f32[8,128,128]{2,1,0:T(8,128)}, u32[]{:S(2)}) copy-start(f32[8,128,128]{2,1,0:T(8,128)} %rhs.9) | copy-start | bytes 1572868
  2.8 13.6 %copy-start.2 = (f32[2,16]{1,0:T(2,128)S(1)}, f32[2,16]{1,0:T(2,128)}, u32[]{:S(2)}) copy-start(f32[2,16]{1,0:T(2,128)} %param.5) | copy-start | bytes 388
  2.9 16.5 %collective-permute-start = (f32[5,128,128]{2,1,0:T(8,128)S(1)}, f32[5,128,128]{2,1,0:T(8,128)S(1)}, u32[]{:S(2)}, u32[]{:S(2)}) collective-permute-start(f32[5,128,128]{2,1,0:T(8,128)S(1)} %pad_maximum_fusion), channel_id=1, source_target_pairs={{0,1},{1,0},{2,3},{3,2},{4,5},{5,4},{6,7},{7,6},{64,65},{65,64},{6... | collective-permute-start | bytes 983048 | tf_op jit(solution)/shard_map/ppermute | solution.py:550
  11.7 8.4 %collective-permute-start.1 = (f32[5,128,128]{2,1,0:T(8,128)S(1)}, f32[5,128,128]{2,1,0:T(8,128)S(1)}, u32[]{:S(2)}, u32[]{:S(2)}) collective-permute-start(f32[5,128,128]{2,1,0:T(8,128)S(1)} %pad_maximum_fusion.1), channel_id=1, source_target_pairs={{1,2},{2,1},{3,4},{4,3},{5,6},{6,5},{7,64},{64,7},{65,66},{66,65},... | collective-permute-start | bytes 983048 | tf_op jit(solution)/shard_map/ppermute | solution.py:550
  13.7 4.8 %collective-permute-start.3 = (f32[16,8,128]{2,1,0:T(8,128)S(1)}, f32[16,8,128]{2,1,0:T(8,128)S(1)}, u32[]{:S(2)}, u32[]{:S(2)}) collective-permute-start(f32[16,8,128]{2,1,0:T(8,128)S(1)} %get-tuple-element.96), channel_id=1, source_target_pairs={{8,16},{16,8},{24,32},{32,24},{40,48},{48,40},{9,17},{17,9},{25,33... | collective-permute-start | bytes 196616 | tf_op jit(solution)/shard_map/ppermute | solution.py:550
  14.3 5.0 %collective-permute-start.2 = (f32[16,8,128]{2,1,0:T(8,128)S(1)}, f32[16,8,128]{2,1,0:T(8,128)S(1)}, u32[]{:S(2)}, u32[]{:S(2)}) collective-permute-start(f32[16,8,128]{2,1,0:T(8,128)S(1)} %get-tuple-element.97), channel_id=1, source_target_pairs={{0,8},{8,0},{16,24},{24,16},{32,40},{40,32},{48,56},{56,48},{1,9},... | collective-permute-start | bytes 196616 | tf_op jit(solution)/shard_map/ppermute | solution.py:550
  21.0 6.1 %collective-permute-start.5 = (f32[8,128]{1,0:T(8,128)S(1)}, f32[8,128]{1,0:T(8,128)S(1)}, u32[]{:S(2)}, u32[]{:S(2)}) collective-permute-start(f32[8,128]{1,0:T(8,128)S(1)} %coarse.1.own), channel_id=1, source_target_pairs={{1,2},{2,1},{3,4},{4,3},{5,6},{6,5},{7,64},{64,7},{65,66},{66,65},... | collective-permute-start | bytes 12296 | tf_op jit(solution)/shard_map/ppermute | solution.py:550
  25.2 3.1 %collective-permute-start.4 = (f32[8,128]{1,0:T(8,128)S(1)}, f32[8,128]{1,0:T(8,128)S(1)}, u32[]{:S(2)}, u32[]{:S(2)}) collective-permute-start(f32[8,128]{1,0:T(8,128)S(1)} %coarse.1.own), channel_id=1, source_target_pairs={{0,1},{1,0},{2,3},{3,2},{4,5},{5,4},{6,7},{7,6},{64,65},{65,64},{6... | collective-permute-start | bytes 12296 | tf_op jit(solution)/shard_map/ppermute | solution.py:550
  28.3 8.1 %collective-permute-start.7 = (f32[13,8,128]{2,1,0:T(8,128)S(1)}, f32[13,8,128]{2,1,0:T(8,128)S(1)}, u32[]{:S(2)}, u32[]{:S(2)}) collective-permute-start(f32[13,8,128]{2,1,0:T(8,128)S(1)} %get-tuple-element.104), channel_id=1, source_target_pairs={{8,16},{16,8},{24,32},{32,24},{40,48},{48,40},{9,17},{17,9},{25,33... | collective-permute-start | bytes 159752 | tf_op jit(solution)/shard_map/ppermute | solution.py:550
  29.0 7.4 %collective-permute-start.6 = (f32[13,8,128]{2,1,0:T(8,128)S(1)}, f32[13,8,128]{2,1,0:T(8,128)S(1)}, u32[]{:S(2)}, u32[]{:S(2)}) collective-permute-start(f32[13,8,128]{2,1,0:T(8,128)S(1)} %get-tuple-element.105), channel_id=1, source_target_pairs={{0,8},{8,0},{16,24},{24,16},{32,40},{40,32},{48,56},{56,48},{1,9},... | collective-permute-start | bytes 159752 | tf_op jit(solution)/shard_map/ppermute | solution.py:550
  42.4 5.4 %collective-permute-start.8 = (f32[264,128]{1,0:T(8,128)S(1)}, f32[264,128]{1,0:T(8,128)S(1)}, u32[]{:S(2)}, u32[]{:S(2)}) collective-permute-start(f32[264,128]{1,0:T(8,128)S(1)} %get-tuple-element.42), channel_id=1, source_target_pairs={{0,1},{1,0},{2,3},{3,2},{4,5},{5,4},{6,7},{7,6},{64,65},{65,64},{6... | collective-permute-start | bytes 405512 | tf_op jit(solution)/shard_map/ppermute | solution.py:550
  45.0 6.3 %collective-permute-start.9 = (f32[264,128]{1,0:T(8,128)S(1)}, f32[264,128]{1,0:T(8,128)S(1)}, u32[]{:S(2)}, u32[]{:S(2)}) collective-permute-start(f32[264,128]{1,0:T(8,128)S(1)} %get-tuple-element.43), channel_id=1, source_target_pairs={{1,2},{2,1},{3,4},{4,3},{5,6},{6,5},{7,64},{64,7},{65,66},{66,65},... | collective-permute-start | bytes 405512 | tf_op jit(solution)/shard_map/ppermute | solution.py:550
  51.5 6.7 %collective-permute-start.11 = (f32[15,8,128]{2,1,0:T(8,128)S(1)}, f32[15,8,128]{2,1,0:T(8,128)S(1)}, u32[]{:S(2)}, u32[]{:S(2)}) collective-permute-start(f32[15,8,128]{2,1,0:T(8,128)S(1)} %get-tuple-element.100), channel_id=1, source_target_pairs={{8,16},{16,8},{24,32},{32,24},{40,48},{48,40},{9,17},{17,9},{25,33... | collective-permute-start | bytes 184328 | tf_op jit(solution)/shard_map/ppermute | solution.py:550
  52.2 6.7 %collective-permute-start.10 = (f32[15,8,128]{2,1,0:T(8,128)S(1)}, f32[15,8,128]{2,1,0:T(8,128)S(1)}, u32[]{:S(2)}, u32[]{:S(2)}) collective-permute-start(f32[15,8,128]{2,1,0:T(8,128)S(1)} %get-tuple-element.101), channel_id=1, source_target_pairs={{0,8},{8,0},{16,24},{24,16},{32,40},{40,32},{48,56},{56,48},{1,9},... | collective-permute-start | bytes 184328 | tf_op jit(solution)/shard_map/ppermute | solution.py:550

commit v4 on v3

--- a/solution.py
+++ b/solution.py
@@ -88,7 +88,7 @@
             fz[i, rows, :] = jnp.where(iota((size, NZ), 1) < NZ - 1, z, 0.0)
         return 0
 
-    lax.fori_loop(0, NXL, plane, 0)
+    lax.fori_loop(0, NXL, plane, 0, unroll=True)
     first = iota((8, NZ), 0) == 0
     for f in range(1, 4):
         for j in range(4):
@@ -229,7 +229,7 @@
         v[i, ROWS - 8 : ROWS, :] = jnp.zeros((8, NZ), F32)
         return 0
 
-    lax.fori_loop(0, PLANES, plane, 0)
+    lax.fori_loop(0, PLANES, plane, 0, unroll=True)
 
 
 def looked_up(inside, table, kh, kv, i, at, size, classes, *sides):
@@ -263,7 +263,7 @@
         looked_up(inside, table, kh, kv, x + HX, 144, 8, yhi[x], 3)
         return 0
 
-    lax.fori_loop(0, NXL, rims, 0)
+    lax.fori_loop(0, NXL, rims, 0, unroll=True)
     for n in range(3):
         for side, base, msg in ((0, 0, xlo), (1, HX + NXL, xhi)):
             looked_up(inside, table, kh, kv, base + n, OWN, NYL, msg[n], side)
@@ -277,7 +277,7 @@
         fy[i, 144:152, :] = harmonic(kh[i, 143:151, :], kh[i, 144:152, :])
         return 0
 
-    lax.fori_loop(HX, HX + NXL, faces, 0)
+    lax.fori_loop(HX, HX + NXL, faces, 0, unroll=True)
     end = HX + NXL
     fx[end, 16:144, :] = harmonic(kh[end - 1, 16:144, :], kh[end, 16:144, :])
 
@@ -287,7 +287,7 @@
             set_scale(x + HX, at, size, 1.0, source, fx, fy, fz, scale, centre, s1)
         return 0
 
-    lax.fori_loop(0, NXL, scales, 0)
+    lax.fori_loop(0, NXL, scales, 0, unroll=True)
 
 
 RIM_PLANES = (1, 2, HX + NXL, HX + NXL + 1)
@@ -313,7 +313,7 @@
         fy[i, ROWS - 8 : ROWS, :] = ones
         return 0
 
-    lax.fori_loop(0, PLANES, pads, 0)
+    lax.fori_loop(0, PLANES, pads, 0, unroll=True)
     zero_pads(s1)
     zero_pads(d)
 
@@ -343,7 +343,7 @@
             set_faces(i, at, size)
         return 0
 
-    lax.fori_loop(1, PLANES - 1, rim_faces, 0)
+    lax.fori_loop(1, PLANES - 1, rim_faces, 0, unroll=True)
     for i in RIM_PLANES:
         for at, size, _j in OWN_CHUNKS:
             set_faces(i, at, size)
@@ -360,7 +360,7 @@
         rim_scales(x + HX, 1.0, ylo[NXL + x], yhi[NXL + x])
         return 0
 
-    lax.fori_loop(0, NXL, own_rims, 0)
+    lax.fori_loop(0, NXL, own_rims, 0, unroll=True)
     for n in range(2):
         for side, i, msg in ((0, 1 + n, xlo), (1, HX + NXL + n, xhi)):
             corner = 6 + 2 * side + n
@@ -374,7 +374,7 @@
             smooth_chunk(s1, d, fx, fy, fz, scale, spread, i, at, size, j)
         return 0
 
-    lax.fori_loop(HX - 1, HX + NXL + 1, smooth, 0)
+    lax.fori_loop(HX - 1, HX + NXL + 1, smooth, 0, unroll=True)
 
     def image(x, _):
         i = x + HX
@@ -385,7 +385,7 @@
             d_out[x, pl.ds(at - OWN, size), :] = here
         return 0
 
-    lax.fori_loop(0, NXL, image, 0)
+    lax.fori_loop(0, NXL, image, 0, unroll=True)
     for a in range(4):
         for j in range(4):
             rows = pl.ds(32 * j, 32)
@@ -429,7 +429,7 @@
         return sums
 
     zero = jnp.zeros((8, NZ), F32)
-    rd, dq = lax.fori_loop(0, NXL, plane, (zero, zero))
+    rd, dq = lax.fori_loop(0, NXL, plane, (zero, zero), unroll=True)
     known[0:8, :] = rd
     known[8:16, :] = dq
 
@@ -438,7 +438,7 @@
             smooth_chunk(s1, d, fx, fy, fz, scale, None, i, at, size, j)
         return 0
 
-    lax.fori_loop(HX + 1, HX + NXL - 1, smooth, 0)
+    lax.fori_loop(HX + 1, HX + NXL - 1, smooth, 0, unroll=True)
 
 
 def second_kernel(
@@ -456,7 +456,7 @@
         s1[i, 144:152, :] = scale[i, 144:152, :] * above[i - 1]
         return 0
 
-    lax.fori_loop(1, PLANES - 1, rims, 0)
+    lax.fori_loop(1, PLANES - 1, rims, 0, unroll=True)
     for n in range(2):
         for i, msg in ((1 + n, xlo), (HX + NXL + n, xhi)):
             s1[i, 16:144, :] = scale[i, 16:144, :] * msg[pl.ds(128 * n, 128), :]
@@ -473,7 +473,7 @@
             d[i, rows, :] = d[i, rows, :] + spread[j + 1, pl.ds((i + 5) // 2, 1), :]
         return 0
 
-    lax.fori_loop(HX + 1, HX + NXL - 1, smooth, 0)
+    lax.fori_loop(HX + 1, HX + NXL - 1, smooth, 0, unroll=True)
 
     def image(x, sums):
         i = x + HX
@@ -491,7 +491,7 @@
         return sums
 
     zero = jnp.zeros((8, NZ), F32)
-    sums = lax.fori_loop(0, NXL, image, (zero,) * 4)
+    sums = lax.fori_loop(0, NXL, image, (zero,) * 4, unroll=True)
     sums = (known[0:8, :], known[8:16, :]) + sums
     sublane, lane = iota((8, NZ), 0), iota((8, NZ), 1)
     tile = zero
@@ -523,7 +523,7 @@
             r_out[x, rows, :] = rhs[x, rows, :] - u * q0[x, rows, :] + v * s[x, rows, :]
         return 0
 
-    lax.fori_loop(0, NXL, plane, 0)
+    lax.fori_loop(0, NXL, plane, 0, unroll=True)
 
 
 VMEM = pl.BlockSpec(memory_space=pltpu.VMEM)

time: 103 us -> 98.8 us (0.959)
  Pallas kernels: 16.8 us -> 10.2 us
    pallas_call x7, Pallas kernels: 16.8 us -> 10.2 us  [call(): pl.pallas_call(kernel, name=name, out_shape=[jax.ShapeDtypeStruct(s, F32)...]
  transfers between devices with their start and end apart: 12 -> 12, of which waited for: 5 -> 6; matrix products, arithmetic and copies ran while one was open for 0% -> 0% of each run, Pallas kernels for 6% -> 4%
where the time goes in v4:
time: 98.8 us; the launch traced here: 98.2 us
  blocking collectives  40.1 us (41%)
  starting transfers between devices  36.5 us (37%)
  Pallas kernels  10.2 us (10%)
  waiting for transfers between devices  7.76 us (8%)
  other arithmetic  1.38 us (1%)
  local copies, waits for them, and re-layouts  1.22 us (1%)
  between operations  1.1 us (1%)
    all_to_all x2, blocking collectives, exchange(): return lax.all_to_all(rows, axes, 0, 0).reshape(count, NZ)  40.1 us
    ppermute x12, starting transfers between devices, swap(): return lax.ppermute(values, axis, pairs)  36.5 us
    pallas_call x7, Pallas kernels, call(): pl.pallas_call(kernel, name=name, out_shape=[jax.ShapeDtypeStruct(s, F32)...  10.2 us
    ppermute x12, waiting for transfers between devices, swap(): return lax.ppermute(values, axis, pairs)  7.76 us
  transfers between devices with their start and end apart: 12, of which 6 were waited for; matrix products, arithmetic and copies ran while one was open for 0% of the time, Pallas kernels for 4%

profile of v4, /device:TPU:1, one launch (start us, length us, event | category | flops | bytes accessed | tf_op | source)
XLA Modules:
  0.0 98.2 jit_solution(17924022678139998833)
XLA Ops:
  0.7 1.0 %constant_dynamic-slice_fusion = (f32[2,128,128]{2,1,0:T(8,128)S(1)}, f32[2,128,128]{2,1,0:T(8,128)S(1)}) fusion(f32[8,128,128]{2,1,0:T(8,128)} %rhs.9, s32[]{:T(128)S(6)} %select_n.133, s32[]{:T(128)S(6)} %select_n.131), kind=kLoop, calls=%fused_computation.66 | loop fusion | bytes 524296 | tf_op jit(solution)/shard_map/dynamic_slice | solution.py:586
  1.6 0.0 copy-start.1
  1.7 0.0 copy-start
  1.7 1.1 %dynamic-slice_convert_fusion = (f32[3,128,128]{2,1,0:T(8,128)S(1)}, f32[3,128,128]{2,1,0:T(8,128)S(1)}) fusion(s32[8,128,128]{2,1,0:T(8,128)} %cls.1, s32[]{:T(128)S(6)} %select_n.132, s32[]{:T(128)S(6)} %select_n.130), kind=kLoop, calls=%fused_computation.2 | loop fusion | flops 98304 | bytes 786440 | tf_op jit(solution)/shard_map/convert_element_type | solution.py:582
  2.9 8.7 %collective-permute-start = (f32[5,128,128]{2,1,0:T(8,128)S(1)}, f32[5,128,128]{2,1,0:T(8,128)S(1)}, u32[]{:S(2)}, u32[]{:S(2)}) collective-permute-start(f32[5,128,128]{2,1,0:T(8,128)S(1)} %pad_maximum_fusion), channel_id=1, source_target_pairs={{0,1},{1,0},{2,3},{3,2},{4,5},{5,4},{6,7},{7,6},{64,65},{65,64},{6... | collective-permute-start | bytes 983048 | tf_op jit(solution)/shard_map/ppermute | solution.py:550
  11.7 1.9 %collective-permute-start.1 = (f32[5,128,128]{2,1,0:T(8,128)S(1)}, f32[5,128,128]{2,1,0:T(8,128)S(1)}, u32[]{:S(2)}, u32[]{:S(2)}) collective-permute-start(f32[5,128,128]{2,1,0:T(8,128)S(1)} %pad_maximum_fusion.1), channel_id=1, source_target_pairs={{1,2},{2,1},{3,4},{4,3},{5,6},{6,5},{7,64},{64,7},{65,66},{66,65},... | collective-permute-start | bytes 983048 | tf_op jit(solution)/shard_map/ppermute | solution.py:550
  13.7 0.7 collective-permute-start.3
  14.3 1.9 %collective-permute-start.2 = (f32[16,8,128]{2,1,0:T(8,128)S(1)}, f32[16,8,128]{2,1,0:T(8,128)S(1)}, u32[]{:S(2)}, u32[]{:S(2)}) collective-permute-start(f32[16,8,128]{2,1,0:T(8,128)S(1)} %get-tuple-element.97), channel_id=1, source_target_pairs={{0,8},{8,0},{16,24},{24,16},{32,40},{40,32},{48,56},{56,48},{1,9},... | collective-permute-start | bytes 196616 | tf_op jit(solution)/shard_map/ppermute | solution.py:550
  16.3 0.1 stack.23
  16.4 1.8 %own.1 = (f32[14,160,128]{2,1,0:T(8,128)S(1)}, f32[14,160,128]{2,1,0:T(8,128)S(1)}, f32[14,160,128]{2,1,0:T(8,128)S(1)}, f32[448,128]{1,0:T(8,128)S(1)}) custom-call(f32[8,128]{1,0:T(8,128)S(1)} %pad.4.table, s32[8,128,128]{2,1,0:T(8,128)S(1)} %copy-done.1, f32[8,128,128]{2,1,0:T(8,128)S(1)} %copy-done), custom_call_target="tpu_custom_call" | custom-call | tf_op jit(solution)/shard_map/own/pallas_call | solution.py:534
  18.2 1.1 %collective-permute-done.2 = f32[16,8,128]{2,1,0:T(8,128)S(1)} collective-permute-done((f32[16,8,128]{2,1,0:T(8,128)S(1)}, f32[16,8,128]{2,1,0:T(8,128)S(1)}, u32[]{:S(2)}, u32[]{:S(2)}) %collective-permute-start.2) | collective-permute-done | bytes 65568 | tf_op jit(solution)/shard_map/ppermute | solution.py:550
  19.4 0.7 collective-permute-done.1
  20.1 0.9 coarse.1.own
  21.0 4.1 %collective-permute-start.5 = (f32[8,128]{1,0:T(8,128)S(1)}, f32[8,128]{1,0:T(8,128)S(1)}, u32[]{:S(2)}, u32[]{:S(2)}) collective-permute-start(f32[8,128]{1,0:T(8,128)S(1)} %coarse.1.own), channel_id=1, source_target_pairs={{1,2},{2,1},{3,4},{4,3},{5,6},{6,5},{7,64},{64,7},{65,66},{66,65},... | collective-permute-start | bytes 12296 | tf_op jit(solution)/shard_map/ppermute | solution.py:550
  25.2 1.9 %collective-permute-start.4 = (f32[8,128]{1,0:T(8,128)S(1)}, f32[8,128]{1,0:T(8,128)S(1)}, u32[]{:S(2)}, u32[]{:S(2)}) collective-permute-start(f32[8,128]{1,0:T(8,128)S(1)} %coarse.1.own), channel_id=1, source_target_pairs={{0,1},{1,0},{2,3},{3,2},{4,5},{5,4},{6,7},{7,6},{64,65},{65,64},{6... | collective-permute-start | bytes 12296 | tf_op jit(solution)/shard_map/ppermute | solution.py:550
  27.2 1.1 %collective-permute-done.4 = f32[8,128]{1,0:T(8,128)S(1)} collective-permute-done((f32[8,128]{1,0:T(8,128)S(1)}, f32[8,128]{1,0:T(8,128)S(1)}, u32[]{:S(2)}, u32[]{:S(2)}) %collective-permute-start.4) | collective-permute-done | bytes 4128 | tf_op jit(solution)/shard_map/ppermute | solution.py:550
  28.3 0.7 collective-permute-start.7
  29.0 4.7 %collective-permute-start.6 = (f32[13,8,128]{2,1,0:T(8,128)S(1)}, f32[13,8,128]{2,1,0:T(8,128)S(1)}, u32[]{:S(2)}, u32[]{:S(2)}) collective-permute-start(f32[13,8,128]{2,1,0:T(8,128)S(1)} %get-tuple-element.105), channel_id=1, source_target_pairs={{0,8},{8,0},{16,24},{24,16},{32,40},{40,32},{48,56},{56,48},{1,9},... | collective-permute-start | bytes 159752 | tf_op jit(solution)/shard_map/ppermute | solution.py:550
  33.7 1.3 %cells.1 = (f32[14,160,128]{2,1,0:T(8,128)S(1)}, f32[14,160,128]{2,1,0:T(8,128)S(1)}, f32[14,160,128]{2,1,0:T(8,128)S(1)}, f32[14,160,128]{2,1,0:T(8,128)S(1)}, ...) custom-call(f32[5]{0:T(128)S(1)} %convert_element_type.15.inside, ...), custom_call_target="tpu_custom_call", output_to_operand_aliasing={{0}: (7, {}), {1}: (8, {})} | custom-call | tf_op jit(solution)/shard_map/cells/pallas_call | solution.py:534
  35.0 0.1 collective-permute-done.6
  35.2 2.7 %first.1 = (f32[8,128,128]{2,1,0:T(8,128)S(1)}, f32[8,128,128]{2,1,0:T(8,128)S(1)}, f32[264,128]{1,0:T(8,128)S(1)}, f32[264,128]{1,0:T(8,128)S(1)}, f32[8,128]{1...) custom-call(f32[5]{0:T(128)S(1)} %convert_element_type.15.inside, ...), custom_call_target="tpu_custom_call", output_to_operand_aliasing={{6}: (12, {}), {7}: (13, {}), {8}: (14, {}), {9}: (15, {}),... | custom-call | tf_op jit(solution)/shard_map/first/pallas_call | solution.py:534
  37.9 3.2 %collective-permute-start.8 = (f32[264,128]{1,0:T(8,128)S(1)}, f32[264,128]{1,0:T(8,128)S(1)}, u32[]{:S(2)}, u32[]{:S(2)}) collective-permute-start(f32[264,128]{1,0:T(8,128)S(1)} %get-tuple-element.42), channel_id=1, source_target_pairs={{0,1},{1,0},{2,3},{3,2},{4,5},{5,4},{6,7},{7,6},{64,65},{65,64},{6... | collective-permute-start | bytes 405512 | tf_op jit(solution)/shard_map/ppermute | solution.py:550
  41.1 2.7 %collective-permute-start.9 = (f32[264,128]{1,0:T(8,128)S(1)}, f32[264,128]{1,0:T(8,128)S(1)}, u32[]{:S(2)}, u32[]{:S(2)}) collective-permute-start(f32[264,128]{1,0:T(8,128)S(1)} %get-tuple-element.43), channel_id=1, source_target_pairs={{1,2},{2,1},{3,4},{4,3},{5,6},{6,5},{7,64},{64,7},{65,66},{66,65},... | collective-permute-start | bytes 405512 | tf_op jit(solution)/shard_map/ppermute | solution.py:550
  43.9 3.6 %collective-permute-done.9 = f32[264,128]{1,0:T(8,128)S(1)} collective-permute-done((f32[264,128]{1,0:T(8,128)S(1)}, f32[264,128]{1,0:T(8,128)S(1)}, u32[]{:S(2)}, u32[]{:S(2)}) %collective-permute-start.9) | collective-permute-done | bytes 135200 | tf_op jit(solution)/shard_map/ppermute | solution.py:550
  47.6 0.7 collective-permute-start.11
  48.3 5.2 %collective-permute-start.10 = (f32[15,8,128]{2,1,0:T(8,128)S(1)}, f32[15,8,128]{2,1,0:T(8,128)S(1)}, u32[]{:S(2)}, u32[]{:S(2)}) collective-permute-start(f32[15,8,128]{2,1,0:T(8,128)S(1)} %get-tuple-element.101), channel_id=1, source_target_pairs={{0,8},{8,0},{16,24},{24,16},{32,40},{40,32},{48,56},{56,48},{1,9},... | collective-permute-start | bytes 184328 | tf_op jit(solution)/shard_map/ppermute | solution.py:550
  53.5 0.5 inner.1
  53.9 1.1 %collective-permute-done.10 = f32[15,8,128]{2,1,0:T(8,128)S(1)} collective-permute-done((f32[15,8,128]{2,1,0:T(8,128)S(1)}, f32[15,8,128]{2,1,0:T(8,128)S(1)}, u32[]{:S(2)}, u32[]{:S(2)}) %collective-permute-start.10) | collective-permute-done | bytes 61472 | tf_op jit(solution)/shard_map/ppermute | solution.py:550
  55.1 1.8 %second.1 = (f32[8,128,128]{2,1,0:T(8,128)S(1)}, f32[8,128,128]{2,1,0:T(8,128)S(1)}, f32[1,128]{1,0:T(1,128)S(1)}, f32[14,160,128]{2,1,0:T(8,128)S(1)}, f32[14,160,128]{2,1,0:T(8,128)S(1)}) custom-call(f32[8,128,128]{2,1,0:T(8,128)S(1)} %copy-done, f32[8,128,128]{2,1,0:T(8,128)S(1)} %get-tuple-element.40.d0, ...), custom_call_target="tpu_custom_call", output_to_operand_aliasing={{3}: (15, {}), {4}: (16, {})} | custom-call | tf_op jit(solution)/shard_map/second/pallas_call | solution.py:534
  56.8 22.1 %all_to_all.10 = f32[64,1,128]{2,1,0:T(1,128)S(1)} all-to-all(f32[64,1,128]{2,1,0:T(1,128)S(1)} %broadcast_in_dim.76), channel_id=1, replica_groups=mesh['sx'=8,'sy'=8,'cg'=8] {'sy','cg'}, dimensions={0} | all-to-all | bytes 65536 | tf_op jit(solution)/shard_map/all_to_all | solution.py:566
  79.0 17.9 %all_to_all.11 = f32[8,1,128]{2,1,0:T(1,128)S(1)} all-to-all(f32[8,1,128]{2,1,0:T(1,128)S(1)} %broadcast_in_dim.77), channel_id=1, replica_groups=mesh['sx'=8,'sy'=8,'cg'=8] {'sx'}, dimensions={0} | all-to-all | bytes 8192 | tf_op jit(solution)/shard_map/all_to_all | solution.py:566
  96.9 1.3 %last.1 = (f32[8,128,128]{2,1,0:T(8,128)}, f32[8,128,128]{2,1,0:T(8,128)}) custom-call(f32[8,128]{1,0:T(8,128)S(1)} %bitcast.64, f32[8,128,128]{2,1,0:T(8,128)S(1)} %copy-done, f32[8,128,128]{2,1,0:T(8,128)S(1)} %get-tuple-element.40.d0, f32[8,128,128]{2,1,0:T(8,128)S(1)} %get-tuple-element.41.q0, f32[8,128,128]{2,1,0:T(8,128)S(1)} %get-tuple-element.54.p, ...), custom_call_target="tpu_custom_call" | custom-call | tf_op jit(solution)/shard_map/last/pallas_call | solution.py:534
  (44 shorter events, 0.4 us)
Async XLA Ops:
  1.6 11.9 %copy-start.1 = (s32[8,128,128]{2,1,0:T(8,128)S(1)}, s32[8,128,128]{2,1,0:T(8,128)}, u32[]{:S(2)}) copy-start(s32[8,128,128]{2,1,0:T(8,128)} %cls.1) | copy-start | bytes 1572868
  1.7 12.0 %copy-start = (f32[8,128,128]{2,1,0:T(8,128)S(1)}, f32[8,128,128]{2,1,0:T(8,128)}, u32[]{:S(2)}) copy-start(f32[8,128,128]{2,1,0:T(8,128)} %rhs.9) | copy-start | bytes 1572868
  2.8 13.6 %copy-start.2 = (f32[2,16]{1,0:T(2,128)S(1)}, f32[2,16]{1,0:T(2,128)}, u32[]{:S(2)}) copy-start(f32[2,16]{1,0:T(2,128)} %param.5) | copy-start | bytes 388
  2.9 16.5 %collective-permute-start = (f32[5,128,128]{2,1,0:T(8,128)S(1)}, f32[5,128,128]{2,1,0:T(8,128)S(1)}, u32[]{:S(2)}, u32[]{:S(2)}) collective-permute-start(f32[5,128,128]{2,1,0:T(8,128)S(1)} %pad_maximum_fusion), channel_id=1, source_target_pairs={{0,1},{1,0},{2,3},{3,2},{4,5},{5,4},{6,7},{7,6},{64,65},{65,64},{6... | collective-permute-start | bytes 983048 | tf_op jit(solution)/shard_map/ppermute | solution.py:550
  11.7 8.4 %collective-permute-start.1 = (f32[5,128,128]{2,1,0:T(8,128)S(1)}, f32[5,128,128]{2,1,0:T(8,128)S(1)}, u32[]{:S(2)}, u32[]{:S(2)}) collective-permute-start(f32[5,128,128]{2,1,0:T(8,128)S(1)} %pad_maximum_fusion.1), channel_id=1, source_target_pairs={{1,2},{2,1},{3,4},{4,3},{5,6},{6,5},{7,64},{64,7},{65,66},{66,65},... | collective-permute-start | bytes 983048 | tf_op jit(solution)/shard_map/ppermute | solution.py:550
  13.7 4.5 %collective-permute-start.3 = (f32[16,8,128]{2,1,0:T(8,128)S(1)}, f32[16,8,128]{2,1,0:T(8,128)S(1)}, u32[]{:S(2)}, u32[]{:S(2)}) collective-permute-start(f32[16,8,128]{2,1,0:T(8,128)S(1)} %get-tuple-element.96), channel_id=1, source_target_pairs={{8,16},{16,8},{24,32},{32,24},{40,48},{48,40},{9,17},{17,9},{25,33... | collective-permute-start | bytes 196616 | tf_op jit(solution)/shard_map/ppermute | solution.py:550
  14.3 5.0 %collective-permute-start.2 = (f32[16,8,128]{2,1,0:T(8,128)S(1)}, f32[16,8,128]{2,1,0:T(8,128)S(1)}, u32[]{:S(2)}, u32[]{:S(2)}) collective-permute-start(f32[16,8,128]{2,1,0:T(8,128)S(1)} %get-tuple-element.97), channel_id=1, source_target_pairs={{0,8},{8,0},{16,24},{24,16},{32,40},{40,32},{48,56},{56,48},{1,9},... | collective-permute-start | bytes 196616 | tf_op jit(solution)/shard_map/ppermute | solution.py:550
  21.0 6.1 %collective-permute-start.5 = (f32[8,128]{1,0:T(8,128)S(1)}, f32[8,128]{1,0:T(8,128)S(1)}, u32[]{:S(2)}, u32[]{:S(2)}) collective-permute-start(f32[8,128]{1,0:T(8,128)S(1)} %coarse.1.own), channel_id=1, source_target_pairs={{1,2},{2,1},{3,4},{4,3},{5,6},{6,5},{7,64},{64,7},{65,66},{66,65},... | collective-permute-start | bytes 12296 | tf_op jit(solution)/shard_map/ppermute | solution.py:550
  25.2 3.1 %collective-permute-start.4 = (f32[8,128]{1,0:T(8,128)S(1)}, f32[8,128]{1,0:T(8,128)S(1)}, u32[]{:S(2)}, u32[]{:S(2)}) collective-permute-start(f32[8,128]{1,0:T(8,128)S(1)} %coarse.1.own), channel_id=1, source_target_pairs={{0,1},{1,0},{2,3},{3,2},{4,5},{5,4},{6,7},{7,6},{64,65},{65,64},{6... | collective-permute-start | bytes 12296 | tf_op jit(solution)/shard_map/ppermute | solution.py:550
  28.3 6.7 %collective-permute-start.7 = (f32[13,8,128]{2,1,0:T(8,128)S(1)}, f32[13,8,128]{2,1,0:T(8,128)S(1)}, u32[]{:S(2)}, u32[]{:S(2)}) collective-permute-start(f32[13,8,128]{2,1,0:T(8,128)S(1)} %get-tuple-element.104), channel_id=1, source_target_pairs={{8,16},{16,8},{24,32},{32,24},{40,48},{48,40},{9,17},{17,9},{25,33... | collective-permute-start | bytes 159752 | tf_op jit(solution)/shard_map/ppermute | solution.py:550
  29.0 6.2 %collective-permute-start.6 = (f32[13,8,128]{2,1,0:T(8,128)S(1)}, f32[13,8,128]{2,1,0:T(8,128)S(1)}, u32[]{:S(2)}, u32[]{:S(2)}) collective-permute-start(f32[13,8,128]{2,1,0:T(8,128)S(1)} %get-tuple-element.105), channel_id=1, source_target_pairs={{0,8},{8,0},{16,24},{24,16},{32,40},{40,32},{48,56},{56,48},{1,9},... | collective-permute-start | bytes 159752 | tf_op jit(solution)/shard_map/ppermute | solution.py:550
  37.9 6.0 %collective-permute-start.8 = (f32[264,128]{1,0:T(8,128)S(1)}, f32[264,128]{1,0:T(8,128)S(1)}, u32[]{:S(2)}, u32[]{:S(2)}) collective-permute-start(f32[264,128]{1,0:T(8,128)S(1)} %get-tuple-element.42), channel_id=1, source_target_pairs={{0,1},{1,0},{2,3},{3,2},{4,5},{5,4},{6,7},{7,6},{64,65},{65,64},{6... | collective-permute-start | bytes 405512 | tf_op jit(solution)/shard_map/ppermute | solution.py:550
  41.1 6.3 %collective-permute-start.9 = (f32[264,128]{1,0:T(8,128)S(1)}, f32[264,128]{1,0:T(8,128)S(1)}, u32[]{:S(2)}, u32[]{:S(2)}) collective-permute-start(f32[264,128]{1,0:T(8,128)S(1)} %get-tuple-element.43), channel_id=1, source_target_pairs={{1,2},{2,1},{3,4},{4,3},{5,6},{6,5},{7,64},{64,7},{65,66},{66,65},... | collective-permute-start | bytes 405512 | tf_op jit(solution)/shard_map/ppermute | solution.py:550
  47.6 6.4 %collective-permute-start.11 = (f32[15,8,128]{2,1,0:T(8,128)S(1)}, f32[15,8,128]{2,1,0:T(8,128)S(1)}, u32[]{:S(2)}, u32[]{:S(2)}) collective-permute-start(f32[15,8,128]{2,1,0:T(8,128)S(1)} %get-tuple-element.100), channel_id=1, source_target_pairs={{8,16},{16,8},{24,32},{32,24},{40,48},{48,40},{9,17},{17,9},{25,33... | collective-permute-start | bytes 184328 | tf_op jit(solution)/shard_map/ppermute | solution.py:550
  48.3 6.8 %collective-permute-start.10 = (f32[15,8,128]{2,1,0:T(8,128)S(1)}, f32[15,8,128]{2,1,0:T(8,128)S(1)}, u32[]{:S(2)}, u32[]{:S(2)}) collective-permute-start(f32[15,8,128]{2,1,0:T(8,128)S(1)} %get-tuple-element.101), channel_id=1, source_target_pairs={{0,8},{8,0},{16,24},{24,16},{32,40},{40,32},{48,56},{56,48},{1,9},... | collective-permute-start | bytes 184328 | tf_op jit(solution)/shard_map/ppermute | solution.py:550

commit v5 on v4

--- a/solution.py
+++ b/solution.py
@@ -643,9 +643,25 @@
     for axes in STAGES[:-1]:
         dots = exchange(dots, axes).sum(0, keepdims=True)
     dots = exchange(dots, STAGES[-1])
-    return tuple(
-        call(last_kernel, "last", (dots, right_side, d0, q0, p, s), [block, block], [])
-    )
+    fast_args = (dots, right_side, d0, q0, p, s)
+    total = dots.sum(0)
+    rd, dq, rp, qp = total[0], total[1], total[2], total[3]
+    a0 = rd / dq
+    rz = rd - a0 * rp - a0 * dq + a0 * a0 * qp
+
+    def fast():
+        return tuple(call(last_kernel, "last", fast_args, [block, block], []))
+
+    def careful():
+        r1, z1, w1 = right_side - a0 * q0, d0 - a0 * p, q0 - a0 * s
+        parts = jnp.stack([jnp.sum(r1 * z1), jnp.sum(z1 * w1), jnp.sum(z1 * q0)])
+        left = lax.psum(parts, ("sx", "sy", "cg"))
+        ratio = left[0] / rd
+        a1 = left[0] / (left[1] + 2.0 * ratio * left[2] + ratio * ratio * dq)
+        x = a0 * d0 + a1 * (z1 + ratio * d0)
+        return x, r1 - a1 * (w1 + ratio * q0)
+
+    return lax.cond(rz > 0.02 * rd, fast, careful)
 
 
 def solution(mesh):

time: 98.8 us -> 104 us (1.053)
  between operations: 1.1 us -> 5.83 us
  transfers between devices with their start and end apart: 12 -> 12, of which waited for: 6 -> 6; matrix products, arithmetic and copies ran while one was open for 0% -> 0% of each run, Pallas kernels for 4% -> 3%
where the time goes in v5:
time: 104 us
  blocking collectives  40.1 us (39%)
  starting transfers between devices  36.5 us (35%)
  Pallas kernels  10.4 us (10%)
  waiting for transfers between devices  7.75 us (7%)
  between operations  5.83 us (6%)
  local copies, waits for them, and re-layouts  1.87 us (2%)
  other arithmetic  1.4 us (1%)
    all_to_all x2, blocking collectives, exchange(): return lax.all_to_all(rows, axes, 0, 0).reshape(count, NZ)  40.1 us
    ppermute x12, starting transfers between devices, swap(): return lax.ppermute(values, axis, pairs)  36.5 us
    pallas_call x7, Pallas kernels, call(): pl.pallas_call(kernel, name=name, out_shape=[jax.ShapeDtypeStruct(s, F32)...  10.4 us
    ppermute x12, waiting for transfers between devices, swap(): return lax.ppermute(values, axis, pairs)  7.75 us
  transfers between devices with their start and end apart: 12, of which 6 were waited for; matrix products, arithmetic and copies ran while one was open for 0% of the time, Pallas kernels for 3%

profile of v5, /device:TPU:1, one launch (start us, length us, event | category | flops | bytes accessed | tf_op | source)
XLA Modules:
  0.0 103.8 jit_solution(9717901796150086027)
XLA Ops:
  0.7 1.0 constant_dynamic-slice_fusion
  1.7 1.1 %dynamic-slice_convert_fusion = (f32[3,128,128]{2,1,0:T(8,128)S(1)}, f32[3,128,128]{2,1,0:T(8,128)S(1)}) fusion(s32[8,128,128]{2,1,0:T(8,128)} %cls.1, s32[]{:T(128)S(6)} %select_n.132, s32[]{:T(128)S(6)} %select_n.130), kind=kLoop, calls=%fused_computation.11 | loop fusion | flops 98304 | bytes 786440 | tf_op jit(solution)/shard_map/convert_element_type | solution.py:582
  2.9 8.7 %collective-permute-start = (f32[5,128,128]{2,1,0:T(8,128)S(1)}, f32[5,128,128]{2,1,0:T(8,128)S(1)}, u32[]{:S(2)}, u32[]{:S(2)}) collective-permute-start(f32[5,128,128]{2,1,0:T(8,128)S(1)} %pad_maximum_fusion.1), channel_id=1, source_target_pairs={{0,1},{1,0},{2,3},{3,2},{4,5},{5,4},{6,7},{7,6},{64,65},{65,64},{6... | collective-permute-start | bytes 983048 | tf_op jit(solution)/shard_map/ppermute | solution.py:550
  11.7 1.9 %collective-permute-start.1 = (f32[5,128,128]{2,1,0:T(8,128)S(1)}, f32[5,128,128]{2,1,0:T(8,128)S(1)}, u32[]{:S(2)}, u32[]{:S(2)}) collective-permute-start(f32[5,128,128]{2,1,0:T(8,128)S(1)} %pad_maximum_fusion.2), channel_id=1, source_target_pairs={{1,2},{2,1},{3,4},{4,3},{5,6},{6,5},{7,64},{64,7},{65,66},{66,65},... | collective-permute-start | bytes 983048 | tf_op jit(solution)/shard_map/ppermute | solution.py:550
  13.7 0.7 collective-permute-start.3
  14.3 1.9 %collective-permute-start.2 = (f32[16,8,128]{2,1,0:T(8,128)S(1)}, f32[16,8,128]{2,1,0:T(8,128)S(1)}, u32[]{:S(2)}, u32[]{:S(2)}) collective-permute-start(f32[16,8,128]{2,1,0:T(8,128)S(1)} %get-tuple-element.170), channel_id=1, source_target_pairs={{0,8},{8,0},{16,24},{24,16},{32,40},{40,32},{48,56},{56,48},{1,9},... | collective-permute-start | bytes 196616 | tf_op jit(solution)/shard_map/ppermute | solution.py:550
  16.3 0.1 stack.35
  16.4 1.8 %own.1 = (f32[14,160,128]{2,1,0:T(8,128)S(1)}, f32[14,160,128]{2,1,0:T(8,128)S(1)}, f32[14,160,128]{2,1,0:T(8,128)S(1)}, f32[448,128]{1,0:T(8,128)S(1)}) custom-call(f32[8,128]{1,0:T(8,128)S(1)} %pad.4.table, s32[8,128,128]{2,1,0:T(8,128)S(1)} %copy-done, f32[8,128,128]{2,1,0:T(8,128)S(1)} %copy-done.1), custom_call_target="tpu_custom_call" | custom-call | tf_op jit(solution)/shard_map/own/pallas_call | solution.py:534
  18.2 1.1 %collective-permute-done.2 = f32[16,8,128]{2,1,0:T(8,128)S(1)} collective-permute-done((f32[16,8,128]{2,1,0:T(8,128)S(1)}, f32[16,8,128]{2,1,0:T(8,128)S(1)}, u32[]{:S(2)}, u32[]{:S(2)}) %collective-permute-start.2) | collective-permute-done | bytes 65568 | tf_op jit(solution)/shard_map/ppermute | solution.py:550
  19.4 0.7 collective-permute-done.1
  20.1 0.9 coarse.1.own
  21.0 4.1 %collective-permute-start.5 = (f32[8,128]{1,0:T(8,128)S(1)}, f32[8,128]{1,0:T(8,128)S(1)}, u32[]{:S(2)}, u32[]{:S(2)}) collective-permute-start(f32[8,128]{1,0:T(8,128)S(1)} %coarse.1.own), channel_id=1, source_target_pairs={{1,2},{2,1},{3,4},{4,3},{5,6},{6,5},{7,64},{64,7},{65,66},{66,65},... | collective-permute-start | bytes 12296 | tf_op jit(solution)/shard_map/ppermute | solution.py:550
  25.2 1.9 %collective-permute-start.4 = (f32[8,128]{1,0:T(8,128)S(1)}, f32[8,128]{1,0:T(8,128)S(1)}, u32[]{:S(2)}, u32[]{:S(2)}) collective-permute-start(f32[8,128]{1,0:T(8,128)S(1)} %coarse.1.own), channel_id=1, source_target_pairs={{0,1},{1,0},{2,3},{3,2},{4,5},{5,4},{6,7},{7,6},{64,65},{65,64},{6... | collective-permute-start | bytes 12296 | tf_op jit(solution)/shard_map/ppermute | solution.py:550
  27.2 1.1 %collective-permute-done.4 = f32[8,128]{1,0:T(8,128)S(1)} collective-permute-done((f32[8,128]{1,0:T(8,128)S(1)}, f32[8,128]{1,0:T(8,128)S(1)}, u32[]{:S(2)}, u32[]{:S(2)}) %collective-permute-start.4) | collective-permute-done | bytes 4128 | tf_op jit(solution)/shard_map/ppermute | solution.py:550
  28.3 0.7 collective-permute-start.7
  29.0 4.7 %collective-permute-start.6 = (f32[13,8,128]{2,1,0:T(8,128)S(1)}, f32[13,8,128]{2,1,0:T(8,128)S(1)}, u32[]{:S(2)}, u32[]{:S(2)}) collective-permute-start(f32[13,8,128]{2,1,0:T(8,128)S(1)} %get-tuple-element.178), channel_id=1, source_target_pairs={{0,8},{8,0},{16,24},{24,16},{32,40},{40,32},{48,56},{56,48},{1,9},... | collective-permute-start | bytes 159752 | tf_op jit(solution)/shard_map/ppermute | solution.py:550
  33.7 1.3 %cells.1 = (f32[14,160,128]{2,1,0:T(8,128)S(1)}, f32[14,160,128]{2,1,0:T(8,128)S(1)}, f32[14,160,128]{2,1,0:T(8,128)S(1)}, f32[14,160,128]{2,1,0:T(8,128)S(1)}, ...) custom-call(f32[5]{0:T(128)S(1)} %convert_element_type.18.inside, ...), custom_call_target="tpu_custom_call", output_to_operand_aliasing={{0}: (7, {}), {1}: (8, {})} | custom-call | tf_op jit(solution)/shard_map/cells/pallas_call | solution.py:534
  35.0 0.1 collective-permute-done.6
  35.2 2.8 %first.1 = (f32[8,128,128]{2,1,0:T(8,128)S(1)}, f32[8,128,128]{2,1,0:T(8,128)S(1)}, f32[264,128]{1,0:T(8,128)S(1)}, f32[264,128]{1,0:T(8,128)S(1)}, f32[8,128]{1...) custom-call(f32[5]{0:T(128)S(1)} %convert_element_type.18.inside, ...), custom_call_target="tpu_custom_call", output_to_operand_aliasing={{6}: (12, {}), {7}: (13, {}), {8}: (14, {}), {9}: (15, {}),... | custom-call | tf_op jit(solution)/shard_map/first/pallas_call | solution.py:534
  38.0 3.2 %collective-permute-start.8 = (f32[264,128]{1,0:T(8,128)S(1)}, f32[264,128]{1,0:T(8,128)S(1)}, u32[]{:S(2)}, u32[]{:S(2)}) collective-permute-start(f32[264,128]{1,0:T(8,128)S(1)} %get-tuple-element.85), channel_id=1, source_target_pairs={{0,1},{1,0},{2,3},{3,2},{4,5},{5,4},{6,7},{7,6},{64,65},{65,64},{6... | collective-permute-start | bytes 405512 | tf_op jit(solution)/shard_map/ppermute | solution.py:550
  41.2 2.7 %collective-permute-start.9 = (f32[264,128]{1,0:T(8,128)S(1)}, f32[264,128]{1,0:T(8,128)S(1)}, u32[]{:S(2)}, u32[]{:S(2)}) collective-permute-start(f32[264,128]{1,0:T(8,128)S(1)} %get-tuple-element.86), channel_id=1, source_target_pairs={{1,2},{2,1},{3,4},{4,3},{5,6},{6,5},{7,64},{64,7},{65,66},{66,65},... | collective-permute-start | bytes 405512 | tf_op jit(solution)/shard_map/ppermute | solution.py:550
  43.9 3.6 %collective-permute-done.9 = f32[264,128]{1,0:T(8,128)S(1)} collective-permute-done((f32[264,128]{1,0:T(8,128)S(1)}, f32[264,128]{1,0:T(8,128)S(1)}, u32[]{:S(2)}, u32[]{:S(2)}) %collective-permute-start.9) | collective-permute-done | bytes 135200 | tf_op jit(solution)/shard_map/ppermute | solution.py:550
  47.7 0.7 collective-permute-start.11
  48.3 5.2 %collective-permute-start.10 = (f32[15,8,128]{2,1,0:T(8,128)S(1)}, f32[15,8,128]{2,1,0:T(8,128)S(1)}, u32[]{:S(2)}, u32[]{:S(2)}) collective-permute-start(f32[15,8,128]{2,1,0:T(8,128)S(1)} %get-tuple-element.174), channel_id=1, source_target_pairs={{0,8},{8,0},{16,24},{24,16},{32,40},{40,32},{48,56},{56,48},{1,9},... | collective-permute-start | bytes 184328 | tf_op jit(solution)/shard_map/ppermute | solution.py:550
  53.5 0.5 inner.1
  54.0 1.1 %collective-permute-done.10 = f32[15,8,128]{2,1,0:T(8,128)S(1)} collective-permute-done((f32[15,8,128]{2,1,0:T(8,128)S(1)}, f32[15,8,128]{2,1,0:T(8,128)S(1)}, u32[]{:S(2)}, u32[]{:S(2)}) %collective-permute-start.10) | collective-permute-done | bytes 61472 | tf_op jit(solution)/shard_map/ppermute | solution.py:550
  55.1 1.8 %second.1 = (f32[8,128,128]{2,1,0:T(8,128)S(1)}, f32[8,128,128]{2,1,0:T(8,128)S(1)}, f32[1,128]{1,0:T(1,128)S(1)}, f32[14,160,128]{2,1,0:T(8,128)S(1)}, f32[14,160,128]{2,1,0:T(8,128)S(1)}) custom-call(f32[8,128,128]{2,1,0:T(8,128)S(1)} %copy-done.1, f32[8,128,128]{2,1,0:T(8,128)S(1)} %get-tuple-element.83.d0, ...), custom_call_target="tpu_custom_call", output_to_operand_aliasing={{3}: (15, {}), {4}: (16, {})} | custom-call | tf_op jit(solution)/shard_map/second/pallas_call | solution.py:534
  56.9 22.1 %all_to_all.10 = f32[64,1,128]{2,1,0:T(1,128)S(1)} all-to-all(f32[64,1,128]{2,1,0:T(1,128)S(1)} %broadcast_in_dim.76), channel_id=1, replica_groups=mesh['sx'=8,'sy'=8,'cg'=8] {'sy','cg'}, dimensions={0} | all-to-all | bytes 65536 | tf_op jit(solution)/shard_map/all_to_all | solution.py:566
  79.1 17.9 %all_to_all.11 = f32[8,1,128]{2,1,0:T(1,128)S(1)} all-to-all(f32[8,1,128]{2,1,0:T(1,128)S(1)} %broadcast_in_dim.77), channel_id=1, replica_groups=mesh['sx'=8,'sy'=8,'cg'=8] {'sx'}, dimensions={0} | all-to-all | bytes 8192 | tf_op jit(solution)/shard_map/all_to_all | solution.py:566
  97.1 0.7 fusion.4
  102.5 1.3 %conditional.1 = ((f32[8,128,128]{2,1,0:T(8,128)}, f32[8,128,128]{2,1,0:T(8,128)})) conditional(s32[]{:T(128)} %convert_element_type.23, (f32[]{:T(128)}, f32[8,128,128]{2,1,0:T(8,128)S(1)}, f32[8,128,128]{2,1,0:T(8,128)S(1)}, f32[8,128,128]{2,1,0:T(8,128)S(1)}, f32[8,128,128]{2,1,0:T(8,128)S(1)}, /*index=5*/f32[8,128,128]{2,1,0:T(8,128)S(1)}, ...), branch_computations={%region_2.7_spmd, %region_7.8_spmd} | conditional | flops 3538958 | bytes 6291676 | solution.py:664
  102.5 1.3 %last.1 = (f32[8,128,128]{2,1,0:T(8,128)}, f32[8,128,128]{2,1,0:T(8,128)}) custom-call(f32[8,128]{1,0:T(8,128)S(1)} %bitcast.77, f32[8,128,128]{2,1,0:T(8,128)S(1)} %get-tuple-element.38.rhs, f32[8,128,128]{2,1,0:T(8,128)S(1)} %get-tuple-element.39.d0, f32[8,128,128]{2,1,0:T(8,128)S(1)} %get-tuple-element.40.q0, f32[8,128,128]{2,1,0:T(8,128)S(1)} %get-tuple-element.41.p, ...), custom_call_target="tpu_custom_call" | custom-call | tf_op jit(solution)/shard_map/cond/branch_1_fun/last/pallas_call | solution.py:534
  (47 shorter events, 0.4 us)
Async XLA Ops:
  1.6 11.9 %copy-start = (s32[8,128,128]{2,1,0:T(8,128)S(1)}, s32[8,128,128]{2,1,0:T(8,128)}, u32[]{:S(2)}) copy-start(s32[8,128,128]{2,1,0:T(8,128)} %cls.1) | copy-start | bytes 1572868
  1.7 12.0 %copy-start.1 = (f32[8,128,128]{2,1,0:T(8,128)S(1)}, f32[8,128,128]{2,1,0:T(8,128)}, u32[]{:S(2)}) copy-start(f32[8,128,128]{2,1,0:T(8,128)} %rhs.7) | copy-start | bytes 1572868
  2.8 13.6 %copy-start.2 = (f32[2,16]{1,0:T(2,128)S(1)}, f32[2,16]{1,0:T(2,128)}, u32[]{:S(2)}) copy-start(f32[2,16]{1,0:T(2,128)} %param.7) | copy-start | bytes 388
  2.9 16.5 %collective-permute-start = (f32[5,128,128]{2,1,0:T(8,128)S(1)}, f32[5,128,128]{2,1,0:T(8,128)S(1)}, u32[]{:S(2)}, u32[]{:S(2)}) collective-permute-start(f32[5,128,128]{2,1,0:T(8,128)S(1)} %pad_maximum_fusion.1), channel_id=1, source_target_pairs={{0,1},{1,0},{2,3},{3,2},{4,5},{5,4},{6,7},{7,6},{64,65},{65,64},{6... | collective-permute-start | bytes 983048 | tf_op jit(solution)/shard_map/ppermute | solution.py:550
  11.7 8.4 %collective-permute-start.1 = (f32[5,128,128]{2,1,0:T(8,128)S(1)}, f32[5,128,128]{2,1,0:T(8,128)S(1)}, u32[]{:S(2)}, u32[]{:S(2)}) collective-permute-start(f32[5,128,128]{2,1,0:T(8,128)S(1)} %pad_maximum_fusion.2), channel_id=1, source_target_pairs={{1,2},{2,1},{3,4},{4,3},{5,6},{6,5},{7,64},{64,7},{65,66},{66,65},... | collective-permute-start | bytes 983048 | tf_op jit(solution)/shard_map/ppermute | solution.py:550
  13.7 4.5 %collective-permute-start.3 = (f32[16,8,128]{2,1,0:T(8,128)S(1)}, f32[16,8,128]{2,1,0:T(8,128)S(1)}, u32[]{:S(2)}, u32[]{:S(2)}) collective-permute-start(f32[16,8,128]{2,1,0:T(8,128)S(1)} %get-tuple-element.169), channel_id=1, source_target_pairs={{8,16},{16,8},{24,32},{32,24},{40,48},{48,40},{9,17},{17,9},{25,33... | collective-permute-start | bytes 196616 | tf_op jit(solution)/shard_map/ppermute | solution.py:550
  14.3 5.0 %collective-permute-start.2 = (f32[16,8,128]{2,1,0:T(8,128)S(1)}, f32[16,8,128]{2,1,0:T(8,128)S(1)}, u32[]{:S(2)}, u32[]{:S(2)}) collective-permute-start(f32[16,8,128]{2,1,0:T(8,128)S(1)} %get-tuple-element.170), channel_id=1, source_target_pairs={{0,8},{8,0},{16,24},{24,16},{32,40},{40,32},{48,56},{56,48},{1,9},... | collective-permute-start | bytes 196616 | tf_op jit(solution)/shard_map/ppermute | solution.py:550
  21.0 6.1 %collective-permute-start.5 = (f32[8,128]{1,0:T(8,128)S(1)}, f32[8,128]{1,0:T(8,128)S(1)}, u32[]{:S(2)}, u32[]{:S(2)}) collective-permute-start(f32[8,128]{1,0:T(8,128)S(1)} %coarse.1.own), channel_id=1, source_target_pairs={{1,2},{2,1},{3,4},{4,3},{5,6},{6,5},{7,64},{64,7},{65,66},{66,65},... | collective-permute-start | bytes 12296 | tf_op jit(solution)/shard_map/ppermute | solution.py:550
  25.2 3.1 %collective-permute-start.4 = (f32[8,128]{1,0:T(8,128)S(1)}, f32[8,128]{1,0:T(8,128)S(1)}, u32[]{:S(2)}, u32[]{:S(2)}) collective-permute-start(f32[8,128]{1,0:T(8,128)S(1)} %coarse.1.own), channel_id=1, source_target_pairs={{0,1},{1,0},{2,3},{3,2},{4,5},{5,4},{6,7},{7,6},{64,65},{65,64},{6... | collective-permute-start | bytes 12296 | tf_op jit(solution)/shard_map/ppermute | solution.py:550
  28.3 6.7 %collective-permute-start.7 = (f32[13,8,128]{2,1,0:T(8,128)S(1)}, f32[13,8,128]{2,1,0:T(8,128)S(1)}, u32[]{:S(2)}, u32[]{:S(2)}) collective-permute-start(f32[13,8,128]{2,1,0:T(8,128)S(1)} %get-tuple-element.177), channel_id=1, source_target_pairs={{8,16},{16,8},{24,32},{32,24},{40,48},{48,40},{9,17},{17,9},{25,33... | collective-permute-start | bytes 159752 | tf_op jit(solution)/shard_map/ppermute | solution.py:550
  29.0 6.2 %collective-permute-start.6 = (f32[13,8,128]{2,1,0:T(8,128)S(1)}, f32[13,8,128]{2,1,0:T(8,128)S(1)}, u32[]{:S(2)}, u32[]{:S(2)}) collective-permute-start(f32[13,8,128]{2,1,0:T(8,128)S(1)} %get-tuple-element.178), channel_id=1, source_target_pairs={{0,8},{8,0},{16,24},{24,16},{32,40},{40,32},{48,56},{56,48},{1,9},... | collective-permute-start | bytes 159752 | tf_op jit(solution)/shard_map/ppermute | solution.py:550
  38.0 6.0 %collective-permute-start.8 = (f32[264,128]{1,0:T(8,128)S(1)}, f32[264,128]{1,0:T(8,128)S(1)}, u32[]{:S(2)}, u32[]{:S(2)}) collective-permute-start(f32[264,128]{1,0:T(8,128)S(1)} %get-tuple-element.85), channel_id=1, source_target_pairs={{0,1},{1,0},{2,3},{3,2},{4,5},{5,4},{6,7},{7,6},{64,65},{65,64},{6... | collective-permute-start | bytes 405512 | tf_op jit(solution)/shard_map/ppermute | solution.py:550
  41.2 6.3 %collective-permute-start.9 = (f32[264,128]{1,0:T(8,128)S(1)}, f32[264,128]{1,0:T(8,128)S(1)}, u32[]{:S(2)}, u32[]{:S(2)}) collective-permute-start(f32[264,128]{1,0:T(8,128)S(1)} %get-tuple-element.86), channel_id=1, source_target_pairs={{1,2},{2,1},{3,4},{4,3},{5,6},{6,5},{7,64},{64,7},{65,66},{66,65},... | collective-permute-start | bytes 405512 | tf_op jit(solution)/shard_map/ppermute | solution.py:550
  47.7 6.3 %collective-permute-start.11 = (f32[15,8,128]{2,1,0:T(8,128)S(1)}, f32[15,8,128]{2,1,0:T(8,128)S(1)}, u32[]{:S(2)}, u32[]{:S(2)}) collective-permute-start(f32[15,8,128]{2,1,0:T(8,128)S(1)} %get-tuple-element.173), channel_id=1, source_target_pairs={{8,16},{16,8},{24,32},{32,24},{40,48},{48,40},{9,17},{17,9},{25,33... | collective-permute-start | bytes 184328 | tf_op jit(solution)/shard_map/ppermute | solution.py:550
  48.3 6.8 %collective-permute-start.10 = (f32[15,8,128]{2,1,0:T(8,128)S(1)}, f32[15,8,128]{2,1,0:T(8,128)S(1)}, u32[]{:S(2)}, u32[]{:S(2)}) collective-permute-start(f32[15,8,128]{2,1,0:T(8,128)S(1)} %get-tuple-element.174), channel_id=1, source_target_pairs={{0,8},{8,0},{16,24},{24,16},{32,40},{40,32},{48,56},{56,48},{1,9},... | collective-permute-start | bytes 184328 | tf_op jit(solution)/shard_map/ppermute | solution.py:550
